TPU v7x, 32 devices: a whole 2x2x4 slice. The times are simulated.
32 devices in a mesh: blk: 16 (over z, x, core), grp: 2 (over y).
Axes of the slice: x: 2, y: 2, z: 4, core: 2. Of those that a mesh axis runs over, the one named last changes fastest.
Arguments:
- spectra: float32 [1024, 2, 4, 512], P(('blk', 'grp')), may hold values from -120 to 120
- channel_ids: int32 [1024], replicated, may hold values from 0 to 1023, each once
- plan: int32 [16, 9], P('blk'), may hold values from 0 to 8, each once within a row
Outputs:
- correlations: bfloat16 [16, 9, 2, 64, 32, 400], P('blk', None, 'grp')
Inputs may be any that keep to these rules, and one draw needn't show every extreme that they name: `channel_ids`: each channel number appears once. `plan`: each row holds every offset 0 to 8 once.
All inputs are finite; a program needn't handle non-finite values.
Results may differ from a plain program's by a relative error of at most 0.0068.
Values may be sent and summed in bfloat16 or wider, within the bound.
No kernel may reach another device: no remote copies, remote signals or barrier semaphores. Data moves between devices by JAX's collectives and lax.ppermute only.
A program may use at most 128 MiB of HBM per device.

v0:
```python
import math

import jax
import jax.numpy as jnp
from jax import lax
from jax.sharding import PartitionSpec as P

NFFT = 2000
HALF_LAG = 200


def passed_along(block, axis, distance):
    devices = range(lax.axis_size(axis))
    route = [((i - distance) % len(devices), i) for i in devices]
    return lax.ppermute(block, axis, route)


def whiten(spectra):
    seg_power = jnp.mean(spectra * spectra, axis=(1, 3))
    whitened = spectra * lax.rsqrt(seg_power + 1e-06)[:, None, :, None]
    whitened = whitened.astype(jnp.bfloat16)
    return whitened.reshape(spectra.shape[0], 2 * spectra.shape[2], spectra.shape[3])


def lag_tables(freq_count):
    freq_axis = jnp.arange(freq_count, dtype=jnp.int32)
    lag_axis = jnp.arange(2 * HALF_LAG, dtype=jnp.int32) - HALF_LAG
    phase_index = freq_axis[:, None] * lag_axis[None, :] % NFFT
    angles = 2.0 * math.pi / NFFT * phase_index.astype(jnp.float32)
    weights = jnp.where(freq_axis == 0, 1.0, 2.0).astype(jnp.float32)[:, None]
    cos_tab = (weights * jnp.cos(angles)).astype(jnp.bfloat16)
    sin_tab = (-weights * jnp.sin(angles)).astype(jnp.bfloat16)
    return (cos_tab, sin_tab)


def on_device(spectra, channel_ids, plan):
    col_count = spectra.shape[0]
    seg_count = spectra.shape[2]
    freq_count = spectra.shape[3]
    whitened = whiten(spectra)
    row_block = lax.all_gather(whitened, "grp", axis=0, tiled=True)
    row_count = row_block.shape[0]
    rotated = jnp.concatenate([row_block[:, seg_count:], -row_block[:, :seg_count]], axis=1)
    paired = jnp.stack([row_block, rotated])
    blk_count = lax.axis_size("blk")
    step_count = blk_count // 2 + 1
    blk_index = lax.axis_index("blk")
    grp_index = lax.axis_index("grp")
    cos_tab, sin_tab = lag_tables(freq_count)
    lag_count = cos_tab.shape[1]
    row_start = blk_index * row_count
    row_ids = lax.dynamic_slice_in_dim(channel_ids, row_start, row_count, 0)
    row_slots = row_start + jnp.arange(row_count, dtype=jnp.int32)
    slot_list = jnp.arange(step_count, dtype=jnp.int32)
    scaling = 1.0 / math.sqrt(2.0 * freq_count * seg_count)

    def correlate(offset, columns, output):
        col_start = (blk_index + offset) % blk_count * row_count + grp_index * col_count
        col_ids = lax.dynamic_slice_in_dim(channel_ids, col_start, col_count, 0)
        col_slots = col_start + jnp.arange(col_count, dtype=jnp.int32)
        cross_spec = jnp.einsum(
            "prsf,csf->prcf", paired, columns, preferred_element_type=jnp.float32
        )
        cross_spec = cross_spec.astype(jnp.bfloat16).reshape(2, row_count * col_count, freq_count)
        real_part = jnp.dot(cross_spec[0], cos_tab, preferred_element_type=jnp.float32)
        imag_part = jnp.dot(cross_spec[1], sin_tab, preferred_element_type=jnp.float32)
        orient = (
            jnp.where(row_ids[:, None] < col_ids[None, :], 1.0, -1.0)
            .astype(jnp.float32)
            .reshape(-1, 1)
        )
        keeper = (row_slots[:, None] != col_slots[None, :]).astype(jnp.float32).reshape(-1, 1)
        lagged = ((real_part + orient * imag_part) * (scaling * keeper)).astype(jnp.bfloat16)
        lagged = lagged.reshape(1, 1, 1, row_count, col_count, lag_count)
        out_slot = jnp.sum(slot_list * (plan[0] == offset).astype(jnp.int32))
        return lax.dynamic_update_slice(output, lagged, (0, out_slot, 0, 0, 0, 0))

    output = jnp.zeros((1, step_count, 1, row_count, col_count, lag_count), jnp.bfloat16)

    def advance(offset, carry):
        columns, output = carry
        output = correlate(offset, columns, output)
        columns = passed_along(columns, "blk", -1)
        return (columns, output)

    columns, output = lax.fori_loop(0, step_count - 1, advance, (whitened, output))
    output = correlate(step_count - 1, columns, output)
    return output


def solution(mesh):
    return jax.shard_map(
        on_device,
        mesh=mesh,
        in_specs=(P(("blk", "grp"), None, None, None), P(), P("blk", None)),
        out_specs=P("blk", None, "grp", None, None, None),
        check_vma=False,
    )
```

profile of v0, /device:TPU:0, one launch (start us, length us, event | category | flops | bytes accessed | tf_op | source)
XLA Modules:
  0.0 416.1 jit_solution(18046994656492659904)
XLA Ops:
  2.5 9.9 %all_gather.3 = bf16[64,8,512]{2,1,0:T(8,128)(2,1)S(1)} all-gather(bf16[32,8,512]{2,1,0:T(8,128)(2,1)S(1)} %reshape.167), channel_id=1, replica_groups=mesh['blk'=16,'grp'=2] {'grp'}, dimensions={0}, use_global_device_ids=true | all-gather | bytes 786432 | tf_op jit(solution)/shard_map/all_gather | solution.py:41
  17.3 6.7 %broadcast_in_dim.49 = bf16[1,9,1,64,32,400]{5,4,3,2,1,0:T(8,128)(2,1)} broadcast(bf16[]{:T(256)} %constant.165.clone.1), dimensions={} | broadcast | bytes 14745602 | tf_op jit(solution)/shard_map/broadcast_in_dim | solution.py:78
  24.0 347.4 %while.19 = (s32[]{:T(128)}, bf16[32,8,512]{2,1,0:T(8,128)(2,1)S(1)}, bf16[1,9,1,64,32,400]{5,4,3,2,1,0:T(8,128)(2,1)}, bf16[2,64,8,512]{1,2,0,3:T(8,128)(2,1)},...) while((s32[]{:T(128)}, ...), condition=%wide.region_3.4_spmd.clone.clone, body=%wide.region_1.3_spmd.clone.clone.sunk | while | flops 1721163776 | bytes 52241416 | solution.py:86
  48.3 5.8 %copy.64 = bf16[1,64,32,512]{3,2,1,0:T(8,128)(2,1)S(1)} copy(bf16[1,64,32,512]{1,2,0,3:T(8,128)(2,1)} %get-tuple-element.505) | data formatting | bytes 4194304 | tf_op jit(solution)/shard_map/while/body/eval_jaxpr/slice | solution.py:65
  54.1 6.9 %copy.65 = bf16[1,64,32,512]{3,2,1,0:T(8,128)(2,1)} copy(bf16[1,64,32,512]{1,2,0,3:T(8,128)(2,1)} %get-tuple-element.506) | data formatting | bytes 4194304 | tf_op jit(solution)/shard_map/while/body/eval_jaxpr/slice | solution.py:66
  67.1 6.2 %multiply_convert_fusion.16 = bf16[2048,400]{0,1:T(8,128)(2,1)} fusion(f32[2048,400]{0,1:T(8,128)S(1)} %fusion.78, bf16[2048,512]{1,0:T(8,128)(2,1)S(1)} %bitcast.52, f32[2048]{0:T(1024)S(1)} %mul.578, f32[2048]{0:T(1024)S(1)} %select_n.177, f32[512]{0:T(512)S(1)} %get-tuple-element.558, s32[400]{0:T(512)S(1)} %get-tuple-element.556), kind=kOutput, calls=%fused_computation.5.clone.1 | convolution fusion | flops 844390400 | bytes 7032384 | tf_op jit(solution)/shard_map/while/body/eval_jaxpr/dot_general | solution.py:66
  90.8 5.8 %copy.64 = bf16[1,64,32,512]{3,2,1,0:T(8,128)(2,1)S(1)} copy(bf16[1,64,32,512]{1,2,0,3:T(8,128)(2,1)} %get-tuple-element.505) | data formatting | bytes 4194304 | tf_op jit(solution)/shard_map/while/body/eval_jaxpr/slice | solution.py:65
  96.7 6.9 %copy.65 = bf16[1,64,32,512]{3,2,1,0:T(8,128)(2,1)} copy(bf16[1,64,32,512]{1,2,0,3:T(8,128)(2,1)} %get-tuple-element.506) | data formatting | bytes 4194304 | tf_op jit(solution)/shard_map/while/body/eval_jaxpr/slice | solution.py:66
  109.6 6.2 %multiply_convert_fusion.16 = bf16[2048,400]{0,1:T(8,128)(2,1)} fusion(f32[2048,400]{0,1:T(8,128)S(1)} %fusion.78, bf16[2048,512]{1,0:T(8,128)(2,1)S(1)} %bitcast.52, f32[2048]{0:T(1024)S(1)} %mul.578, f32[2048]{0:T(1024)S(1)} %select_n.177, f32[512]{0:T(512)S(1)} %get-tuple-element.558, s32[400]{0:T(512)S(1)} %get-tuple-element.556), kind=kOutput, calls=%fused_computation.5.clone.1 | convolution fusion | flops 844390400 | bytes 7032384 | tf_op jit(solution)/shard_map/while/body/eval_jaxpr/dot_general | solution.py:66
  137.7 6.9 %copy.65 = bf16[1,64,32,512]{3,2,1,0:T(8,128)(2,1)} copy(bf16[1,64,32,512]{1,2,0,3:T(8,128)(2,1)} %get-tuple-element.506) | data formatting | bytes 4194304 | tf_op jit(solution)/shard_map/while/body/eval_jaxpr/slice | solution.py:66
  150.6 6.2 %multiply_convert_fusion.16 = bf16[2048,400]{0,1:T(8,128)(2,1)} fusion(f32[2048,400]{0,1:T(8,128)S(1)} %fusion.78, bf16[2048,512]{1,0:T(8,128)(2,1)S(1)} %bitcast.52, f32[2048]{0:T(1024)S(1)} %mul.578, f32[2048]{0:T(1024)S(1)} %select_n.177, f32[512]{0:T(512)S(1)} %get-tuple-element.558, s32[400]{0:T(512)S(1)} %get-tuple-element.556), kind=kOutput, calls=%fused_computation.5.clone.1 | convolution fusion | flops 844390400 | bytes 7032384 | tf_op jit(solution)/shard_map/while/body/eval_jaxpr/dot_general | solution.py:66
  179.3 6.9 %copy.65 = bf16[1,64,32,512]{3,2,1,0:T(8,128)(2,1)} copy(bf16[1,64,32,512]{1,2,0,3:T(8,128)(2,1)} %get-tuple-element.506) | data formatting | bytes 4194304 | tf_op jit(solution)/shard_map/while/body/eval_jaxpr/slice | solution.py:66
  192.2 6.2 %multiply_convert_fusion.16 = bf16[2048,400]{0,1:T(8,128)(2,1)} fusion(f32[2048,400]{0,1:T(8,128)S(1)} %fusion.78, bf16[2048,512]{1,0:T(8,128)(2,1)S(1)} %bitcast.52, f32[2048]{0:T(1024)S(1)} %mul.578, f32[2048]{0:T(1024)S(1)} %select_n.177, f32[512]{0:T(512)S(1)} %get-tuple-element.558, s32[400]{0:T(512)S(1)} %get-tuple-element.556), kind=kOutput, calls=%fused_computation.5.clone.1 | convolution fusion | flops 844390400 | bytes 7032384 | tf_op jit(solution)/shard_map/while/body/eval_jaxpr/dot_general | solution.py:66
  220.4 6.9 %copy.65 = bf16[1,64,32,512]{3,2,1,0:T(8,128)(2,1)} copy(bf16[1,64,32,512]{1,2,0,3:T(8,128)(2,1)} %get-tuple-element.506) | data formatting | bytes 4194304 | tf_op jit(solution)/shard_map/while/body/eval_jaxpr/slice | solution.py:66
  233.3 6.2 %multiply_convert_fusion.16 = bf16[2048,400]{0,1:T(8,128)(2,1)} fusion(f32[2048,400]{0,1:T(8,128)S(1)} %fusion.78, bf16[2048,512]{1,0:T(8,128)(2,1)S(1)} %bitcast.52, f32[2048]{0:T(1024)S(1)} %mul.578, f32[2048]{0:T(1024)S(1)} %select_n.177, f32[512]{0:T(512)S(1)} %get-tuple-element.558, s32[400]{0:T(512)S(1)} %get-tuple-element.556), kind=kOutput, calls=%fused_computation.5.clone.1 | convolution fusion | flops 844390400 | bytes 7032384 | tf_op jit(solution)/shard_map/while/body/eval_jaxpr/dot_general | solution.py:66
  262.8 6.9 %copy.65 = bf16[1,64,32,512]{3,2,1,0:T(8,128)(2,1)} copy(bf16[1,64,32,512]{1,2,0,3:T(8,128)(2,1)} %get-tuple-element.506) | data formatting | bytes 4194304 | tf_op jit(solution)/shard_map/while/body/eval_jaxpr/slice | solution.py:66
  275.7 6.2 %multiply_convert_fusion.16 = bf16[2048,400]{0,1:T(8,128)(2,1)} fusion(f32[2048,400]{0,1:T(8,128)S(1)} %fusion.78, bf16[2048,512]{1,0:T(8,128)(2,1)S(1)} %bitcast.52, f32[2048]{0:T(1024)S(1)} %mul.578, f32[2048]{0:T(1024)S(1)} %select_n.177, f32[512]{0:T(512)S(1)} %get-tuple-element.558, s32[400]{0:T(512)S(1)} %get-tuple-element.556), kind=kOutput, calls=%fused_computation.5.clone.1 | convolution fusion | flops 844390400 | bytes 7032384 | tf_op jit(solution)/shard_map/while/body/eval_jaxpr/dot_general | solution.py:66
  303.9 6.9 %copy.65 = bf16[1,64,32,512]{3,2,1,0:T(8,128)(2,1)} copy(bf16[1,64,32,512]{1,2,0,3:T(8,128)(2,1)} %get-tuple-element.506) | data formatting | bytes 4194304 | tf_op jit(solution)/shard_map/while/body/eval_jaxpr/slice | solution.py:66
  316.8 6.2 %multiply_convert_fusion.16 = bf16[2048,400]{0,1:T(8,128)(2,1)} fusion(f32[2048,400]{0,1:T(8,128)S(1)} %fusion.78, bf16[2048,512]{1,0:T(8,128)(2,1)S(1)} %bitcast.52, f32[2048]{0:T(1024)S(1)} %mul.578, f32[2048]{0:T(1024)S(1)} %select_n.177, f32[512]{0:T(512)S(1)} %get-tuple-element.558, s32[400]{0:T(512)S(1)} %get-tuple-element.556), kind=kOutput, calls=%fused_computation.5.clone.1 | convolution fusion | flops 844390400 | bytes 7032384 | tf_op jit(solution)/shard_map/while/body/eval_jaxpr/dot_general | solution.py:66
  345.5 6.9 %copy.65 = bf16[1,64,32,512]{3,2,1,0:T(8,128)(2,1)} copy(bf16[1,64,32,512]{1,2,0,3:T(8,128)(2,1)} %get-tuple-element.506) | data formatting | bytes 4194304 | tf_op jit(solution)/shard_map/while/body/eval_jaxpr/slice | solution.py:66
  358.4 6.2 %multiply_convert_fusion.16 = bf16[2048,400]{0,1:T(8,128)(2,1)} fusion(f32[2048,400]{0,1:T(8,128)S(1)} %fusion.78, bf16[2048,512]{1,0:T(8,128)(2,1)S(1)} %bitcast.52, f32[2048]{0:T(1024)S(1)} %mul.578, f32[2048]{0:T(1024)S(1)} %select_n.177, f32[512]{0:T(512)S(1)} %get-tuple-element.558, s32[400]{0:T(512)S(1)} %get-tuple-element.556), kind=kOutput, calls=%fused_computation.5.clone.1 | convolution fusion | flops 844390400 | bytes 7032384 | tf_op jit(solution)/shard_map/while/body/eval_jaxpr/dot_general | solution.py:66
  386.3 6.6 %fusion.36 = f32[2048,400]{0,1:T(8,128)} fusion(bf16[2048,512]{1,0:T(8,128)(2,1)S(1)} %bitcast.54, s32[400]{0:T(512)S(1)} %get-tuple-element.569, f32[512]{0:T(512)S(1)} %get-tuple-element.570), kind=kOutput, calls=%fused_computation.50 | convolution fusion | flops 841113600 | bytes 5377600 | tf_op jit(solution)/shard_map/dot_general | solution.py:65
  393.0 7.1 %copy.50 = bf16[1,64,32,512]{3,2,1,0:T(8,128)(2,1)} copy(bf16[1,64,32,512]{1,2,0,3:T(8,128)(2,1)} %get-tuple-element.418) | data formatting | bytes 4194304 | tf_op jit(solution)/shard_map/slice | solution.py:66
  401.1 7.7 %multiply_convert_fusion.5 = bf16[2048,400]{0,1:T(8,128)(2,1)} fusion(f32[2048,400]{0,1:T(8,128)S(1)} %copy-done.2, bf16[2048,512]{1,0:T(8,128)(2,1)} %bitcast.59, f32[2048]{0:T(1024)S(1)} %mul.220, f32[2048]{0:T(1024)S(1)} %select_n.116, f32[512]{0:T(512)S(1)} %get-tuple-element.572, s32[400]{0:T(512)S(1)} %get-tuple-element.569), kind=kOutput, calls=%fused_computation.38 | convolution fusion | flops 844390400 | bytes 7032384 | tf_op jit(solution)/shard_map/dot_general | solution.py:66
  (191 shorter events, 231.4 us)
Async XLA Ops:
  13.5 3.0 copy-start.1
  14.7 9.4 %copy-start.3 = (bf16[1,64,8,512]{1,2,0,3:T(8,128)(2,1)}, bf16[1,64,8,512]{1,2,0,3:T(8,128)(2,1)S(1)}, u32[]{:S(2)}) copy-start(bf16[1,64,8,512]{1,2,0,3:T(8,128)(2,1)S(1)} %maximum_bitcast_fusion) | copy-start | bytes 1572868
  17.3 6.8 %copy-start.4 = (s32[1,9]{1,0:T(1,128)S(1)}, s32[1,9]{1,0:T(1,128)}, u32[]{:S(2)}) copy-start(s32[1,9]{1,0:T(1,128)} %param.7) | copy-start | bytes 112
  35.8 44.3 %collective-permute-start = (bf16[32,8,512]{2,1,0:T(8,128)(2,1)S(1)}, bf16[32,8,512]{2,1,0:T(8,128)(2,1)S(1)}, u32[]{:S(2)}, u32[]{:S(2)}) collective-permute-start(bf16[32,8,512]{2,1,0:T(8,128)(2,1)S(1)} %copy.72), channel_id=1, source_target_pairs={{2,0},{4,2},{6,4},{8,6},{10,8},{12,10},{14,12},{16,14},{18,16},{20... | collective-permute-start | bytes 786440 | tf_op jit(solution)/shard_map/while/body/eval_jaxpr/ppermute | solution.py:15
  62.1 4.9 %copy-start = (bf16[1,64,32,512]{3,2,1,0:T(8,128)(2,1)S(1)}, bf16[1,64,32,512]{3,2,1,0:T(8,128)(2,1)}, u32[]{:S(2)}) copy-start(bf16[1,64,32,512]{3,2,1,0:T(8,128)(2,1)} %copy.65) | copy-start | bytes 6291460 | tf_op jit(solution)/shard_map/while
  80.1 42.5 %collective-permute-start = (bf16[32,8,512]{2,1,0:T(8,128)(2,1)S(1)}, bf16[32,8,512]{2,1,0:T(8,128)(2,1)S(1)}, u32[]{:S(2)}, u32[]{:S(2)}) collective-permute-start(bf16[32,8,512]{2,1,0:T(8,128)(2,1)S(1)} %copy.72), channel_id=1, source_target_pairs={{2,0},{4,2},{6,4},{8,6},{10,8},{12,10},{14,12},{16,14},{18,16},{20... | collective-permute-start | bytes 786440 | tf_op jit(solution)/shard_map/while/body/eval_jaxpr/ppermute | solution.py:15
  104.7 4.9 %copy-start = (bf16[1,64,32,512]{3,2,1,0:T(8,128)(2,1)S(1)}, bf16[1,64,32,512]{3,2,1,0:T(8,128)(2,1)}, u32[]{:S(2)}) copy-start(bf16[1,64,32,512]{3,2,1,0:T(8,128)(2,1)} %copy.65) | copy-start | bytes 6291460 | tf_op jit(solution)/shard_map/while
  122.7 41.0 %collective-permute-start = (bf16[32,8,512]{2,1,0:T(8,128)(2,1)S(1)}, bf16[32,8,512]{2,1,0:T(8,128)(2,1)S(1)}, u32[]{:S(2)}, u32[]{:S(2)}) collective-permute-start(bf16[32,8,512]{2,1,0:T(8,128)(2,1)S(1)} %copy.72), channel_id=1, source_target_pairs={{2,0},{4,2},{6,4},{8,6},{10,8},{12,10},{14,12},{16,14},{18,16},{20... | collective-permute-start | bytes 786440 | tf_op jit(solution)/shard_map/while/body/eval_jaxpr/ppermute | solution.py:15
  145.7 4.9 %copy-start = (bf16[1,64,32,512]{3,2,1,0:T(8,128)(2,1)S(1)}, bf16[1,64,32,512]{3,2,1,0:T(8,128)(2,1)}, u32[]{:S(2)}) copy-start(bf16[1,64,32,512]{3,2,1,0:T(8,128)(2,1)} %copy.65) | copy-start | bytes 6291460 | tf_op jit(solution)/shard_map/while
  163.7 41.6 %collective-permute-start = (bf16[32,8,512]{2,1,0:T(8,128)(2,1)S(1)}, bf16[32,8,512]{2,1,0:T(8,128)(2,1)S(1)}, u32[]{:S(2)}, u32[]{:S(2)}) collective-permute-start(bf16[32,8,512]{2,1,0:T(8,128)(2,1)S(1)} %copy.72), channel_id=1, source_target_pairs={{2,0},{4,2},{6,4},{8,6},{10,8},{12,10},{14,12},{16,14},{18,16},{20... | collective-permute-start | bytes 786440 | tf_op jit(solution)/shard_map/while/body/eval_jaxpr/ppermute | solution.py:15
  187.3 4.9 %copy-start = (bf16[1,64,32,512]{3,2,1,0:T(8,128)(2,1)S(1)}, bf16[1,64,32,512]{3,2,1,0:T(8,128)(2,1)}, u32[]{:S(2)}) copy-start(bf16[1,64,32,512]{3,2,1,0:T(8,128)(2,1)} %copy.65) | copy-start | bytes 6291460 | tf_op jit(solution)/shard_map/while
  205.3 41.0 %collective-permute-start = (bf16[32,8,512]{2,1,0:T(8,128)(2,1)S(1)}, bf16[32,8,512]{2,1,0:T(8,128)(2,1)S(1)}, u32[]{:S(2)}, u32[]{:S(2)}) collective-permute-start(bf16[32,8,512]{2,1,0:T(8,128)(2,1)S(1)} %copy.72), channel_id=1, source_target_pairs={{2,0},{4,2},{6,4},{8,6},{10,8},{12,10},{14,12},{16,14},{18,16},{20... | collective-permute-start | bytes 786440 | tf_op jit(solution)/shard_map/while/body/eval_jaxpr/ppermute | solution.py:15
  228.4 4.9 %copy-start = (bf16[1,64,32,512]{3,2,1,0:T(8,128)(2,1)S(1)}, bf16[1,64,32,512]{3,2,1,0:T(8,128)(2,1)}, u32[]{:S(2)}) copy-start(bf16[1,64,32,512]{3,2,1,0:T(8,128)(2,1)} %copy.65) | copy-start | bytes 6291460 | tf_op jit(solution)/shard_map/while
  246.4 42.4 %collective-permute-start = (bf16[32,8,512]{2,1,0:T(8,128)(2,1)S(1)}, bf16[32,8,512]{2,1,0:T(8,128)(2,1)S(1)}, u32[]{:S(2)}, u32[]{:S(2)}) collective-permute-start(bf16[32,8,512]{2,1,0:T(8,128)(2,1)S(1)} %copy.72), channel_id=1, source_target_pairs={{2,0},{4,2},{6,4},{8,6},{10,8},{12,10},{14,12},{16,14},{18,16},{20... | collective-permute-start | bytes 786440 | tf_op jit(solution)/shard_map/while/body/eval_jaxpr/ppermute | solution.py:15
  270.8 4.9 %copy-start = (bf16[1,64,32,512]{3,2,1,0:T(8,128)(2,1)S(1)}, bf16[1,64,32,512]{3,2,1,0:T(8,128)(2,1)}, u32[]{:S(2)}) copy-start(bf16[1,64,32,512]{3,2,1,0:T(8,128)(2,1)} %copy.65) | copy-start | bytes 6291460 | tf_op jit(solution)/shard_map/while
  288.8 41.0 %collective-permute-start = (bf16[32,8,512]{2,1,0:T(8,128)(2,1)S(1)}, bf16[32,8,512]{2,1,0:T(8,128)(2,1)S(1)}, u32[]{:S(2)}, u32[]{:S(2)}) collective-permute-start(bf16[32,8,512]{2,1,0:T(8,128)(2,1)S(1)} %copy.72), channel_id=1, source_target_pairs={{2,0},{4,2},{6,4},{8,6},{10,8},{12,10},{14,12},{16,14},{18,16},{20... | collective-permute-start | bytes 786440 | tf_op jit(solution)/shard_map/while/body/eval_jaxpr/ppermute | solution.py:15
  311.8 4.9 %copy-start = (bf16[1,64,32,512]{3,2,1,0:T(8,128)(2,1)S(1)}, bf16[1,64,32,512]{3,2,1,0:T(8,128)(2,1)}, u32[]{:S(2)}) copy-start(bf16[1,64,32,512]{3,2,1,0:T(8,128)(2,1)} %copy.65) | copy-start | bytes 6291460 | tf_op jit(solution)/shard_map/while
  329.9 41.6 %collective-permute-start = (bf16[32,8,512]{2,1,0:T(8,128)(2,1)S(1)}, bf16[32,8,512]{2,1,0:T(8,128)(2,1)S(1)}, u32[]{:S(2)}, u32[]{:S(2)}) collective-permute-start(bf16[32,8,512]{2,1,0:T(8,128)(2,1)S(1)} %copy.72), channel_id=1, source_target_pairs={{2,0},{4,2},{6,4},{8,6},{10,8},{12,10},{14,12},{16,14},{18,16},{20... | collective-permute-start | bytes 786440 | tf_op jit(solution)/shard_map/while/body/eval_jaxpr/ppermute | solution.py:15
  353.4 4.9 %copy-start = (bf16[1,64,32,512]{3,2,1,0:T(8,128)(2,1)S(1)}, bf16[1,64,32,512]{3,2,1,0:T(8,128)(2,1)}, u32[]{:S(2)}) copy-start(bf16[1,64,32,512]{3,2,1,0:T(8,128)(2,1)} %copy.65) | copy-start | bytes 6291460 | tf_op jit(solution)/shard_map/while
  393.0 8.2 %copy-start.2 = (f32[2048,400]{0,1:T(8,128)S(1)}, f32[2048,400]{0,1:T(8,128)}, u32[]{:S(2)}) copy-start(f32[2048,400]{0,1:T(8,128)} %fusion.36) | copy-start | bytes 9830404
where the time goes:
time: 420 us; the launch traced here: 416 us
  local copies, waits for them, and re-layouts  216 us (51%)
  matrix products  139 us (33%)
  loops' own time  27.4 us (7%)
  other arithmetic  13.1 us (3%)
  blocking collectives  9.94 us (2%)
  starting transfers between devices  8.08 us (2%)
    slice x18, local copies, waits for them, and re-layouts, correlate(): cross_spec[1]  101 us
    dot_general x9, matrix products, correlate(): jnp.dot(cross_spec[1], sin_tab, preferred_element_type=jnp.float32)  57.6 us
    slice x9, local copies, waits for them, and re-layouts, correlate(): cross_spec[0]  52.5 us
    dot_general x9, matrix products, correlate(): jnp.dot(cross_spec[0], cos_tab, preferred_element_type=jnp.float32)  45.9 us
    dot_general x9, matrix products, correlate(): jnp.einsum('prsf,csf->prcf', paired, columns, preferred_element_type=jnp....  35.7 us
    another operation x1, loops' own time, on_device(): lax.fori_loop(0, step_count - 1, advance, (whitened, output))  27.4 us
    convert_element_type x9, local copies, waits for them, and re-layouts, correlate(): ((real_part + orient * imag_part) * (scaling * keeper)).astype(jnp.bfloat16)  24.8 us
    dynamic_update_slice x9, local copies, waits for them, and re-layouts, correlate(): return lax.dynamic_update_slice(output, lagged, (0, out_slot, 0, 0, 0, 0))  13.2 us
  transfers between devices with their start and end apart: 8, of which 0 were waited for; matrix products, arithmetic and copies ran while one was open for 75% of the time, Pallas kernels for 0%

commit v1 on v0

--- a/solution.py
+++ b/solution.py
@@ -1,12 +1,17 @@
+import functools
 import math
 
 import jax
 import jax.numpy as jnp
 from jax import lax
+from jax.experimental import pallas as pl
+from jax.experimental.pallas import tpu as pltpu
 from jax.sharding import PartitionSpec as P
 
 NFFT = 2000
 HALF_LAG = 200
+LANES = 128
+PACK = 16
 
 
 def passed_along(block, axis, distance):
@@ -31,6 +36,161 @@
     cos_tab = (weights * jnp.cos(angles)).astype(jnp.bfloat16)
     sin_tab = (-weights * jnp.sin(angles)).astype(jnp.bfloat16)
     return (cos_tab, sin_tab)
+
+
+def tree_sum(terms):
+    while len(terms) > 1:
+        paired = [a + b for a, b in zip(terms[::2], terms[1::2])]
+        terms = paired + terms[len(terms) - len(terms) % 2:]
+    return terms[0]
+
+
+def correlate_kernel(info, row_ids, col_ids, table, own, partner, *rest, scale, chunk):
+    out, rows, sign, cols, sems, cross_a, cross_b = rest[-7:]
+    count = cols.shape[0]
+    col_hbm = rest[:count]
+    crosses = (cross_a, cross_b)
+    parts, col_count, freq_count = own.shape
+    seg_count = parts // 2
+    row_count = rows.shape[0]
+    step = pl.program_id(0)
+    group = info[2 * count]
+
+    def fetch(k):
+        return pltpu.make_async_copy(col_hbm[k], cols.at[k], sems.at[k])
+
+    @pl.when(step == 0)
+    def _():
+        for k in range(count):
+            fetch(k).start()
+        for source, first in ((own, group * col_count), (partner, (1 - group) * col_count)):
+            for i in range(col_count):
+                for s in range(parts):
+                    line = source[s, i:i + 1, :]
+                    rows[first + i, s] = jnp.broadcast_to(line, (PACK, freq_count))
+
+    for k in range(count):
+        @pl.when(step == k)
+        def _():
+            fetch(k).wait()
+
+    ids = col_ids[0]
+
+    def mark(i, carry):
+        sign[i] = jnp.where(row_ids[i] < ids, 1.0, -1.0).astype(jnp.bfloat16)
+        return carry
+
+    lax.fori_loop(0, row_count, mark, 0)
+    columns = cols.at[step]
+
+    def form(cross, first):
+        for tile in range(freq_count // LANES):
+            lane = pl.ds(tile * LANES, LANES)
+            c = [columns[s, :, lane] for s in range(parts)]
+            for i in range(chunk):
+                r = [jnp.concatenate([rows[first + i, s, :, lane]] * (col_count // PACK), axis=0) for s in range(parts)]
+                re = tree_sum([r[s] * c[s] for s in range(parts)])
+                im = tree_sum([r[seg_count + s] * c[s] - r[s] * c[seg_count + s] for s in range(seg_count)])
+                here = pl.ds(i * col_count, col_count)
+                cross[here, pl.ds(tile * LANES, LANES)] = re
+                cross[here, pl.ds(freq_count + tile * LANES, LANES)] = im * sign[first + i]
+
+    def transform(cross, first):
+        lagged = jnp.dot(cross[...], table[...], preferred_element_type=jnp.float32) * scale
+        out[0, 0, 0, pl.ds(first, chunk)] = lagged.astype(jnp.bfloat16).reshape(chunk, col_count, -1)
+
+    form(crosses[0], 0)
+    for k in range(row_count // chunk):
+        if (k + 1) * chunk < row_count:
+            form(crosses[(k + 1) % 2], (k + 1) * chunk)
+        transform(crosses[k % 2], k * chunk)
+
+    @pl.when(info[count + step] == 0)
+    def _():
+        for j in range(col_count):
+            out[0, 0, 0, group * col_count + j, j:j + 1, :] = jnp.zeros((1, out.shape[-1]), jnp.bfloat16)
+
+
+def correlate(info, row_ids, col_ids, table, own, partner, columns, output, step_count, scale):
+    count = len(columns)
+    parts, col_count, freq_count = own.shape
+    row_count = 2 * col_count
+    lag_count = table.shape[-1]
+    kept = [] if output is None else [output]
+    chunk = 32
+
+    def whole(array):
+        return pl.BlockSpec(array.shape, lambda d, *_: (0,) * array.ndim)
+
+    return pl.pallas_call(
+        functools.partial(correlate_kernel, scale=scale, chunk=chunk),
+        grid_spec=pltpu.PrefetchScalarGridSpec(
+            num_scalar_prefetch=2,
+            grid=(count,),
+            in_specs=[
+                pl.BlockSpec((1, col_count, LANES), lambda d, *_: (d, 0, 0)),
+                whole(table),
+                whole(own),
+                whole(partner),
+            ] + [pl.BlockSpec(memory_space=pl.ANY)] * (count + len(kept)),
+            out_specs=pl.BlockSpec(
+                (1, 1, 1, row_count, col_count, lag_count),
+                lambda d, info, _: (0, info[d], 0, 0, 0, 0),
+            ),
+            scratch_shapes=[
+                pltpu.VMEM((row_count, parts, PACK, freq_count), jnp.bfloat16),
+                pltpu.VMEM((row_count, col_count, LANES), jnp.bfloat16),
+                pltpu.VMEM((count, parts, col_count, freq_count), jnp.bfloat16),
+                pltpu.SemaphoreType.DMA((count,)),
+                pltpu.VMEM((chunk * col_count, 2 * freq_count), jnp.bfloat16),
+                pltpu.VMEM((chunk * col_count, 2 * freq_count), jnp.bfloat16),
+            ],
+        ),
+        out_shape=jax.ShapeDtypeStruct((1, step_count, 1, row_count, col_count, lag_count), jnp.bfloat16),
+        input_output_aliases={6 + count: 0} if kept else {},
+        compiler_params=pltpu.CompilerParams(vmem_limit_bytes=56 << 20),
+    )(info, row_ids, col_ids, table, own, partner, *columns, *kept)
+
+
+def on_device_fused(spectra, channel_ids, plan):
+    col_count, _, seg_count, freq_count = spectra.shape
+    own = jnp.transpose(whiten(spectra), (1, 0, 2))
+    partner = passed_along(own, "grp", 1)
+    blk_count = lax.axis_size("blk")
+    row_count = 2 * col_count
+    step_count = blk_count // 2 + 1
+    blk_index = lax.axis_index("blk")
+    group = lax.axis_index("grp")
+    odd = blk_index % 2 == 1
+
+    even = [own, passed_along(own, "blk", -2), passed_along(own, "blk", -4)]
+    while 2 * (len(even) - 1) < step_count - 1:
+        even.append(passed_along(even[-1], "blk", -2) if len(even) % 2 else passed_along(even[-2], "blk", -4))
+    columns = []
+    for d in range(step_count):
+        if d % 2 == 0:
+            columns.append(even[d // 2])
+        else:
+            given = jnp.where(odd, even[d // 2], even[d // 2 + 1])
+            columns.append(lax.ppermute(given, "blk", [(i ^ 1, i) for i in range(blk_count)]))
+
+    cos_tab, sin_tab = lag_tables(freq_count)
+    table = jnp.concatenate([cos_tab, sin_tab], axis=0)
+    scale = 1.0 / math.sqrt(2.0 * freq_count * seg_count)
+    row_ids = lax.dynamic_slice_in_dim(channel_ids, blk_index * row_count, row_count, 0)
+    offsets = jnp.arange(step_count, dtype=jnp.int32)
+    slots = jnp.sum(jnp.where(plan[0][None, :] == offsets[:, None], offsets[None, :], 0), axis=1)
+    id_table = channel_ids.reshape(blk_count, lax.axis_size("grp"), col_count)[:, group]
+    id_table = jnp.concatenate([id_table, id_table], axis=0)
+    col_ids = lax.dynamic_slice_in_dim(id_table, blk_index, step_count, 0)
+    col_ids = jnp.broadcast_to(col_ids[:, :, None], (step_count, col_count, LANES))
+
+    output = None
+    cuts = [0, 1, step_count // 2 + 1, step_count]
+    for lo, hi in zip(cuts[:-1], cuts[1:]):
+        info = jnp.concatenate([slots[lo:hi], offsets[lo:hi], group[None]])
+        output = correlate(info, row_ids, col_ids[lo:hi], table, own, partner, columns[lo:hi], output, step_count, scale)
+    return output
 
 
 def on_device(spectra, channel_ids, plan):
@@ -54,7 +214,7 @@
     slot_list = jnp.arange(step_count, dtype=jnp.int32)
     scaling = 1.0 / math.sqrt(2.0 * freq_count * seg_count)
 
-    def correlate(offset, columns, output):
+    def correlate_one(offset, columns, output):
         col_start = (blk_index + offset) % blk_count * row_count + grp_index * col_count
         col_ids = lax.dynamic_slice_in_dim(channel_ids, col_start, col_count, 0)
         col_slots = col_start + jnp.arange(col_count, dtype=jnp.int32)
@@ -79,20 +239,27 @@
 
     def advance(offset, carry):
         columns, output = carry
-        output = correlate(offset, columns, output)
+        output = correlate_one(offset, columns, output)
         columns = passed_along(columns, "blk", -1)
         return (columns, output)
 
     columns, output = lax.fori_loop(0, step_count - 1, advance, (whitened, output))
-    output = correlate(step_count - 1, columns, output)
+    output = correlate_one(step_count - 1, columns, output)
     return output
 
 
 def solution(mesh):
-    return jax.shard_map(
-        on_device,
-        mesh=mesh,
-        in_specs=(P(("blk", "grp"), None, None, None), P(), P("blk", None)),
-        out_specs=P("blk", None, "grp", None, None, None),
-        check_vma=False,
-    )
+    blk_count, grp_count = mesh.shape["blk"], mesh.shape["grp"]
+
+    def program(spectra, channel_ids, plan):
+        col_count = spectra.shape[0] // (blk_count * grp_count)
+        fused = col_count % (2 * PACK) == 0 and grp_count == 2 and blk_count % 8 == 0
+        return jax.shard_map(
+            on_device_fused if fused else on_device,
+            mesh=mesh,
+            in_specs=(P(("blk", "grp"), None, None, None), P(), P("blk", None)),
+            out_specs=P("blk", None, "grp", None, None, None),
+            check_vma=False,
+        )(spectra, channel_ids, plan)
+
+    return program

time: 420 us -> 92.5 us (0.22)
  local copies, waits for them, and re-layouts: 216 us -> 4.66 us
  matrix products: 139 us -> 0 us
  Pallas kernels: 0 us -> 54.6 us
  loops' own time: 27.4 us -> 0 us
  waiting for transfers between devices: 0.02 us -> 11.4 us
  blocking collectives: 9.94 us -> 0 us
    slice x27 -> x5, local copies, waits for them, and re-layouts: 153 us -> 0.22 us  [the longest x3 0.22 us: on_device_fused(): info = jnp.concatenate([slots[lo:hi], offsets[lo:hi], group[None]])]
    dot_general x27 -> x0, matrix products: 139 us -> none  [the longest x9 57.6 us: correlate(): jnp.dot(cross_spec[1], sin_tab, preferred_element_type=jnp.float32)]
    pallas_call x0 -> x3, Pallas kernels: none -> 54.6 us  [correlate(): pl.pallas_call(functools.partial(correlate_kernel, scale=scale, chunk=chu...]
    another operation x1 -> x0, loops' own time: 27.4 us -> none  [on_device(): lax.fori_loop(0, step_count - 1, advance, (whitened, output))]
    convert_element_type x9 -> x1, local copies, waits for them, and re-layouts: 24.8 us -> 0.08 us  [whiten(): whitened = whitened.astype(jnp.bfloat16)]
    dynamic_update_slice x9 -> x0, local copies, waits for them, and re-layouts: 13.2 us -> none  [correlate(): return lax.dynamic_update_slice(output, lagged, (0, out_slot, 0, 0, 0, 0))]
    ppermute x8 -> x5, waiting for transfers between devices: 0.02 us -> 11.3 us  [passed_along(): return lax.ppermute(block, axis, route)]
    all_gather x1 -> x0, blocking collectives: 9.94 us -> none  [on_device(): row_block = lax.all_gather(whitened, 'grp', axis=0, tiled=True)]
  transfers between devices with their start and end apart: 8 -> 9, of which waited for: 0 -> 3; matrix products, arithmetic and copies ran while one was open for 75% -> 13% of each run, Pallas kernels for 0% -> 35%
where the time goes in v1:
time: 92.5 us; the launch traced here: 92 us
  Pallas kernels  54.6 us (59%)
  waiting for transfers between devices  11.4 us (12%)
  other arithmetic  11 us (12%)
  starting transfers between devices  10 us (11%)
  local copies, waits for them, and re-layouts  4.66 us (5%)
    pallas_call x3, Pallas kernels, correlate(): pl.pallas_call(functools.partial(correlate_kernel, scale=scale, chunk=chu...  54.6 us
    ppermute x5, waiting for transfers between devices, passed_along(): return lax.ppermute(block, axis, route)  11.3 us
    ppermute x5, starting transfers between devices, passed_along(): return lax.ppermute(block, axis, route)  8.98 us
    convert_element_type x1, other arithmetic, lag_tables(): cos_tab = (weights * jnp.cos(angles)).astype(jnp.bfloat16)  4.56 us
    broadcast_in_dim x3, local copies, waits for them, and re-layouts, on_device_fused(): jnp.broadcast_to(col_ids[:, :, None], (step_count, col_count, LANES))  2.29 us
  transfers between devices with their start and end apart: 9, of which 3 were waited for; matrix products, arithmetic and copies ran while one was open for 13% of the time, Pallas kernels for 35%

profile of v1, /device:TPU:0, one launch (start us, length us, event | category | flops | bytes accessed | tf_op | source)
XLA Modules:
  0.0 92.0 jit_solution(13514791833790953400)
XLA Ops:
  0.0 1.2 %multiply_reduce_fusion = f32[32,4]{1,0:T(8,128)S(1)} fusion(f32[32,2,4,512]{3,2,1,0:T(4,128)} %param.3), kind=kLoop, calls=%fused_computation.11 | loop fusion | flops 262016 | bytes 524800 | tf_op jit(solution)/shard_map/reduce_sum | solution.py:24
  1.2 1.2 %multiply_convert_fusion.2 = bf16[32,2,4,512]{3,2,1,0:T(4,128)(2,1)S(1)} fusion(f32[32,2,4,512]{3,2,1,0:T(4,128)} %param.3, f32[32,4]{1,0:T(8,128)S(1)} %add_rsqrt_fusion), kind=kLoop, calls=%fused_computation.10 | loop fusion | flops 262144 | bytes 786944 | tf_op jit(solution)/shard_map/convert_element_type | solution.py:26
  2.5 5.1 %collective-permute-start.1 = (bf16[8,32,512]{2,1,0:T(8,128)(2,1)S(1)}, bf16[8,32,512]{2,1,0:T(8,128)(2,1)S(1)}, u32[]{:S(2)}, u32[]{:S(2)}) collective-permute-start(bf16[8,32,512]{2,1,0:T(8,128)(2,1)S(1)} %bitcast.11), channel_id=1, source_target_pairs={{8,0},{10,2},{12,4},{14,6},{16,8},{18,10},{20,12},{22,14},{24,16},... | collective-permute-start | bytes 786440 | tf_op jit(solution)/shard_map/ppermute | solution.py:20
  7.6 1.4 %collective-permute-start.6 = (bf16[8,32,512]{2,1,0:T(8,128)(2,1)S(1)}, bf16[8,32,512]{2,1,0:T(8,128)(2,1)S(1)}, u32[]{:S(2)}, u32[]{:S(2)}) collective-permute-start(bf16[8,32,512]{2,1,0:T(8,128)(2,1)S(1)} %bitcast.12), channel_id=1, source_target_pairs={{4,0},{6,2},{8,4},{10,6},{12,8},{14,10},{16,12},{18,14},{20,16},{2... | collective-permute-start | bytes 786440 | tf_op jit(solution)/shard_map/ppermute | solution.py:20
  9.0 1.5 %collective-permute-start = (bf16[8,32,512]{2,1,0:T(8,128)(2,1)S(1)}, bf16[8,32,512]{2,1,0:T(8,128)(2,1)S(1)}, u32[]{:S(2)}, u32[]{:S(2)}) collective-permute-start(bf16[8,32,512]{2,1,0:T(8,128)(2,1)S(1)} %bitcast.13), channel_id=1, source_target_pairs={{1,0},{0,1},{3,2},{2,3},{5,4},{4,5},{7,6},{6,7},{9,8},{8,9},{11,10... | collective-permute-start | bytes 786440 | tf_op jit(solution)/shard_map/ppermute | solution.py:20
  10.5 0.8 reshape.27
  11.3 0.8 select_reduce_fusion
  12.1 4.6 %multiply_convert_fusion.1 = (bf16[512,400]{1,0:T(8,128)(2,1)S(1)}, bf16[512,400]{1,0:T(8,128)(2,1)S(1)}) fusion(s32[400]{0:T(512)S(1)} %iota_add_fusion, f32[512]{0:T(512)S(1)} %get-tuple-element.17, f32[512]{0:T(512)S(1)} %get-tuple-element.18), kind=kLoop, calls=%fused_computation.5 | loop fusion | flops 2662400 | bytes 824896 | tf_op jit(solution)/shard_map/convert_element_type | solution.py:36
  16.7 1.1 %pad_maximum_fusion.table = bf16[1024,400]{1,0:T(8,128)(2,1)} fusion(bf16[512,400]{1,0:T(8,128)(2,1)S(1)} %get-tuple-element.12, bf16[512,400]{1,0:T(8,128)(2,1)S(1)} %get-tuple-element.11), kind=kLoop, calls=%fused_computation.3 | loop fusion | flops 1638400 | bytes 1638400 | tf_op jit(solution)/shard_map/concatenate | solution.py:178
  18.0 0.5 collective-permute-start.2
  19.0 0.6 add_add_fusion
  19.9 5.6 %collective-permute-done.2.rest_1_ = bf16[8,32,512]{2,1,0:T(8,128)(2,1)S(1)} collective-permute-done((bf16[8,32,512]{2,1,0:T(8,128)(2,1)S(1)}, bf16[8,32,512]{2,1,0:T(8,128)(2,1)S(1)}, u32[]{:S(2)}, u32[]{:S(2)}) %collective-permute-start.2) | collective-permute-done | bytes 262176 | tf_op jit(solution)/shard_map/ppermute | solution.py:20
  25.5 5.4 %collective-permute-done.4.rest_3_ = bf16[8,32,512]{2,1,0:T(8,128)(2,1)S(1)} collective-permute-done((bf16[8,32,512]{2,1,0:T(8,128)(2,1)S(1)}, bf16[8,32,512]{2,1,0:T(8,128)(2,1)S(1)}, u32[]{:S(2)}, u32[]{:S(2)}) %collective-permute-start.4) | collective-permute-done | bytes 262176 | tf_op jit(solution)/shard_map/ppermute | solution.py:20
  31.0 0.8 broadcast_select_fusion
  31.8 0.5 collective-permute-start.8
  32.3 0.5 collective-permute-start.5
  32.8 0.7 pad_add_fusion.info
  33.5 1.2 %dynamic_slice.9.row_ids = s32[64]{0:T(128)} dynamic-slice(s32[1024]{0:T(1024)} %param.4, s32[]{:T(128)S(6)} %select_n.62), dynamic_slice_sizes={64} | dynamic-slice | bytes 516 | tf_op jit(solution)/shard_map/dynamic_slice | solution.py:180
  34.8 0.7 broadcast_in_dim.48.col_ids
  35.5 9.3 %shard_map.37.rest_4_ = bf16[1,9,1,64,32,400]{5,4,3,2,1,0:T(8,128)(2,1)} custom-call(s32[3]{0:T(128)} %pad_add_fusion.info, s32[64]{0:T(128)} %dynamic_slice.9.row_ids, s32[1,32,128]{2,1,0:T(8,128)} %broadcast_in_dim.48.col_ids, bf16[1024,400]{1,0:T(8,128)(2,1)} %pad_maximum_fusion.table, bf16[8,32,512]{2,1,0:T(8,128)(2,1)} %bitcast.14, ...), custom_call_target="tpu_custom_call" | custom-call | tf_op jit(solution)/shard_map/pallas_call | solution.py:125
  44.9 0.8 broadcast_in_dim.47.col_ids
  45.7 22.7 %shard_map.38.rest_4_ = bf16[1,9,1,64,32,400]{5,4,3,2,1,0:T(8,128)(2,1)} custom-call(s32[9]{0:T(128)} %get-tuple-element.16.info, s32[64]{0:T(128)} %dynamic_slice.9.row_ids, s32[4,32,128]{2,1,0:T(8,128)} %broadcast_in_dim.47.col_ids, bf16[1024,400]{1,0:T(8,128)(2,1)} %pad_maximum_fusion.table, ...), custom_call_target="tpu_custom_call", output_to_operand_aliasing={{}: (10, {})} | custom-call | tf_op jit(solution)/shard_map/pallas_call | solution.py:125
  68.4 0.8 broadcast_in_dim.44.col_ids
  69.2 22.7 %shard_map.39 = bf16[1,9,1,64,32,400]{5,4,3,2,1,0:T(8,128)(2,1)} custom-call(s32[9]{0:T(128)} %get-tuple-element.15.info, s32[64]{0:T(128)} %dynamic_slice.9.row_ids, s32[4,32,128]{2,1,0:T(8,128)} %broadcast_in_dim.44.col_ids, bf16[1024,400]{1,0:T(8,128)(2,1)} %pad_maximum_fusion.table, ...), custom_call_target="tpu_custom_call", output_to_operand_aliasing={{}: (10, {})} | custom-call | tf_op jit(solution)/shard_map/pallas_call | solution.py:125
  (44 shorter events, 1.1 us)
Async XLA Ops:
  2.5 33.0 %copy-start = (bf16[32,2,4,512]{3,0,2,1:T(8,128)(2,1)}, bf16[32,2,4,512]{3,0,2,1:T(8,128)(2,1)S(1)}, u32[]{:S(2)}) copy-start(bf16[32,2,4,512]{3,0,2,1:T(8,128)(2,1)S(1)} %copy.13) | copy-start | bytes 786436
  2.5 15.5 %collective-permute-start.1 = (bf16[8,32,512]{2,1,0:T(8,128)(2,1)S(1)}, bf16[8,32,512]{2,1,0:T(8,128)(2,1)S(1)}, u32[]{:S(2)}, u32[]{:S(2)}) collective-permute-start(bf16[8,32,512]{2,1,0:T(8,128)(2,1)S(1)} %bitcast.11), channel_id=1, source_target_pairs={{8,0},{10,2},{12,4},{14,6},{16,8},{18,10},{20,12},{22,14},{24,16},... | collective-permute-start | bytes 786440 | tf_op jit(solution)/shard_map/ppermute | solution.py:20
  7.6 12.2 %collective-permute-start.6 = (bf16[8,32,512]{2,1,0:T(8,128)(2,1)S(1)}, bf16[8,32,512]{2,1,0:T(8,128)(2,1)S(1)}, u32[]{:S(2)}, u32[]{:S(2)}) collective-permute-start(bf16[8,32,512]{2,1,0:T(8,128)(2,1)S(1)} %bitcast.12), channel_id=1, source_target_pairs={{4,0},{6,2},{8,4},{10,6},{12,8},{14,10},{16,12},{18,14},{20,16},{2... | collective-permute-start | bytes 786440 | tf_op jit(solution)/shard_map/ppermute | solution.py:20
  9.0 25.8 %collective-permute-start = (bf16[8,32,512]{2,1,0:T(8,128)(2,1)S(1)}, bf16[8,32,512]{2,1,0:T(8,128)(2,1)S(1)}, u32[]{:S(2)}, u32[]{:S(2)}) collective-permute-start(bf16[8,32,512]{2,1,0:T(8,128)(2,1)S(1)} %bitcast.13), channel_id=1, source_target_pairs={{1,0},{0,1},{3,2},{2,3},{5,4},{4,5},{7,6},{6,7},{9,8},{8,9},{11,10... | collective-permute-start | bytes 786440 | tf_op jit(solution)/shard_map/ppermute | solution.py:20
  18.0 27.6 %copy-start.2 = (bf16[8,32,512]{2,1,0:T(8,128)(2,1)}, bf16[8,32,512]{2,1,0:T(8,128)(2,1)S(1)}, u32[]{:S(2)}) copy-start(bf16[8,32,512]{2,1,0:T(8,128)(2,1)S(1)} %collective-permute-done.1.rest_3_) | copy-start | bytes 786436
  18.0 7.5 %collective-permute-start.2 = (bf16[8,32,512]{2,1,0:T(8,128)(2,1)S(1)}, bf16[8,32,512]{2,1,0:T(8,128)(2,1)S(1)}, u32[]{:S(2)}, u32[]{:S(2)}) collective-permute-start(bf16[8,32,512]{2,1,0:T(8,128)(2,1)S(1)} %collective-permute-done.1.rest_3_), channel_id=1, source_target_pairs={{4,0},{6,2},{8,4},{10,6},{12,8},{14,10},{16,12},{18,14},{20,16},{2... | collective-permute-start | bytes 786440 | tf_op jit(solution)/shard_map/ppermute | solution.py:20
  18.6 12.4 %collective-permute-start.4 = (bf16[8,32,512]{2,1,0:T(8,128)(2,1)S(1)}, bf16[8,32,512]{2,1,0:T(8,128)(2,1)S(1)}, u32[]{:S(2)}, u32[]{:S(2)}) collective-permute-start(bf16[8,32,512]{2,1,0:T(8,128)(2,1)S(1)} %collective-permute-done.1.rest_3_), channel_id=1, source_target_pairs={{8,0},{10,2},{12,4},{14,6},{16,8},{18,10},{20,12},{22,14},{24,16},... | collective-permute-start | bytes 786440 | tf_op jit(solution)/shard_map/ppermute | solution.py:20
  19.9 25.8 %copy-start.3 = (bf16[8,32,512]{2,1,0:T(8,128)(2,1)}, bf16[8,32,512]{2,1,0:T(8,128)(2,1)S(1)}, u32[]{:S(2)}) copy-start(bf16[8,32,512]{2,1,0:T(8,128)(2,1)S(1)} %collective-permute-done.6.rest_1_) | copy-start | bytes 786436
  25.5 42.8 %copy-start.4 = (bf16[8,32,512]{2,1,0:T(8,128)(2,1)}, bf16[8,32,512]{2,1,0:T(8,128)(2,1)S(1)}, u32[]{:S(2)}) copy-start(bf16[8,32,512]{2,1,0:T(8,128)(2,1)S(1)} %collective-permute-done.2.rest_1_) | copy-start | bytes 786436
  31.0 37.4 %copy-start.5 = (bf16[8,32,512]{2,1,0:T(8,128)(2,1)}, bf16[8,32,512]{2,1,0:T(8,128)(2,1)S(1)}, u32[]{:S(2)}) copy-start(bf16[8,32,512]{2,1,0:T(8,128)(2,1)S(1)} %collective-permute-done.4.rest_3_) | copy-start | bytes 786436
  31.8 13.0 %collective-permute-start.7 = (bf16[8,32,512]{2,1,0:T(8,128)(2,1)}, bf16[8,32,512]{2,1,0:T(8,128)(2,1)S(1)}, u32[]{:S(2)}, u32[]{:S(2)}) collective-permute-start(bf16[8,32,512]{2,1,0:T(8,128)(2,1)} %get-tuple-element.8), channel_id=1, source_target_pairs={{2,0},{0,2},{6,4},{4,6},{10,8},{8,10},{14,12},{12,14},{18,16},{16,... | collective-permute-start | bytes 786440 | tf_op jit(solution)/shard_map/ppermute | solution.py:175
  31.8 13.0 %collective-permute-start.8 = (bf16[8,32,512]{2,1,0:T(8,128)(2,1)S(1)}, bf16[8,32,512]{2,1,0:T(8,128)(2,1)S(1)}, u32[]{:S(2)}, u32[]{:S(2)}) collective-permute-start(bf16[8,32,512]{2,1,0:T(8,128)(2,1)S(1)} %get-tuple-element.5), channel_id=1, source_target_pairs={{2,0},{0,2},{6,4},{4,6},{10,8},{8,10},{14,12},{12,14},{18,16},{16,... | collective-permute-start | bytes 786440 | tf_op jit(solution)/shard_map/ppermute | solution.py:175
  32.3 36.0 %collective-permute-start.3 = (bf16[8,32,512]{2,1,0:T(8,128)(2,1)S(1)}, bf16[8,32,512]{2,1,0:T(8,128)(2,1)S(1)}, u32[]{:S(2)}, u32[]{:S(2)}) collective-permute-start(bf16[8,32,512]{2,1,0:T(8,128)(2,1)S(1)} %get-tuple-element.6), channel_id=1, source_target_pairs={{2,0},{0,2},{6,4},{4,6},{10,8},{8,10},{14,12},{12,14},{18,16},{16,... | collective-permute-start | bytes 786440 | tf_op jit(solution)/shard_map/ppermute | solution.py:175
  32.3 36.1 %collective-permute-start.5 = (bf16[8,32,512]{2,1,0:T(8,128)(2,1)S(1)}, bf16[8,32,512]{2,1,0:T(8,128)(2,1)S(1)}, u32[]{:S(2)}, u32[]{:S(2)}) collective-permute-start(bf16[8,32,512]{2,1,0:T(8,128)(2,1)S(1)} %get-tuple-element.7), channel_id=1, source_target_pairs={{2,0},{0,2},{6,4},{4,6},{10,8},{8,10},{14,12},{12,14},{18,16},{16,... | collective-permute-start | bytes 786440 | tf_op jit(solution)/shard_map/ppermute | solution.py:175
  34.8 0.7 copy-start.1
  44.8 0.8 copy-start.8
  44.8 0.8 copy-start.9
  68.4 0.8 copy-start.6
  68.4 0.8 copy-start.7

commit v2 on v0

--- a/solution.py
+++ b/solution.py
@@ -1,12 +1,23 @@
+import functools
 import math
 
 import jax
 import jax.numpy as jnp
 from jax import lax
+from jax.experimental import pallas as pl
+from jax.experimental.pallas import tpu as pltpu
 from jax.sharding import PartitionSpec as P
 
 NFFT = 2000
 HALF_LAG = 200
+LANES = 128
+PACK = 16
+TURN = 16
+REST = 72
+MIDDLE = 56
+TOGETHER = 4
+DELAY = 2
+HELD_ROWS = 1024
 
 
 def passed_along(block, axis, distance):
@@ -31,6 +42,213 @@
     cos_tab = (weights * jnp.cos(angles)).astype(jnp.bfloat16)
     sin_tab = (-weights * jnp.sin(angles)).astype(jnp.bfloat16)
     return (cos_tab, sin_tab)
+
+
+def tree_sum(terms):
+    while len(terms) > 1:
+        paired = [a + b for a, b in zip(terms[::2], terms[1::2])]
+        terms = paired + terms[len(terms) - len(terms) % 2:]
+    return terms[0]
+
+
+def half_lag_tables(freq_count, scale):
+    tile = lax.broadcasted_iota(jnp.int32, (2, freq_count, LANES), 0)
+    freq = lax.broadcasted_iota(jnp.int32, (2, freq_count, LANES), 1)
+    lane = lax.broadcasted_iota(jnp.int32, (2, freq_count, LANES), 2)
+    wrapped = jnp.where(lane <= TURN, MIDDLE + LANES + lane, MIDDLE + lane)
+    lag = jnp.where(tile == 0, wrapped, jnp.where(lane <= TURN, MIDDLE + lane, jnp.maximum(lane - REST, 0)))
+    angles = 2.0 * math.pi / NFFT * (freq * lag % NFFT).astype(jnp.float32)
+    weights = jnp.where(freq == 0, scale, 2.0 * scale)
+    return (weights * jnp.cos(angles)).astype(jnp.bfloat16), (-weights * jnp.sin(angles)).astype(jnp.bfloat16)
+
+
+def correlate_kernel(place, channels, plan, row_ids, cos_tab, sin_tab, own, partner, *rest, first, picks):
+    out, rows, turn, cols, sems = rest[-5:]
+    count = cols.shape[0]
+    tiles, parts, col_count, _ = own.shape
+    seg_count = parts // 2
+    row_count = rows.shape[0]
+    depth = 2 * LANES
+    blk, group, blk_count = place[0], place[1], place[2]
+    step = pl.program_id(0)
+
+    def fetch(k):
+        source, index = picks[k]
+        array = rest[source] if index is None else rest[source].at[index]
+        return pltpu.make_async_copy(array, cols.at[k], sems.at[k])
+
+    @pl.when(step == 0)
+    def _():
+        for k in range(count):
+            fetch(k).start()
+        for source, start in ((own, group * col_count), (partner, (1 - group) * col_count)):
+            def spread(n, carry, source=source, start=start):
+                q, s = n // parts, n % parts
+                for b in range(0, col_count, PACK):
+                    lines = source[q, s, b:b + PACK, :]
+                    for k in range(PACK):
+                        rows[start + b + k, q, s] = jnp.broadcast_to(lines[k:k + 1, :], (PACK, LANES))
+                return carry
+
+            lax.fori_loop(0, tiles * parts, spread, 0)
+
+    for k in range(count):
+        @pl.when(step == k)
+        def _(k=k):
+            fetch(k).wait()
+
+    id_line = row_ids[0]
+    col_start = (blk + first + step) % blk_count * row_count + group * col_count
+    for j in range(col_count):
+        turn[j:j + 1, :] = jnp.where(id_line < channels[col_start + j], 1.0, -1.0)
+
+    lane = lax.broadcasted_iota(jnp.int32, (col_count, LANES), 1)
+    low = lane <= TURN
+    late = lane >= REST
+    mirror = (TURN - lane) & (LANES - 1)
+
+    def form(c, i, tile):
+        r = [jnp.concatenate([rows[i, tile, s]] * (col_count // PACK), axis=0) for s in range(parts)]
+        re = tree_sum([r[s] * c[s] for s in range(parts)])
+        im = tree_sum([r[seg_count + s] * c[s] - r[s] * c[seg_count + s] for s in range(seg_count)])
+        return re, im
+
+    def push(h):
+        deep = pl.ds(h * depth, depth)
+        for unit, tab in enumerate((cos_tab, sin_tab)):
+            side = jnp.concatenate([tab[0, deep, :], tab[1, deep, :]], axis=1)
+            pltpu.matmul_push_rhs(side, staging_register=h % 2, mxu_index=unit)
+
+    def finish(i, even, odd):
+        sign = jnp.broadcast_to(turn[:, i:i + 1], (col_count, LANES))
+        odd_u, odd_v = odd[:, :LANES] * sign, odd[:, LANES:] * sign
+        even_u, even_v = even[:, :LANES], even[:, LANES:]
+        ahead_u = (even_u + odd_u).astype(jnp.bfloat16)
+        ahead_v = (even_v + odd_v).astype(jnp.bfloat16)
+        back_u = jnp.take_along_axis(even_u - odd_u, mirror, axis=1, mode="promise_in_bounds")
+        back_v = jnp.take_along_axis(even_v - odd_v, mirror, axis=1, mode="promise_in_bounds")
+        line = out.at[0, 0, 0, i]
+        line[:, 0:LANES] = back_u.astype(jnp.bfloat16)
+        line[:, LANES:2 * LANES] = jnp.where(late, ahead_v, back_v.astype(jnp.bfloat16))
+        line[:, 2 * LANES:3 * LANES] = jnp.where(low, ahead_v, ahead_u)
+        line[:, 3 * LANES:] = ahead_u[:, :out.shape[-1] - 3 * LANES]
+
+    def multiply(*sums):
+        held = len(sums) // 2
+        sums_even, sums_odd = sums[:held], sums[held:]
+        halves = tiles // 2
+        push(0)
+        for block in range(0, row_count, held):
+            for h in range(halves):
+                if h + 1 < halves or block + held < row_count:
+                    push((h + 1) % halves)
+                for g0 in range(0, held, TOGETHER):
+                    formed = []
+                    for tile in (2 * h, 2 * h + 1):
+                        c = [cols[step, tile, s] for s in range(parts)]
+                        formed.append([form(c, block + g0 + k, tile) for k in range(TOGETHER)])
+                    for k in range(TOGETHER):
+                        g = g0 + k
+                        fresh = h % 2 if g == 0 else None
+                        for part, held_sums in enumerate((sums_even, sums_odd)):
+                            side = jnp.concatenate([formed[0][k][part], formed[1][k][part]], axis=1)
+                            pltpu.matmul_acc_lhs(held_sums[g], side, load_staged_rhs=fresh)
+                        if h == halves - 1 and g >= DELAY:
+                            finish(block + g - DELAY, pltpu.matmul_pop(sums_even[g - DELAY]), pltpu.matmul_pop(sums_odd[g - DELAY]))
+            for g in range(held - DELAY, held):
+                finish(block + g, pltpu.matmul_pop(sums_even[g]), pltpu.matmul_pop(sums_odd[g]))
+
+    held = min(row_count, HELD_ROWS // col_count)
+    pl.run_scoped(
+        multiply,
+        *[pltpu.ACC(0)((col_count, depth), jnp.float32)] * held,
+        *[pltpu.ACC(1)((col_count, depth), jnp.float32)] * held,
+    )
+
+    if first == 0:
+        @pl.when(step == 0)
+        def _():
+            for j in range(col_count):
+                out[0, 0, 0, group * col_count + j, j:j + 1, :] = jnp.zeros((1, out.shape[-1]), jnp.bfloat16)
+
+
+def correlate(place, channels, plan, row_ids, tables, own, partner, arrays, picks, first, output, step_count):
+    count = len(picks)
+    tiles, parts, col_count, _ = own.shape
+    row_count = 2 * col_count
+    lag_count = 2 * HALF_LAG
+    kept = [] if output is None else [output]
+
+    def whole(array):
+        return pl.BlockSpec(array.shape, lambda d, *_: (0,) * array.ndim)
+
+    def slot(d, place, channels, plan):
+        return (0, sum(jnp.where(plan[0, t] == first + d, t, 0) for t in range(step_count)), 0, 0, 0, 0)
+
+    pairs = count * row_count * col_count * tiles * LANES
+    return pl.pallas_call(
+        functools.partial(correlate_kernel, first=first, picks=picks),
+        grid_spec=pltpu.PrefetchScalarGridSpec(
+            num_scalar_prefetch=3,
+            grid=(count,),
+            in_specs=[
+                pl.BlockSpec((1, 1, row_count), lambda d, place, *_: (place[0], 0, 0)),
+                whole(tables[0]),
+                whole(tables[1]),
+                whole(own),
+                whole(partner),
+            ] + [pl.BlockSpec(memory_space=pl.ANY)] * (len(arrays) + len(kept)),
+            out_specs=pl.BlockSpec((1, 1, 1, row_count, col_count, lag_count), slot),
+            scratch_shapes=[
+                pltpu.VMEM((row_count, tiles, parts, PACK, LANES), jnp.bfloat16),
+                pltpu.VMEM((col_count, row_count), jnp.float32),
+                pltpu.VMEM((count, tiles, parts, col_count, LANES), jnp.bfloat16),
+                pltpu.SemaphoreType.DMA((count,)),
+            ],
+        ),
+        out_shape=jax.ShapeDtypeStruct((1, step_count, 1, row_count, col_count, lag_count), jnp.bfloat16),
+        input_output_aliases={8 + len(arrays): 0} if kept else {},
+        cost_estimate=pl.CostEstimate(flops=1600 * pairs, bytes_accessed=count * 3000000, transcendentals=0),
+        compiler_params=pltpu.CompilerParams(vmem_limit_bytes=56 << 20),
+    )(place, channels, plan, row_ids, *tables, own, partner, *arrays, *kept)
+
+
+def whiten_tiles(spectra):
+    whitened = whiten(spectra)
+    channels, parts, freq_count = whitened.shape
+    return jnp.transpose(whitened.reshape(channels, parts, freq_count // LANES, LANES), (2, 1, 0, 3))
+
+
+def on_device_fused(spectra, channel_ids, plan):
+    col_count, _, seg_count, freq_count = spectra.shape
+    blk_count = lax.axis_size("blk")
+    row_count = 2 * col_count
+    step_count = blk_count // 2 + 1
+    blk_index = lax.axis_index("blk")
+    group = lax.axis_index("grp")
+    odd = blk_index % 2 == 1
+    place = jnp.stack([blk_index, group, jnp.int32(blk_count)])
+    row_ids = channel_ids.reshape(blk_count, 1, row_count)
+
+    own = whiten_tiles(spectra)
+    partner = passed_along(own, "grp", 1)
+    near, far = passed_along(own, "blk", -2), passed_along(own, "blk", -4)
+    tables = half_lag_tables(freq_count, 1.0 / math.sqrt(2.0 * freq_count * seg_count))
+
+    def stage(arrays, picks, first, output):
+        return correlate(place, channel_ids, plan, row_ids, tables, own, partner, arrays, picks, first, output, step_count)
+
+    output = stage([own], [(0, None)], 0, None)
+    even = own
+    for first in range(1, step_count, 4):
+        near, far, output = lax.optimization_barrier((near, far, output))
+        if first + 4 < step_count:
+            later = passed_along(far, "blk", -2), passed_along(far, "blk", -4)
+        given = jnp.where(odd, jnp.stack([even, near]), jnp.stack([near, far]))
+        taken = lax.ppermute(given, "blk", [(i ^ 1, i) for i in range(blk_count)])
+        output = stage([taken, near, far], [(0, 0), (1, None), (0, 1), (2, None)], first, output)
+        even, (near, far) = far, later
+    return output
 
 
 def on_device(spectra, channel_ids, plan):
@@ -54,7 +272,7 @@
     slot_list = jnp.arange(step_count, dtype=jnp.int32)
     scaling = 1.0 / math.sqrt(2.0 * freq_count * seg_count)
 
-    def correlate(offset, columns, output):
+    def correlate_one(offset, columns, output):
         col_start = (blk_index + offset) % blk_count * row_count + grp_index * col_count
         col_ids = lax.dynamic_slice_in_dim(channel_ids, col_start, col_count, 0)
         col_slots = col_start + jnp.arange(col_count, dtype=jnp.int32)
@@ -79,20 +297,28 @@
 
     def advance(offset, carry):
         columns, output = carry
-        output = correlate(offset, columns, output)
+        output = correlate_one(offset, columns, output)
         columns = passed_along(columns, "blk", -1)
         return (columns, output)
 
     columns, output = lax.fori_loop(0, step_count - 1, advance, (whitened, output))
-    output = correlate(step_count - 1, columns, output)
+    output = correlate_one(step_count - 1, columns, output)
     return output
 
 
 def solution(mesh):
-    return jax.shard_map(
-        on_device,
-        mesh=mesh,
-        in_specs=(P(("blk", "grp"), None, None, None), P(), P("blk", None)),
-        out_specs=P("blk", None, "grp", None, None, None),
-        check_vma=False,
-    )
+    blk_count, grp_count = mesh.shape["blk"], mesh.shape["grp"]
+
+    def program(spectra, channel_ids, plan):
+        col_count = spectra.shape[0] // (blk_count * grp_count)
+        fused = col_count == 2 * PACK and grp_count == 2 and blk_count % 8 == 0
+        fused = fused and spectra.shape[3] % (4 * LANES) == 0
+        return jax.shard_map(
+            on_device_fused if fused else on_device,
+            mesh=mesh,
+            in_specs=(P(("blk", "grp"), None, None, None), P(), P("blk", None)),
+            out_specs=P("blk", None, "grp", None, None, None),
+            check_vma=False,
+        )(spectra, channel_ids, plan)
+
+    return program

time: 420 us -> 70 us (0.17)
  local copies, waits for them, and re-layouts: 216 us -> 3.87 us
  matrix products: 139 us -> 0 us
  Pallas kernels: 0 us -> 44.6 us
  loops' own time: 27.4 us -> 0 us
  blocking collectives: 9.94 us -> 0 us
  other arithmetic: 13.1 us -> 8.75 us
    slice x27 -> x0, local copies, waits for them, and re-layouts: 153 us -> none  [the longest x18 101 us: correlate(): cross_spec[1]]
    dot_general x27 -> x0, matrix products: 139 us -> none  [the longest x9 57.6 us: correlate(): jnp.dot(cross_spec[1], sin_tab, preferred_element_type=jnp.float32)]
    pallas_call x0 -> x3, Pallas kernels: none -> 44.6 us  [correlate(): pl.pallas_call(functools.partial(correlate_kernel, first=first, picks=pic...]
    another operation x1 -> x0, loops' own time: 27.4 us -> none  [on_device(): lax.fori_loop(0, step_count - 1, advance, (whitened, output))]
    convert_element_type x9 -> x0, local copies, waits for them, and re-layouts: 24.8 us -> none  [correlate(): ((real_part + orient * imag_part) * (scaling * keeper)).astype(jnp.bfloat16)]
    dynamic_update_slice x9 -> x0, local copies, waits for them, and re-layouts: 13.2 us -> none  [correlate(): return lax.dynamic_update_slice(output, lagged, (0, out_slot, 0, 0, 0, 0))]
    all_gather x1 -> x0, blocking collectives: 9.94 us -> none  [on_device(): row_block = lax.all_gather(whitened, 'grp', axis=0, tiled=True)]
    while x33 -> x0, local copies, waits for them, and re-layouts: 7.74 us -> none
  transfers between devices with their start and end apart: 8 -> 7, of which waited for: 0 -> 2; matrix products, arithmetic and copies ran while one was open for 75% -> 8% of each run, Pallas kernels for 0% -> 39%
where the time goes in v2:
time: 70 us; the launch traced here: 69.5 us
  Pallas kernels  44.6 us (64%)
  starting transfers between devices  9.56 us (14%)
  other arithmetic  8.75 us (12%)
  local copies, waits for them, and re-layouts  3.87 us (6%)
  waiting for transfers between devices  2.4 us (3%)
    pallas_call x3, Pallas kernels, correlate(): pl.pallas_call(functools.partial(correlate_kernel, first=first, picks=pic...  44.6 us
    ppermute x5, starting transfers between devices, passed_along(): return lax.ppermute(block, axis, route)  9.29 us
    convert_element_type x1, other arithmetic, half_lag_tables(): (-weights * jnp.sin(angles)).astype(jnp.bfloat16)  3.23 us
    select_n x2, other arithmetic, on_device_fused(): given = jnp.where(odd, jnp.stack([even, near]), jnp.stack([near, far]))  2.41 us
    ppermute x2, waiting for transfers between devices, on_device_fused(): taken = lax.ppermute(given, 'blk', [(i ^ 1, i) for i in range(blk_count)])  2.39 us
    unnamed x16, local copies, waits for them, and re-layouts  2.3 us
  transfers between devices with their start and end apart: 7, of which 2 were waited for; matrix products, arithmetic and copies ran while one was open for 8% of the time, Pallas kernels for 39%

profile of v2, /device:TPU:0, one launch (start us, length us, event | category | flops | bytes accessed | tf_op | source)
XLA Modules:
  0.0 69.5 jit_solution(5430249505045108383)
XLA Ops:
  0.0 1.2 %multiply_reduce_fusion = f32[32,4]{1,0:T(8,128)S(1)} fusion(f32[32,2,4,512]{3,2,1,0:T(4,128)} %param.3), kind=kLoop, calls=%fused_computation.6 | loop fusion | flops 262016 | bytes 524800 | tf_op jit(solution)/shard_map/reduce_sum | solution.py:30
  1.2 1.2 %multiply_convert_fusion = bf16[32,2,4,512]{3,2,1,0:T(4,128)(2,1)S(1)} fusion(f32[32,2,4,512]{3,2,1,0:T(4,128)} %param.3, f32[32,4]{1,0:T(8,128)S(1)} %add_rsqrt_fusion), kind=kLoop, calls=%fused_computation.5 | loop fusion | flops 262144 | bytes 786944 | tf_op jit(solution)/shard_map/convert_element_type | solution.py:32
  2.4 0.1 reshape.9
  2.5 0.1 copy.20
  2.7 3.0 %collective-permute-start = (bf16[4,8,32,128]{3,2,1,0:T(8,128)(2,1)S(1)}, bf16[4,8,32,128]{3,2,1,0:T(8,128)(2,1)S(1)}, u32[]{:S(2)}, u32[]{:S(2)}) collective-permute-start(bf16[4,8,32,128]{3,2,1,0:T(8,128)(2,1)S(1)} %bitcast.12), channel_id=1, source_target_pairs={{1,0},{0,1},{3,2},{2,3},{5,4},{4,5},{7,6},{6,7},{9,8},{8,9},{11,10... | collective-permute-start | bytes 786440 | tf_op jit(solution)/shard_map/ppermute | solution.py:26
  5.7 4.5 %collective-permute-start.1 = (bf16[4,8,32,128]{3,2,1,0:T(8,128)(2,1)S(1)}, bf16[4,8,32,128]{3,2,1,0:T(8,128)(2,1)S(1)}, u32[]{:S(2)}, u32[]{:S(2)}) collective-permute-start(bf16[4,8,32,128]{3,2,1,0:T(8,128)(2,1)S(1)} %bitcast.13), channel_id=1, source_target_pairs={{4,0},{6,2},{8,4},{10,6},{12,8},{14,10},{16,12},{18,14},{20,16},{2... | collective-permute-start | bytes 786440 | tf_op jit(solution)/shard_map/ppermute | solution.py:26
  10.2 0.4 collective-permute-start.2
  10.7 1.4 %reshape.8.row_ids = s32[16,1,64]{2,1,0:T(1,128)} reshape(s32[1024]{0:T(1024)} %channels.5) | data formatting | bytes 8192 | tf_op jit(solution)/shard_map/reshape | solution.py:231
  12.1 3.2 %multiply_convert_fusion.1 = (bf16[2,512,128]{2,1,0:T(8,128)(2,1)}, bf16[2,512,128]{2,1,0:T(8,128)(2,1)}) fusion(f32[512]{0:T(512)S(1)} %get-tuple-element.22, s32[128]{0:T(128)S(1)} %fusion.7, s32[128]{0:T(128)S(1)} %get-tuple-element.23, s32[128]{0:T(128)S(1)} %get-tuple-element.24, pred[128]{0:T(512)(128)(4,1)S(1)} %iota_compare_fusion.1, ...), kind=kLoop, calls=%fused_computation.7 | loop fusion | flops 2097152 | bytes 530050 | tf_op jit(solution)/shard_map/convert_element_type | solution.py:62
  15.3 0.7 pad_add_fusion.place
  16.0 0.7 %copy-done.1 = bf16[4,8,32,128]{3,2,1,0:T(8,128)(2,1)} copy-done((bf16[4,8,32,128]{3,2,1,0:T(8,128)(2,1)}, bf16[4,8,32,128]{3,2,1,0:T(8,128)(2,1)S(1)}, u32[]{:S(2)}) %copy-start.1) | copy-done | bytes 262168
  16.7 8.9 %shard_map.37.rest_3_ = bf16[1,9,1,64,32,400]{5,4,3,2,1,0:T(8,128)(2,1)} custom-call(s32[3]{0:T(128)} %pad_add_fusion.place, s32[1024]{0:T(1024)} %channels.5, s32[1,9]{1,0:T(1,128)} %plan.5, s32[16,1,64]{2,1,0:T(1,128)} %reshape.8.row_ids, bf16[2,512,128]{2,1,0:T(8,128)(2,1)} %get-tuple-element.20.cos_tab, bf16[2,512,128]{2,1,0:T(8,128)(2,1)} %get-tuple-element.19.sin_tab, ...), custom_call_target="tpu_custom_call" | custom-call | flops 1677721600 | bytes 3000000 | tf_op jit(solution)/shard_map/pallas_call | solution.py:189
  25.7 1.2 %maximum_select_fusion = bf16[2,4,8,32,128]{4,3,2,1,0:T(8,128)(2,1)S(1)} fusion(bf16[1,4,8,32,128]{4,3,2,1,0:T(8,128)(2,1)S(1)} %bitcast.22, bf16[1,4,8,32,128]{4,3,2,1,0:T(8,128)(2,1)} %bitcast.17, bf16[1,4,8,32,128]{4,3,2,1,0:T(8,128)(2,1)S(1)} %bitcast.20, pred[]{:T(512)S(6)} %eq.37), kind=kLoop, calls=%fused_computation.3 | loop fusion | flops 786432 | bytes 1310721 | tf_op jit(solution)/shard_map/jit(_where)/select_n | solution.py:247
  26.9 0.1 collective-permute-start.5
  26.9 0.8 %collective-permute-start.3 = (bf16[4,8,32,128]{3,2,1,0:T(8,128)(2,1)S(1)}, bf16[4,8,32,128]{3,2,1,0:T(8,128)(2,1)S(1)}, u32[]{:S(2)}, u32[]{:S(2)}) collective-permute-start(bf16[4,8,32,128]{3,2,1,0:T(8,128)(2,1)S(1)} %collective-permute-done.2.rest_2_), channel_id=1, source_target_pairs={{4,0},{6,2},{8,4},{10,6},{12,8},{14,10},{16,12},{18,14},{20,16},{2... | collective-permute-start | bytes 786440 | tf_op jit(solution)/shard_map/ppermute | solution.py:26
  27.8 0.5 collective-permute-start.4
  28.2 0.6 collective-permute-done.5.rest_0_
  28.8 0.8 %copy-done.6 = bf16[2,4,8,32,128]{4,3,2,1,0:T(8,128)(2,1)} copy-done((bf16[2,4,8,32,128]{4,3,2,1,0:T(8,128)(2,1)}, bf16[2,4,8,32,128]{4,3,2,1,0:T(8,128)(2,1)S(1)}, u32[]{:S(2)}) %copy-start.6) | copy-done | bytes 524312
  29.6 17.9 %shard_map.38.rest_3_ = bf16[1,9,1,64,32,400]{5,4,3,2,1,0:T(8,128)(2,1)} custom-call(s32[3]{0:T(128)} %pad_add_fusion.place, s32[1024]{0:T(1024)} %channels.5, s32[1,9]{1,0:T(1,128)} %plan.5, s32[16,1,64]{2,1,0:T(1,128)} %reshape.8.row_ids, bf16[2,512,128]{2,1,0:T(8,128)(2,1)} %get-tuple-element.20.cos_tab, ...), custom_call_target="tpu_custom_call", output_to_operand_aliasing={{}: (11, {})} | custom-call | flops 6710886400 | bytes 12000000 | tf_op jit(solution)/shard_map/pallas_call | solution.py:189
  47.5 1.2 %maximum_select_fusion.1 = bf16[2,4,8,32,128]{4,3,2,1,0:T(8,128)(2,1)S(1)} fusion(bf16[1,4,8,32,128]{4,3,2,1,0:T(8,128)(2,1)S(1)} %bitcast.23, bf16[1,4,8,32,128]{4,3,2,1,0:T(8,128)(2,1)} %bitcast.21, bf16[1,4,8,32,128]{4,3,2,1,0:T(8,128)(2,1)S(1)} %bitcast.24, pred[]{:T(512)S(6)} %eq.37), kind=kLoop, calls=%fused_computation.4 | loop fusion | flops 786432 | bytes 1310721 | tf_op jit(solution)/shard_map/jit(_where)/select_n | solution.py:247
  48.8 0.2 collective-permute-start.6
  49.0 1.8 %collective-permute-done.6.rest_0_ = bf16[2,4,8,32,128]{4,3,2,1,0:T(8,128)(2,1)S(1)} collective-permute-done((bf16[2,4,8,32,128]{4,3,2,1,0:T(8,128)(2,1)S(1)}, bf16[2,4,8,32,128]{4,3,2,1,0:T(8,128)(2,1)S(1)}, u32[]{:S(2)}, u32[]{:S(2)}) %collective-permute-start.6) | collective-permute-done | bytes 524320 | tf_op jit(solution)/shard_map/ppermute | solution.py:248
  50.7 0.8 %copy-done.7 = bf16[2,4,8,32,128]{4,3,2,1,0:T(8,128)(2,1)} copy-done((bf16[2,4,8,32,128]{4,3,2,1,0:T(8,128)(2,1)}, bf16[2,4,8,32,128]{4,3,2,1,0:T(8,128)(2,1)S(1)}, u32[]{:S(2)}) %copy-start.7) | copy-done | bytes 524312
  51.5 17.9 %shard_map.39 = bf16[1,9,1,64,32,400]{5,4,3,2,1,0:T(8,128)(2,1)} custom-call(s32[3]{0:T(128)} %pad_add_fusion.place, s32[1024]{0:T(1024)} %channels.5, s32[1,9]{1,0:T(1,128)} %plan.5, s32[16,1,64]{2,1,0:T(1,128)} %reshape.8.row_ids, bf16[2,512,128]{2,1,0:T(8,128)(2,1)} %get-tuple-element.20.cos_tab, ...), custom_call_target="tpu_custom_call", output_to_operand_aliasing={{}: (11, {})} | custom-call | flops 6710886400 | bytes 12000000 | tf_op jit(solution)/shard_map/pallas_call | solution.py:189
  (24 shorter events, 0.1 us)
Async XLA Ops:
  2.7 13.3 %copy-start = (bf16[32,8,4,128]{3,0,1,2:T(8,128)(2,1)}, bf16[32,8,4,128]{3,0,1,2:T(8,128)(2,1)S(1)}, u32[]{:S(2)}) copy-start(bf16[32,8,4,128]{3,0,1,2:T(8,128)(2,1)S(1)} %copy.20) | copy-start | bytes 786436
  2.7 13.3 %collective-permute-start = (bf16[4,8,32,128]{3,2,1,0:T(8,128)(2,1)S(1)}, bf16[4,8,32,128]{3,2,1,0:T(8,128)(2,1)S(1)}, u32[]{:S(2)}, u32[]{:S(2)}) collective-permute-start(bf16[4,8,32,128]{3,2,1,0:T(8,128)(2,1)S(1)} %bitcast.12), channel_id=1, source_target_pairs={{1,0},{0,1},{3,2},{2,3},{5,4},{4,5},{7,6},{6,7},{9,8},{8,9},{11,10... | collective-permute-start | bytes 786440 | tf_op jit(solution)/shard_map/ppermute | solution.py:26
  5.7 19.9 %collective-permute-start.1 = (bf16[4,8,32,128]{3,2,1,0:T(8,128)(2,1)S(1)}, bf16[4,8,32,128]{3,2,1,0:T(8,128)(2,1)S(1)}, u32[]{:S(2)}, u32[]{:S(2)}) collective-permute-start(bf16[4,8,32,128]{3,2,1,0:T(8,128)(2,1)S(1)} %bitcast.13), channel_id=1, source_target_pairs={{4,0},{6,2},{8,4},{10,6},{12,8},{14,10},{16,12},{18,14},{20,16},{2... | collective-permute-start | bytes 786440 | tf_op jit(solution)/shard_map/ppermute | solution.py:26
  10.2 15.4 %collective-permute-start.2 = (bf16[4,8,32,128]{3,2,1,0:T(8,128)(2,1)S(1)}, bf16[4,8,32,128]{3,2,1,0:T(8,128)(2,1)S(1)}, u32[]{:S(2)}, u32[]{:S(2)}) collective-permute-start(bf16[4,8,32,128]{3,2,1,0:T(8,128)(2,1)S(1)} %bitcast.14), channel_id=1, source_target_pairs={{8,0},{10,2},{12,4},{14,6},{16,8},{18,10},{20,12},{22,14},{24,16},... | collective-permute-start | bytes 786440 | tf_op jit(solution)/shard_map/ppermute | solution.py:26
  16.0 0.7 %copy-start.1 = (bf16[4,8,32,128]{3,2,1,0:T(8,128)(2,1)}, bf16[4,8,32,128]{3,2,1,0:T(8,128)(2,1)S(1)}, u32[]{:S(2)}) copy-start(bf16[4,8,32,128]{3,2,1,0:T(8,128)(2,1)S(1)} %collective-permute-done.partner) | copy-start | bytes 786436
  25.6 3.2 %copy-start.3 = (bf16[4,8,32,128]{3,2,1,0:T(8,128)(2,1)}, bf16[4,8,32,128]{3,2,1,0:T(8,128)(2,1)S(1)}, u32[]{:S(2)}) copy-start(bf16[4,8,32,128]{3,2,1,0:T(8,128)(2,1)S(1)} %collective-permute-done.1.rest_1_) | copy-start | bytes 786436
  25.6 3.2 %copy-start.2 = (bf16[4,8,32,128]{3,2,1,0:T(8,128)(2,1)}, bf16[4,8,32,128]{3,2,1,0:T(8,128)(2,1)S(1)}, u32[]{:S(2)}) copy-start(bf16[4,8,32,128]{3,2,1,0:T(8,128)(2,1)S(1)} %collective-permute-done.2.rest_2_) | copy-start | bytes 786436
  26.9 2.0 %collective-permute-start.5 = (bf16[2,4,8,32,128]{4,3,2,1,0:T(8,128)(2,1)S(1)}, bf16[2,4,8,32,128]{4,3,2,1,0:T(8,128)(2,1)S(1)}, u32[]{:S(2)}, u32[]{:S(2)}) collective-permute-start(bf16[2,4,8,32,128]{4,3,2,1,0:T(8,128)(2,1)S(1)} %maximum_select_fusion), channel_id=1, source_target_pairs={{2,0},{0,2},{6,4},{4,6},{10,8},{8,10},{14,12},{12,14},{18,16},{16,... | collective-permute-start | bytes 1572872 | tf_op jit(solution)/shard_map/ppermute | solution.py:248
  26.9 20.6 %collective-permute-start.3 = (bf16[4,8,32,128]{3,2,1,0:T(8,128)(2,1)S(1)}, bf16[4,8,32,128]{3,2,1,0:T(8,128)(2,1)S(1)}, u32[]{:S(2)}, u32[]{:S(2)}) collective-permute-start(bf16[4,8,32,128]{3,2,1,0:T(8,128)(2,1)S(1)} %collective-permute-done.2.rest_2_), channel_id=1, source_target_pairs={{4,0},{6,2},{8,4},{10,6},{12,8},{14,10},{16,12},{18,14},{20,16},{2... | collective-permute-start | bytes 786440 | tf_op jit(solution)/shard_map/ppermute | solution.py:26
  27.8 19.8 %collective-permute-start.4 = (bf16[4,8,32,128]{3,2,1,0:T(8,128)(2,1)S(1)}, bf16[4,8,32,128]{3,2,1,0:T(8,128)(2,1)S(1)}, u32[]{:S(2)}, u32[]{:S(2)}) collective-permute-start(bf16[4,8,32,128]{3,2,1,0:T(8,128)(2,1)S(1)} %collective-permute-done.2.rest_2_), channel_id=1, source_target_pairs={{8,0},{10,2},{12,4},{14,6},{16,8},{18,10},{20,12},{22,14},{24,16},... | collective-permute-start | bytes 786440 | tf_op jit(solution)/shard_map/ppermute | solution.py:26
  28.8 0.8 %copy-start.6 = (bf16[2,4,8,32,128]{4,3,2,1,0:T(8,128)(2,1)}, bf16[2,4,8,32,128]{4,3,2,1,0:T(8,128)(2,1)S(1)}, u32[]{:S(2)}) copy-start(bf16[2,4,8,32,128]{4,3,2,1,0:T(8,128)(2,1)S(1)} %collective-permute-done.5.rest_0_) | copy-start | bytes 1572868
  47.5 3.2 %copy-start.4 = (bf16[4,8,32,128]{3,2,1,0:T(8,128)(2,1)}, bf16[4,8,32,128]{3,2,1,0:T(8,128)(2,1)S(1)}, u32[]{:S(2)}) copy-start(bf16[4,8,32,128]{3,2,1,0:T(8,128)(2,1)S(1)} %collective-permute-done.3.rest_1_) | copy-start | bytes 786436
  47.5 3.2 %copy-start.5 = (bf16[4,8,32,128]{3,2,1,0:T(8,128)(2,1)}, bf16[4,8,32,128]{3,2,1,0:T(8,128)(2,1)S(1)}, u32[]{:S(2)}) copy-start(bf16[4,8,32,128]{3,2,1,0:T(8,128)(2,1)S(1)} %collective-permute-done.4.rest_2_) | copy-start | bytes 786436
  48.8 2.0 %collective-permute-start.6 = (bf16[2,4,8,32,128]{4,3,2,1,0:T(8,128)(2,1)S(1)}, bf16[2,4,8,32,128]{4,3,2,1,0:T(8,128)(2,1)S(1)}, u32[]{:S(2)}, u32[]{:S(2)}) collective-permute-start(bf16[2,4,8,32,128]{4,3,2,1,0:T(8,128)(2,1)S(1)} %maximum_select_fusion.1), channel_id=1, source_target_pairs={{2,0},{0,2},{6,4},{4,6},{10,8},{8,10},{14,12},{12,14},{18,16},{16,... | collective-permute-start | bytes 1572872 | tf_op jit(solution)/shard_map/ppermute | solution.py:248
  50.7 0.8 %copy-start.7 = (bf16[2,4,8,32,128]{4,3,2,1,0:T(8,128)(2,1)}, bf16[2,4,8,32,128]{4,3,2,1,0:T(8,128)(2,1)S(1)}, u32[]{:S(2)}) copy-start(bf16[2,4,8,32,128]{4,3,2,1,0:T(8,128)(2,1)S(1)} %collective-permute-done.6.rest_0_) | copy-start | bytes 1572868

commit v3 on v2

--- a/solution.py
+++ b/solution.py
@@ -15,9 +15,8 @@
 TURN = 16
 REST = 72
 MIDDLE = 56
-TOGETHER = 4
+TOGETHER = 8
 DELAY = 2
-HELD_ROWS = 1024
 
 
 def passed_along(block, axis, distance):
@@ -52,52 +51,56 @@
 
 
 def half_lag_tables(freq_count, scale):
-    tile = lax.broadcasted_iota(jnp.int32, (2, freq_count, LANES), 0)
-    freq = lax.broadcasted_iota(jnp.int32, (2, freq_count, LANES), 1)
-    lane = lax.broadcasted_iota(jnp.int32, (2, freq_count, LANES), 2)
+    tile = lax.broadcasted_iota(jnp.int32, (2, 1, 1, LANES), 0)
+    lane = lax.broadcasted_iota(jnp.int32, (2, 1, 1, LANES), 3)
     wrapped = jnp.where(lane <= TURN, MIDDLE + LANES + lane, MIDDLE + lane)
     lag = jnp.where(tile == 0, wrapped, jnp.where(lane <= TURN, MIDDLE + lane, jnp.maximum(lane - REST, 0)))
-    angles = 2.0 * math.pi / NFFT * (freq * lag % NFFT).astype(jnp.float32)
-    weights = jnp.where(freq == 0, scale, 2.0 * scale)
-    return (weights * jnp.cos(angles)).astype(jnp.bfloat16), (-weights * jnp.sin(angles)).astype(jnp.bfloat16)
-
-
-def correlate_kernel(place, channels, plan, row_ids, cos_tab, sin_tab, own, partner, *rest, first, picks):
+    coarse = PACK * jnp.arange(freq_count // PACK, dtype=jnp.int32)[None, :, None, None]
+    fine = jnp.arange(PACK, dtype=jnp.int32)[None, None, :, None]
+
+    def turned(freq):
+        angles = 2.0 * math.pi / NFFT * (freq * lag % NFFT).astype(jnp.float32)
+        return jnp.cos(angles), jnp.sin(angles)
+
+    (cos_a, sin_a), (cos_b, sin_b) = lax.optimization_barrier((turned(coarse), turned(fine)))
+    weights = jnp.where(coarse + fine == 0, scale, 2.0 * scale)
+    cos_tab = (weights * (cos_a * cos_b - sin_a * sin_b)).astype(jnp.bfloat16)
+    sin_tab = (-weights * (sin_a * cos_b + cos_a * sin_b)).astype(jnp.bfloat16)
+    return cos_tab.reshape(2, freq_count, LANES), sin_tab.reshape(2, freq_count, LANES)
+
+
+def correlate_kernel(channels, plan, ids, cos_tab, sin_tab, own, partner, *rest, first, picks):
     out, rows, turn, cols, sems = rest[-5:]
     count = cols.shape[0]
     tiles, parts, col_count, _ = own.shape
     seg_count = parts // 2
-    row_count = rows.shape[0]
+    row_count = 2 * col_count
     depth = 2 * LANES
-    blk, group, blk_count = place[0], place[1], place[2]
-    step = pl.program_id(0)
-
-    def fetch(k):
-        source, index = picks[k]
-        array = rest[source] if index is None else rest[source].at[index]
-        return pltpu.make_async_copy(array, cols.at[k], sems.at[k])
-
-    @pl.when(step == 0)
+    blk, group, blk_count = lax.axis_index("blk"), lax.axis_index("grp"), lax.axis_size("blk")
+    step, half = pl.program_id(0), pl.program_id(1)
+
+    def fetch(k, parity):
+        return pltpu.make_async_copy(rest[picks[k][parity]], cols.at[k], sems.at[k])
+
+    @pl.when((step == 0) & (half == 0))
     def _():
-        for k in range(count):
-            fetch(k).start()
-        for source, start in ((own, group * col_count), (partner, (1 - group) * col_count)):
-            def spread(n, carry, source=source, start=start):
-                q, s = n // parts, n % parts
-                for b in range(0, col_count, PACK):
-                    lines = source[q, s, b:b + PACK, :]
-                    for k in range(PACK):
-                        rows[start + b + k, q, s] = jnp.broadcast_to(lines[k:k + 1, :], (PACK, LANES))
-                return carry
-
-            lax.fori_loop(0, tiles * parts, spread, 0)
+        for parity in range(2):
+            @pl.when(blk % 2 == parity)
+            def _(parity=parity):
+                for k in range(count):
+                    fetch(k, parity).start()
+        for source, place in ((own, group), (partner, 1 - group)):
+            for q in range(tiles):
+                rows[place, q] = source[q]
 
     for k in range(count):
-        @pl.when(step == k)
+        @pl.when((step == k) & (half == 0))
         def _(k=k):
-            fetch(k).wait()
-
-    id_line = row_ids[0]
+            fetch(k, 0).wait()
+
+    row_start = blk * row_count + half * col_count
+    line = jnp.broadcast_to(ids[pl.ds(row_start // LANES, 1), :], (8, LANES))
+    id_line = pltpu.roll(line, (LANES - row_start % LANES) % LANES, 1)[0:1, :]
     col_start = (blk + first + step) % blk_count * row_count + group * col_count
     for j in range(col_count):
         turn[j:j + 1, :] = jnp.where(id_line < channels[col_start + j], 1.0, -1.0)
@@ -108,7 +111,9 @@
     mirror = (TURN - lane) & (LANES - 1)
 
     def form(c, i, tile):
-        r = [jnp.concatenate([rows[i, tile, s]] * (col_count // PACK), axis=0) for s in range(parts)]
+        b = i // PACK * PACK
+        lines = [rows[half, tile, s, b:b + PACK, :] for s in range(parts)]
+        r = [jnp.broadcast_to(v[i - b:i - b + 1, :], (col_count, LANES)) for v in lines]
         re = tree_sum([r[s] * c[s] for s in range(parts)])
         im = tree_sum([r[seg_count + s] * c[s] - r[s] * c[seg_count + s] for s in range(seg_count)])
         return re, im
@@ -134,83 +139,73 @@
         line[:, 3 * LANES:] = ahead_u[:, :out.shape[-1] - 3 * LANES]
 
     def multiply(*sums):
-        held = len(sums) // 2
-        sums_even, sums_odd = sums[:held], sums[held:]
-        halves = tiles // 2
+        sums_even, sums_odd = sums[:col_count], sums[col_count:]
         push(0)
-        for block in range(0, row_count, held):
-            for h in range(halves):
-                if h + 1 < halves or block + held < row_count:
-                    push((h + 1) % halves)
-                for g0 in range(0, held, TOGETHER):
-                    formed = []
-                    for tile in (2 * h, 2 * h + 1):
-                        c = [cols[step, tile, s] for s in range(parts)]
-                        formed.append([form(c, block + g0 + k, tile) for k in range(TOGETHER)])
-                    for k in range(TOGETHER):
-                        g = g0 + k
-                        fresh = h % 2 if g == 0 else None
-                        for part, held_sums in enumerate((sums_even, sums_odd)):
-                            side = jnp.concatenate([formed[0][k][part], formed[1][k][part]], axis=1)
-                            pltpu.matmul_acc_lhs(held_sums[g], side, load_staged_rhs=fresh)
-                        if h == halves - 1 and g >= DELAY:
-                            finish(block + g - DELAY, pltpu.matmul_pop(sums_even[g - DELAY]), pltpu.matmul_pop(sums_odd[g - DELAY]))
-            for g in range(held - DELAY, held):
-                finish(block + g, pltpu.matmul_pop(sums_even[g]), pltpu.matmul_pop(sums_odd[g]))
-
-    held = min(row_count, HELD_ROWS // col_count)
+        for h in range(tiles // 2):
+            if h + 1 < tiles // 2:
+                push(h + 1)
+            for g0 in range(0, col_count, TOGETHER):
+                formed = []
+                for tile in (2 * h, 2 * h + 1):
+                    c = [cols[step, tile, s] for s in range(parts)]
+                    formed.append([form(c, g0 + k, tile) for k in range(TOGETHER)])
+                for k in range(TOGETHER):
+                    g = g0 + k
+                    fresh = h % 2 if g == 0 else None
+                    for part, held in enumerate((sums_even, sums_odd)):
+                        side = jnp.concatenate([formed[0][k][part], formed[1][k][part]], axis=1)
+                        pltpu.matmul_acc_lhs(held[g], side, load_staged_rhs=fresh)
+                    if h + 1 == tiles // 2 and g >= DELAY:
+                        finish(g - DELAY, pltpu.matmul_pop(sums_even[g - DELAY]), pltpu.matmul_pop(sums_odd[g - DELAY]))
+        for g in range(col_count - DELAY, col_count):
+            finish(g, pltpu.matmul_pop(sums_even[g]), pltpu.matmul_pop(sums_odd[g]))
+
     pl.run_scoped(
         multiply,
-        *[pltpu.ACC(0)((col_count, depth), jnp.float32)] * held,
-        *[pltpu.ACC(1)((col_count, depth), jnp.float32)] * held,
+        *[pltpu.ACC(0)((col_count, depth), jnp.float32)] * col_count,
+        *[pltpu.ACC(1)((col_count, depth), jnp.float32)] * col_count,
     )
 
     if first == 0:
-        @pl.when(step == 0)
+        @pl.when((step == 0) & (half == group))
         def _():
             for j in range(col_count):
-                out[0, 0, 0, group * col_count + j, j:j + 1, :] = jnp.zeros((1, out.shape[-1]), jnp.bfloat16)
-
-
-def correlate(place, channels, plan, row_ids, tables, own, partner, arrays, picks, first, output, step_count):
+                out[0, 0, 0, j, j:j + 1, :] = jnp.zeros((1, out.shape[-1]), jnp.bfloat16)
+
+
+def correlate(channels, plan, ids, tables, own, partner, arrays, picks, first, output, step_count):
     count = len(picks)
     tiles, parts, col_count, _ = own.shape
-    row_count = 2 * col_count
     lag_count = 2 * HALF_LAG
     kept = [] if output is None else [output]
 
     def whole(array):
-        return pl.BlockSpec(array.shape, lambda d, *_: (0,) * array.ndim)
-
-    def slot(d, place, channels, plan):
-        return (0, sum(jnp.where(plan[0, t] == first + d, t, 0) for t in range(step_count)), 0, 0, 0, 0)
-
-    pairs = count * row_count * col_count * tiles * LANES
+        return pl.BlockSpec(array.shape, lambda *_: (0,) * array.ndim)
+
+    def slot(d, half, channels, plan):
+        return (0, sum(jnp.where(plan[0, t] == first + d, t, 0) for t in range(step_count)), 0, half, 0, 0)
+
+    pairs = count * 2 * col_count * col_count * tiles * LANES
     return pl.pallas_call(
         functools.partial(correlate_kernel, first=first, picks=picks),
         grid_spec=pltpu.PrefetchScalarGridSpec(
-            num_scalar_prefetch=3,
-            grid=(count,),
-            in_specs=[
-                pl.BlockSpec((1, 1, row_count), lambda d, place, *_: (place[0], 0, 0)),
-                whole(tables[0]),
-                whole(tables[1]),
-                whole(own),
-                whole(partner),
-            ] + [pl.BlockSpec(memory_space=pl.ANY)] * (len(arrays) + len(kept)),
-            out_specs=pl.BlockSpec((1, 1, 1, row_count, col_count, lag_count), slot),
+            num_scalar_prefetch=2,
+            grid=(count, 2),
+            in_specs=[whole(ids), whole(tables[0]), whole(tables[1]), whole(own), whole(partner)]
+            + [pl.BlockSpec(memory_space=pl.ANY)] * (len(arrays) + len(kept)),
+            out_specs=pl.BlockSpec((1, 1, 1, col_count, col_count, lag_count), slot),
             scratch_shapes=[
-                pltpu.VMEM((row_count, tiles, parts, PACK, LANES), jnp.bfloat16),
-                pltpu.VMEM((col_count, row_count), jnp.float32),
+                pltpu.VMEM((2, tiles, parts, col_count, LANES), jnp.bfloat16),
+                pltpu.VMEM((col_count, LANES), jnp.float32),
                 pltpu.VMEM((count, tiles, parts, col_count, LANES), jnp.bfloat16),
                 pltpu.SemaphoreType.DMA((count,)),
             ],
         ),
-        out_shape=jax.ShapeDtypeStruct((1, step_count, 1, row_count, col_count, lag_count), jnp.bfloat16),
-        input_output_aliases={8 + len(arrays): 0} if kept else {},
+        out_shape=jax.ShapeDtypeStruct((1, step_count, 1, 2 * col_count, col_count, lag_count), jnp.bfloat16),
+        input_output_aliases={7 + len(arrays): 0} if kept else {},
         cost_estimate=pl.CostEstimate(flops=1600 * pairs, bytes_accessed=count * 3000000, transcendentals=0),
-        compiler_params=pltpu.CompilerParams(vmem_limit_bytes=56 << 20),
-    )(place, channels, plan, row_ids, *tables, own, partner, *arrays, *kept)
+        compiler_params=pltpu.CompilerParams(vmem_limit_bytes=40 << 20),
+    )(channels, plan, ids, *tables, own, partner, *arrays, *kept)
 
 
 def whiten_tiles(spectra):
@@ -222,32 +217,32 @@
 def on_device_fused(spectra, channel_ids, plan):
     col_count, _, seg_count, freq_count = spectra.shape
     blk_count = lax.axis_size("blk")
-    row_count = 2 * col_count
     step_count = blk_count // 2 + 1
-    blk_index = lax.axis_index("blk")
-    group = lax.axis_index("grp")
-    odd = blk_index % 2 == 1
-    place = jnp.stack([blk_index, group, jnp.int32(blk_count)])
-    row_ids = channel_ids.reshape(blk_count, 1, row_count)
+    ids = channel_ids.reshape(-1, LANES)
+
+    def other_core(block):
+        return lax.ppermute(block, "blk", [(i ^ 1, i) for i in range(blk_count)])
 
     own = whiten_tiles(spectra)
     partner = passed_along(own, "grp", 1)
-    near, far = passed_along(own, "blk", -2), passed_along(own, "blk", -4)
     tables = half_lag_tables(freq_count, 1.0 / math.sqrt(2.0 * freq_count * seg_count))
+    sent, tables = lax.optimization_barrier((own, tables))
+    near, far = passed_along(sent, "blk", -2), passed_along(sent, "blk", -4)
 
     def stage(arrays, picks, first, output):
-        return correlate(place, channel_ids, plan, row_ids, tables, own, partner, arrays, picks, first, output, step_count)
-
-    output = stage([own], [(0, None)], 0, None)
-    even = own
+        return correlate(channel_ids, plan, ids, tables, own, partner, arrays, picks, first, output, step_count)
+
+    output = stage([own], [(0, 0)], 0, None)
+    last = own
     for first in range(1, step_count, 4):
-        near, far, output = lax.optimization_barrier((near, far, output))
+        near, far, last, output = lax.optimization_barrier((near, far, last, output))
         if first + 4 < step_count:
             later = passed_along(far, "blk", -2), passed_along(far, "blk", -4)
-        given = jnp.where(odd, jnp.stack([even, near]), jnp.stack([near, far]))
-        taken = lax.ppermute(given, "blk", [(i ^ 1, i) for i in range(blk_count)])
-        output = stage([taken, near, far], [(0, 0), (1, None), (0, 1), (2, None)], first, output)
-        even, (near, far) = far, later
+        taken = other_core(last) if first == 1 else crossed
+        crossed = other_core(far)
+        arrays = [near, far, taken, other_core(near), crossed]
+        output = stage(arrays, [(2, 3), (0, 0), (3, 4), (1, 1)], first, output)
+        last, (near, far) = far, later
     return output
 
 

time: 70 us -> 60.1 us (0.86)
  Pallas kernels: 44.6 us -> 36.3 us
  other arithmetic: 8.75 us -> 3.29 us
  starting transfers between devices: 9.56 us -> 14.3 us
  local copies, waits for them, and re-layouts: 3.87 us -> 1.63 us
  waiting for transfers between devices: 2.4 us -> 4.16 us
    pallas_call x3, Pallas kernels: 44.6 us -> 36.3 us  [correlate(): pl.pallas_call(functools.partial(correlate_kernel, first=first, picks=pic...]
    ppermute x5, starting transfers between devices: 9.29 us -> 13.2 us  [passed_along(): return lax.ppermute(block, axis, route)]
    convert_element_type x1 -> x2, other arithmetic: 3.23 us -> 0.27 us  [the longest x1 0.13 us: half_lag_tables(): sin_tab = (-weights * (sin_a * cos_b + cos_a * sin_b)).astype(jnp.bfloat16)]
    ppermute x5, waiting for transfers between devices: 0.01 us -> 2.76 us  [passed_along(): return lax.ppermute(block, axis, route)]
    select_n x3 -> x2, other arithmetic: 2.41 us -> 0.14 us  [the longest x1 0.07 us: half_lag_tables(): weights = jnp.where(coarse + fine == 0, scale, 2.0 * scale)]
    reshape x1 -> x0, local copies, waits for them, and re-layouts: 1.36 us -> none  [on_device_fused(): row_ids = channel_ids.reshape(blk_count, 1, row_count)]
    ppermute x2 -> x5, waiting for transfers between devices: 2.39 us -> 1.41 us  [other_core(): return lax.ppermute(block, 'blk', [(i ^ 1, i) for i in range(blk_count)])]
    unnamed x16 -> x4, local copies, waits for them, and re-layouts: 2.3 us -> 1.34 us
  transfers between devices with their start and end apart: 7 -> 10, of which waited for: 2 -> 4; matrix products, arithmetic and copies ran while one was open for 8% -> 2% of each run, Pallas kernels for 39% -> 35%
where the time goes in v3:
time: 60.1 us; the launch traced here: 59.8 us
  Pallas kernels  36.3 us (60%)
  starting transfers between devices  14.3 us (24%)
  waiting for transfers between devices  4.16 us (7%)
  other arithmetic  3.29 us (5%)
  local copies, waits for them, and re-layouts  1.63 us (3%)
    pallas_call x3, Pallas kernels, correlate(): pl.pallas_call(functools.partial(correlate_kernel, first=first, picks=pic...  36.3 us
    ppermute x5, starting transfers between devices, passed_along(): return lax.ppermute(block, axis, route)  13.2 us
    ppermute x5, waiting for transfers between devices, passed_along(): return lax.ppermute(block, axis, route)  2.76 us
    ppermute x5, waiting for transfers between devices, other_core(): return lax.ppermute(block, 'blk', [(i ^ 1, i) for i in range(blk_count)])  1.41 us
    unnamed x4, local copies, waits for them, and re-layouts  1.34 us
    reduce_sum x1, other arithmetic, whiten(): seg_power = jnp.mean(spectra * spectra, axis=(1, 3))  1.22 us
  transfers between devices with their start and end apart: 10, of which 4 were waited for; matrix products, arithmetic and copies ran while one was open for 2% of the time, Pallas kernels for 35%

profile of v3, /device:TPU:0, one launch (start us, length us, event | category | flops | bytes accessed | tf_op | source)
XLA Modules:
  0.0 59.8 jit_solution(16440230968107614227)
XLA Ops:
  0.0 1.2 %multiply_reduce_fusion = f32[32,4]{1,0:T(8,128)S(1)} fusion(f32[32,2,4,512]{3,2,1,0:T(4,128)} %param.3), kind=kLoop, calls=%fused_computation.7 | loop fusion | flops 262016 | bytes 524800 | tf_op jit(solution)/shard_map/reduce_sum | solution.py:29
  1.2 1.2 %multiply_convert_fusion = bf16[32,2,4,512]{3,2,1,0:T(4,128)(2,1)S(1)} fusion(f32[32,2,4,512]{3,2,1,0:T(4,128)} %param.3, f32[32,4]{1,0:T(8,128)S(1)} %add_rsqrt_fusion), kind=kLoop, calls=%fused_computation.6 | loop fusion | flops 262144 | bytes 786944 | tf_op jit(solution)/shard_map/convert_element_type | solution.py:31
  2.5 0.1 copy.19
  2.7 3.0 %collective-permute-start = (bf16[4,8,32,128]{3,2,1,0:T(8,128)(2,1)S(1)}, bf16[4,8,32,128]{3,2,1,0:T(8,128)(2,1)S(1)}, u32[]{:S(2)}, u32[]{:S(2)}) collective-permute-start(bf16[4,8,32,128]{3,2,1,0:T(8,128)(2,1)S(1)} %bitcast.16), channel_id=1, source_target_pairs={{1,0},{0,1},{3,2},{2,3},{5,4},{4,5},{7,6},{6,7},{9,8},{8,9},{11,10... | collective-permute-start | bytes 786440 | tf_op jit(solution)/shard_map/ppermute | solution.py:25
  6.0 0.2 fusion.6
  6.3 0.1 multiply_add_fusion
  6.4 0.1 fusion.1.cos_tab
  6.5 0.1 fusion.sin_tab
  6.7 3.7 %collective-permute-start.2 = (bf16[4,8,32,128]{3,2,1,0:T(8,128)(2,1)S(1)}, bf16[4,8,32,128]{3,2,1,0:T(8,128)(2,1)S(1)}, u32[]{:S(2)}, u32[]{:S(2)}) collective-permute-start(bf16[4,8,32,128]{3,2,1,0:T(8,128)(2,1)S(1)} %bitcast.17), channel_id=1, source_target_pairs={{8,0},{10,2},{12,4},{14,6},{16,8},{18,10},{20,12},{22,14},{24,16},... | collective-permute-start | bytes 786440 | tf_op jit(solution)/shard_map/ppermute | solution.py:25
  10.3 1.4 %collective-permute-start.1 = (bf16[4,8,32,128]{3,2,1,0:T(8,128)(2,1)S(1)}, bf16[4,8,32,128]{3,2,1,0:T(8,128)(2,1)S(1)}, u32[]{:S(2)}, u32[]{:S(2)}) collective-permute-start(bf16[4,8,32,128]{3,2,1,0:T(8,128)(2,1)S(1)} %bitcast.18), channel_id=1, source_target_pairs={{4,0},{6,2},{8,4},{10,6},{12,8},{14,10},{16,12},{18,14},{20,16},{2... | collective-permute-start | bytes 786440 | tf_op jit(solution)/shard_map/ppermute | solution.py:25
  11.7 0.3 collective-permute-done.partner
  12.0 0.7 %copy-done = s32[1024]{0:T(1024)S(1)} copy-done((s32[1024]{0:T(1024)S(1)}, s32[1024]{0:T(1024)}, u32[]{:S(2)}) %copy-start) | copy-done | bytes 4120
  12.7 0.7 %copy-done.1 = s32[1,9]{1,0:T(1,128)S(1)} copy-done((s32[1,9]{1,0:T(1,128)S(1)}, s32[1,9]{1,0:T(1,128)}, u32[]{:S(2)}) %copy-start.1) | copy-done | bytes 60
  13.3 5.4 %shard_map.37.rest_5_ = bf16[1,9,1,64,32,400]{5,4,3,2,1,0:T(8,128)(2,1)} custom-call(s32[1024]{0:T(1024)S(1)} %copy-done, s32[1,9]{1,0:T(1,128)S(1)} %copy-done.1, s32[8,128]{1,0:T(8,128)S(1)} %bitcast.24, bf16[2,512,128]{2,1,0:T(8,128)(2,1)S(1)} %fusion.1.cos_tab, bf16[2,512,128]{2,1,0:T(8,128)(2,1)S(1)} %fusion.sin_tab, ...), custom_call_target="tpu_custom_call" | custom-call | flops 1677721600 | bytes 3000000 | tf_op jit(solution)/shard_map/pallas_call | solution.py:189
  18.8 2.5 %collective-permute-done.1.rest_0_ = bf16[4,8,32,128]{3,2,1,0:T(8,128)(2,1)S(1)} collective-permute-done((bf16[4,8,32,128]{3,2,1,0:T(8,128)(2,1)S(1)}, bf16[4,8,32,128]{3,2,1,0:T(8,128)(2,1)S(1)}, u32[]{:S(2)}, u32[]{:S(2)}) %collective-permute-start.1) | collective-permute-done | bytes 262176 | tf_op jit(solution)/shard_map/ppermute | solution.py:25
  21.2 0.5 collective-permute-start.6
  21.8 1.5 %collective-permute-start.4 = (bf16[4,8,32,128]{3,2,1,0:T(8,128)(2,1)S(1)}, bf16[4,8,32,128]{3,2,1,0:T(8,128)(2,1)S(1)}, u32[]{:S(2)}, u32[]{:S(2)}) collective-permute-start(bf16[4,8,32,128]{3,2,1,0:T(8,128)(2,1)S(1)} %collective-permute-done.2.rest_1_), channel_id=1, source_target_pairs={{8,0},{10,2},{12,4},{14,6},{16,8},{18,10},{20,12},{22,14},{24,16},... | collective-permute-start | bytes 786440 | tf_op jit(solution)/shard_map/ppermute | solution.py:25
  23.3 3.7 %collective-permute-start.3 = (bf16[4,8,32,128]{3,2,1,0:T(8,128)(2,1)S(1)}, bf16[4,8,32,128]{3,2,1,0:T(8,128)(2,1)S(1)}, u32[]{:S(2)}, u32[]{:S(2)}) collective-permute-start(bf16[4,8,32,128]{3,2,1,0:T(8,128)(2,1)S(1)} %collective-permute-done.2.rest_1_), channel_id=1, source_target_pairs={{4,0},{6,2},{8,4},{10,6},{12,8},{14,10},{16,12},{18,14},{20,16},{2... | collective-permute-start | bytes 786440 | tf_op jit(solution)/shard_map/ppermute | solution.py:25
  26.9 15.4 %shard_map.38.rest_5_ = bf16[1,9,1,64,32,400]{5,4,3,2,1,0:T(8,128)(2,1)} custom-call(s32[1024]{0:T(1024)S(1)} %copy-done, s32[1,9]{1,0:T(1,128)S(1)} %copy-done.1, s32[8,128]{1,0:T(8,128)S(1)} %bitcast.25, bf16[2,512,128]{2,1,0:T(8,128)(2,1)S(1)} %fusion.1.cos_tab, bf16[2,512,128]{2,1,0:T(8,128)(2,1)S(1)} %fusion.sin_tab, ...), custom_call_target="tpu_custom_call", output_to_operand_aliasing={{}: (12, {})} | custom-call | flops 6710886400 | bytes 12000000 | tf_op jit(solution)/shard_map/pallas_call | solution.py:189
  42.4 0.3 collective-permute-start.8
  42.7 0.3 collective-permute-start.9
  43.0 1.0 %collective-permute-done.8.rest_3_ = bf16[4,8,32,128]{3,2,1,0:T(8,128)(2,1)S(1)} collective-permute-done((bf16[4,8,32,128]{3,2,1,0:T(8,128)(2,1)S(1)}, bf16[4,8,32,128]{3,2,1,0:T(8,128)(2,1)S(1)}, u32[]{:S(2)}, u32[]{:S(2)}) %collective-permute-start.8) | collective-permute-done | bytes 262176 | tf_op jit(solution)/shard_map/ppermute | solution.py:224
  44.0 0.4 collective-permute-done.9.rest_4_
  44.4 15.4 %shard_map.39 = bf16[1,9,1,64,32,400]{5,4,3,2,1,0:T(8,128)(2,1)} custom-call(s32[1024]{0:T(1024)S(1)} %copy-done, s32[1,9]{1,0:T(1,128)S(1)} %copy-done.1, s32[8,128]{1,0:T(8,128)S(1)} %bitcast.26, bf16[2,512,128]{2,1,0:T(8,128)(2,1)S(1)} %fusion.1.cos_tab, bf16[2,512,128]{2,1,0:T(8,128)(2,1)S(1)} %fusion.sin_tab, ...), custom_call_target="tpu_custom_call", output_to_operand_aliasing={{}: (12, {})} | custom-call | flops 6710886400 | bytes 12000000 | tf_op jit(solution)/shard_map/pallas_call | solution.py:189
  (22 shorter events, 0.5 us)
Async XLA Ops:
  2.7 9.3 %collective-permute-start = (bf16[4,8,32,128]{3,2,1,0:T(8,128)(2,1)S(1)}, bf16[4,8,32,128]{3,2,1,0:T(8,128)(2,1)S(1)}, u32[]{:S(2)}, u32[]{:S(2)}) collective-permute-start(bf16[4,8,32,128]{3,2,1,0:T(8,128)(2,1)S(1)} %bitcast.16), channel_id=1, source_target_pairs={{1,0},{0,1},{3,2},{2,3},{5,4},{4,5},{7,6},{6,7},{9,8},{8,9},{11,10... | collective-permute-start | bytes 786440 | tf_op jit(solution)/shard_map/ppermute | solution.py:25
  6.7 12.1 %collective-permute-start.2 = (bf16[4,8,32,128]{3,2,1,0:T(8,128)(2,1)S(1)}, bf16[4,8,32,128]{3,2,1,0:T(8,128)(2,1)S(1)}, u32[]{:S(2)}, u32[]{:S(2)}) collective-permute-start(bf16[4,8,32,128]{3,2,1,0:T(8,128)(2,1)S(1)} %bitcast.17), channel_id=1, source_target_pairs={{8,0},{10,2},{12,4},{14,6},{16,8},{18,10},{20,12},{22,14},{24,16},... | collective-permute-start | bytes 786440 | tf_op jit(solution)/shard_map/ppermute | solution.py:25
  10.3 10.9 %collective-permute-start.1 = (bf16[4,8,32,128]{3,2,1,0:T(8,128)(2,1)S(1)}, bf16[4,8,32,128]{3,2,1,0:T(8,128)(2,1)S(1)}, u32[]{:S(2)}, u32[]{:S(2)}) collective-permute-start(bf16[4,8,32,128]{3,2,1,0:T(8,128)(2,1)S(1)} %bitcast.18), channel_id=1, source_target_pairs={{4,0},{6,2},{8,4},{10,6},{12,8},{14,10},{16,12},{18,14},{20,16},{2... | collective-permute-start | bytes 786440 | tf_op jit(solution)/shard_map/ppermute | solution.py:25
  12.0 0.7 %copy-start = (s32[1024]{0:T(1024)S(1)}, s32[1024]{0:T(1024)}, u32[]{:S(2)}) copy-start(s32[1024]{0:T(1024)} %channels.5) | copy-start | bytes 12292
  12.7 0.7 %copy-start.1 = (s32[1,9]{1,0:T(1,128)S(1)}, s32[1,9]{1,0:T(1,128)}, u32[]{:S(2)}) copy-start(s32[1,9]{1,0:T(1,128)} %plan.5) | copy-start | bytes 112
  21.2 5.7 %collective-permute-start.5 = (bf16[4,8,32,128]{3,2,1,0:T(8,128)(2,1)S(1)}, bf16[4,8,32,128]{3,2,1,0:T(8,128)(2,1)S(1)}, u32[]{:S(2)}, u32[]{:S(2)}) collective-permute-start(bf16[4,8,32,128]{3,2,1,0:T(8,128)(2,1)S(1)} %bitcast.21), channel_id=1, source_target_pairs={{2,0},{0,2},{6,4},{4,6},{10,8},{8,10},{14,12},{12,14},{18,16},{16,... | collective-permute-start | bytes 786440 | tf_op jit(solution)/shard_map/ppermute | solution.py:224
  21.2 5.7 %collective-permute-start.6 = (bf16[4,8,32,128]{3,2,1,0:T(8,128)(2,1)S(1)}, bf16[4,8,32,128]{3,2,1,0:T(8,128)(2,1)S(1)}, u32[]{:S(2)}, u32[]{:S(2)}) collective-permute-start(bf16[4,8,32,128]{3,2,1,0:T(8,128)(2,1)S(1)} %collective-permute-done.1.rest_0_), channel_id=1, source_target_pairs={{2,0},{0,2},{6,4},{4,6},{10,8},{8,10},{14,12},{12,14},{18,16},{16,... | collective-permute-start | bytes 786440 | tf_op jit(solution)/shard_map/ppermute | solution.py:224
  21.8 5.2 %collective-permute-start.7 = (bf16[4,8,32,128]{3,2,1,0:T(8,128)(2,1)S(1)}, bf16[4,8,32,128]{3,2,1,0:T(8,128)(2,1)S(1)}, u32[]{:S(2)}, u32[]{:S(2)}) collective-permute-start(bf16[4,8,32,128]{3,2,1,0:T(8,128)(2,1)S(1)} %collective-permute-done.2.rest_1_), channel_id=1, source_target_pairs={{2,0},{0,2},{6,4},{4,6},{10,8},{8,10},{14,12},{12,14},{18,16},{16,... | collective-permute-start | bytes 786440 | tf_op jit(solution)/shard_map/ppermute | solution.py:224
  21.8 20.6 %collective-permute-start.4 = (bf16[4,8,32,128]{3,2,1,0:T(8,128)(2,1)S(1)}, bf16[4,8,32,128]{3,2,1,0:T(8,128)(2,1)S(1)}, u32[]{:S(2)}, u32[]{:S(2)}) collective-permute-start(bf16[4,8,32,128]{3,2,1,0:T(8,128)(2,1)S(1)} %collective-permute-done.2.rest_1_), channel_id=1, source_target_pairs={{8,0},{10,2},{12,4},{14,6},{16,8},{18,10},{20,12},{22,14},{24,16},... | collective-permute-start | bytes 786440 | tf_op jit(solution)/shard_map/ppermute | solution.py:25
  23.3 19.1 %collective-permute-start.3 = (bf16[4,8,32,128]{3,2,1,0:T(8,128)(2,1)S(1)}, bf16[4,8,32,128]{3,2,1,0:T(8,128)(2,1)S(1)}, u32[]{:S(2)}, u32[]{:S(2)}) collective-permute-start(bf16[4,8,32,128]{3,2,1,0:T(8,128)(2,1)S(1)} %collective-permute-done.2.rest_1_), channel_id=1, source_target_pairs={{4,0},{6,2},{8,4},{10,6},{12,8},{14,10},{16,12},{18,14},{20,16},{2... | collective-permute-start | bytes 786440 | tf_op jit(solution)/shard_map/ppermute | solution.py:25
  42.4 1.6 %collective-permute-start.8 = (bf16[4,8,32,128]{3,2,1,0:T(8,128)(2,1)S(1)}, bf16[4,8,32,128]{3,2,1,0:T(8,128)(2,1)S(1)}, u32[]{:S(2)}, u32[]{:S(2)}) collective-permute-start(bf16[4,8,32,128]{3,2,1,0:T(8,128)(2,1)S(1)} %collective-permute-done.3.rest_0_), channel_id=1, source_target_pairs={{2,0},{0,2},{6,4},{4,6},{10,8},{8,10},{14,12},{12,14},{18,16},{16,... | collective-permute-start | bytes 786440 | tf_op jit(solution)/shard_map/ppermute | solution.py:224
  42.7 1.7 %collective-permute-start.9 = (bf16[4,8,32,128]{3,2,1,0:T(8,128)(2,1)S(1)}, bf16[4,8,32,128]{3,2,1,0:T(8,128)(2,1)S(1)}, u32[]{:S(2)}, u32[]{:S(2)}) collective-permute-start(bf16[4,8,32,128]{3,2,1,0:T(8,128)(2,1)S(1)} %collective-permute-done.4.rest_1_), channel_id=1, source_target_pairs={{2,0},{0,2},{6,4},{4,6},{10,8},{8,10},{14,12},{12,14},{18,16},{16,... | collective-permute-start | bytes 786440 | tf_op jit(solution)/shard_map/ppermute | solution.py:224

commit v4 on v3

--- a/solution.py
+++ b/solution.py
@@ -69,7 +69,7 @@
     return cos_tab.reshape(2, freq_count, LANES), sin_tab.reshape(2, freq_count, LANES)
 
 
-def correlate_kernel(channels, plan, ids, cos_tab, sin_tab, own, partner, *rest, first, picks):
+def correlate_kernel(info, ids, cos_tab, sin_tab, own, partner, *rest, first, picks):
     out, rows, turn, cols, sems = rest[-5:]
     count = cols.shape[0]
     tiles, parts, col_count, _ = own.shape
@@ -80,7 +80,9 @@
     step, half = pl.program_id(0), pl.program_id(1)
 
     def fetch(k, parity):
-        return pltpu.make_async_copy(rest[picks[k][parity]], cols.at[k], sems.at[k])
+        source, index = picks[k][parity]
+        array = rest[source] if index is None else rest[source].at[index]
+        return pltpu.make_async_copy(array, cols.at[k], sems.at[k])
 
     @pl.when((step == 0) & (half == 0))
     def _():
@@ -103,7 +105,7 @@
     id_line = pltpu.roll(line, (LANES - row_start % LANES) % LANES, 1)[0:1, :]
     col_start = (blk + first + step) % blk_count * row_count + group * col_count
     for j in range(col_count):
-        turn[j:j + 1, :] = jnp.where(id_line < channels[col_start + j], 1.0, -1.0)
+        turn[j:j + 1, :] = jnp.where(id_line < info[col_start + j], 1.0, -1.0)
 
     lane = lax.broadcasted_iota(jnp.int32, (col_count, LANES), 1)
     low = lane <= TURN
@@ -173,23 +175,25 @@
                 out[0, 0, 0, j, j:j + 1, :] = jnp.zeros((1, out.shape[-1]), jnp.bfloat16)
 
 
-def correlate(channels, plan, ids, tables, own, partner, arrays, picks, first, output, step_count):
+def correlate(info, plan_start, tables, own, partner, arrays, picks, first, output, step_count):
     count = len(picks)
     tiles, parts, col_count, _ = own.shape
     lag_count = 2 * HALF_LAG
     kept = [] if output is None else [output]
+    ids = info.reshape(-1, LANES)
 
     def whole(array):
         return pl.BlockSpec(array.shape, lambda *_: (0,) * array.ndim)
 
-    def slot(d, half, channels, plan):
-        return (0, sum(jnp.where(plan[0, t] == first + d, t, 0) for t in range(step_count)), 0, half, 0, 0)
+    def slot(d, half, info):
+        place = sum(jnp.where(info[plan_start + t] == first + d, t, 0) for t in range(step_count))
+        return (0, place, 0, half, 0, 0)
 
     pairs = count * 2 * col_count * col_count * tiles * LANES
     return pl.pallas_call(
         functools.partial(correlate_kernel, first=first, picks=picks),
         grid_spec=pltpu.PrefetchScalarGridSpec(
-            num_scalar_prefetch=2,
+            num_scalar_prefetch=1,
             grid=(count, 2),
             in_specs=[whole(ids), whole(tables[0]), whole(tables[1]), whole(own), whole(partner)]
             + [pl.BlockSpec(memory_space=pl.ANY)] * (len(arrays) + len(kept)),
@@ -202,10 +206,10 @@
             ],
         ),
         out_shape=jax.ShapeDtypeStruct((1, step_count, 1, 2 * col_count, col_count, lag_count), jnp.bfloat16),
-        input_output_aliases={7 + len(arrays): 0} if kept else {},
+        input_output_aliases={6 + len(arrays): 0} if kept else {},
         cost_estimate=pl.CostEstimate(flops=1600 * pairs, bytes_accessed=count * 3000000, transcendentals=0),
         compiler_params=pltpu.CompilerParams(vmem_limit_bytes=40 << 20),
-    )(channels, plan, ids, *tables, own, partner, *arrays, *kept)
+    )(info, ids, *tables, own, partner, *arrays, *kept)
 
 
 def whiten_tiles(spectra):
@@ -218,31 +222,36 @@
     col_count, _, seg_count, freq_count = spectra.shape
     blk_count = lax.axis_size("blk")
     step_count = blk_count // 2 + 1
-    ids = channel_ids.reshape(-1, LANES)
+    id_count = channel_ids.shape[0]
+    info = jnp.concatenate([channel_ids, plan[0], jnp.zeros((-(id_count + step_count) % (8 * LANES),), jnp.int32)])
 
     def other_core(block):
         return lax.ppermute(block, "blk", [(i ^ 1, i) for i in range(blk_count)])
 
     own = whiten_tiles(spectra)
     partner = passed_along(own, "grp", 1)
+    sent, info = lax.optimization_barrier((own, info))
+    near, far = passed_along(sent, "blk", -2), passed_along(sent, "blk", -4)
     tables = half_lag_tables(freq_count, 1.0 / math.sqrt(2.0 * freq_count * seg_count))
-    sent, tables = lax.optimization_barrier((own, tables))
-    near, far = passed_along(sent, "blk", -2), passed_along(sent, "blk", -4)
 
     def stage(arrays, picks, first, output):
-        return correlate(channel_ids, plan, ids, tables, own, partner, arrays, picks, first, output, step_count)
-
-    output = stage([own], [(0, 0)], 0, None)
+        return correlate(info, id_count, tables, own, partner, arrays, picks, first, output, step_count)
+
+    output = stage([own], [((0, None), (0, None))], 0, None)
     last = own
     for first in range(1, step_count, 4):
-        near, far, last, output = lax.optimization_barrier((near, far, last, output))
+        if first == 1:
+            near, far, last, output = lax.optimization_barrier((near, far, last, output))
+            pair = jnp.stack([near, far])
+            before = (other_core(last), None)
+        else:
+            pair, output = lax.optimization_barrier((later, output))
+            before = (crossed, 1)
         if first + 4 < step_count:
-            later = passed_along(far, "blk", -2), passed_along(far, "blk", -4)
-        taken = other_core(last) if first == 1 else crossed
-        crossed = other_core(far)
-        arrays = [near, far, taken, other_core(near), crossed]
-        output = stage(arrays, [(2, 3), (0, 0), (3, 4), (1, 1)], first, output)
-        last, (near, far) = far, later
+            later = passed_along(pair, "blk", -4)
+        crossed = other_core(pair)
+        picks = [((0, before[1]), (2, 0)), ((1, 0),) * 2, ((2, 0), (2, 1)), ((1, 1),) * 2]
+        output = stage([before[0], pair, crossed], picks, first, output)
     return output
 
 

time: 60.1 us -> 60 us (level)
  waiting for transfers between devices: 4.16 us -> 5.85 us
  starting transfers between devices: 14.3 us -> 12.9 us
    unnamed x4 -> x0, local copies, waits for them, and re-layouts: 1.34 us -> none
    ppermute x5 -> x4, waiting for transfers between devices: 2.76 us -> 3.95 us  [passed_along(): return lax.ppermute(block, axis, route)]
    ppermute x5 -> x4, starting transfers between devices: 13.2 us -> 12.3 us  [passed_along(): return lax.ppermute(block, axis, route)]
    concatenate x0 -> x1, local copies, waits for them, and re-layouts: none -> 0.76 us  [on_device_fused(): jnp.concatenate([channel_ids, plan[0], jnp.zeros((-(id_count + step_count...]
    ppermute x5 -> x3, waiting for transfers between devices: 1.41 us -> 1.9 us  [other_core(): return lax.ppermute(block, 'blk', [(i ^ 1, i) for i in range(blk_count)])]
  transfers between devices with their start and end apart: 10 -> 7, of which waited for: 4 -> 2; matrix products, arithmetic and copies ran while one was open for 2% -> 3% of each run, Pallas kernels for 35% -> 35%
where the time goes in v4:
time: 60 us; the launch traced here: 59.8 us
  Pallas kernels  36.5 us (61%)
  starting transfers between devices  12.9 us (22%)
  waiting for transfers between devices  5.85 us (10%)
  other arithmetic  3.34 us (6%)
  local copies, waits for them, and re-layouts  1.05 us (2%)
    pallas_call x3, Pallas kernels, correlate(): pl.pallas_call(functools.partial(correlate_kernel, first=first, picks=pic...  36.5 us
    ppermute x4, starting transfers between devices, passed_along(): return lax.ppermute(block, axis, route)  12.3 us
    ppermute x4, waiting for transfers between devices, passed_along(): return lax.ppermute(block, axis, route)  3.95 us
    ppermute x3, waiting for transfers between devices, other_core(): return lax.ppermute(block, 'blk', [(i ^ 1, i) for i in range(blk_count)])  1.9 us
    reduce_sum x1, other arithmetic, whiten(): seg_power = jnp.mean(spectra * spectra, axis=(1, 3))  1.22 us
  transfers between devices with their start and end apart: 7, of which 2 were waited for; matrix products, arithmetic and copies ran while one was open for 3% of the time, Pallas kernels for 35%

profile of v4, /device:TPU:0, one launch (start us, length us, event | category | flops | bytes accessed | tf_op | source)
XLA Modules:
  0.0 59.8 jit_solution(83111189278948145)
XLA Ops:
  0.0 1.2 %multiply_reduce_fusion = f32[32,4]{1,0:T(8,128)S(1)} fusion(f32[32,2,4,512]{3,2,1,0:T(4,128)} %param.3), kind=kLoop, calls=%fused_computation.8 | loop fusion | flops 262016 | bytes 524800 | tf_op jit(solution)/shard_map/reduce_sum | solution.py:29
  1.2 1.2 %multiply_convert_fusion = bf16[32,2,4,512]{3,2,1,0:T(4,128)(2,1)S(1)} fusion(f32[32,2,4,512]{3,2,1,0:T(4,128)} %param.3, f32[32,4]{1,0:T(8,128)S(1)} %add_rsqrt_fusion), kind=kLoop, calls=%fused_computation.7 | loop fusion | flops 262144 | bytes 786944 | tf_op jit(solution)/shard_map/convert_element_type | solution.py:31
  2.4 0.1 reshape.251
  2.5 0.1 copy.19
  2.7 3.0 %collective-permute-start = (bf16[4,8,32,128]{3,2,1,0:T(8,128)(2,1)S(1)}, bf16[4,8,32,128]{3,2,1,0:T(8,128)(2,1)S(1)}, u32[]{:S(2)}, u32[]{:S(2)}) collective-permute-start(bf16[4,8,32,128]{3,2,1,0:T(8,128)(2,1)S(1)} %bitcast.19), channel_id=1, source_target_pairs={{1,0},{0,1},{3,2},{2,3},{5,4},{4,5},{7,6},{6,7},{9,8},{8,9},{11,10... | collective-permute-start | bytes 786440 | tf_op jit(solution)/shard_map/ppermute | solution.py:25
  5.7 0.8 %concatenate.3.info = s32[2048]{0:T(1024)S(1)} concatenate(s32[1024]{0:T(1024)} %param.4, s32[9]{0:T(128)} %bitcast.36, s32[1015]{0:T(1024)S(1)} %broadcast_in_dim.14), dimensions={0} | concatenate | bytes 16384 | tf_op jit(solution)/shard_map/concatenate | solution.py:226
  6.5 4.5 %collective-permute-start.1 = (bf16[4,8,32,128]{3,2,1,0:T(8,128)(2,1)S(1)}, bf16[4,8,32,128]{3,2,1,0:T(8,128)(2,1)S(1)}, u32[]{:S(2)}, u32[]{:S(2)}) collective-permute-start(bf16[4,8,32,128]{3,2,1,0:T(8,128)(2,1)S(1)} %bitcast.20), channel_id=1, source_target_pairs={{4,0},{6,2},{8,4},{10,6},{12,8},{14,10},{16,12},{18,14},{20,16},{2... | collective-permute-start | bytes 786440 | tf_op jit(solution)/shard_map/ppermute | solution.py:25
  11.0 0.4 collective-permute-start.2
  11.5 0.1 select_select_fusion
  11.5 0.1 fusion.13
  11.6 0.2 fusion.6
  11.9 0.1 fusion.16
  11.9 0.1 select_n.104
  12.0 0.1 multiply_add_fusion
  12.1 0.1 fusion.1.cos_tab
  12.3 0.1 fusion.sin_tab
  12.4 5.5 %shard_map.37.rest_3_ = bf16[1,9,1,64,32,400]{5,4,3,2,1,0:T(8,128)(2,1)} custom-call(s32[2048]{0:T(1024)S(1)} %concatenate.3.info, s32[16,128]{1,0:T(8,128)S(1)} %bitcast.27, bf16[2,512,128]{2,1,0:T(8,128)(2,1)S(1)} %fusion.1.cos_tab, bf16[2,512,128]{2,1,0:T(8,128)(2,1)S(1)} %fusion.sin_tab, bf16[4,8,32,128]{3,2,1,0:T(8,128)(2,1)S(1)} %bitcast.22, ...), custom_call_target="tpu_custom_call" | custom-call | flops 1677721600 | bytes 3000000 | tf_op jit(solution)/shard_map/pallas_call | solution.py:193
  17.9 3.9 %collective-permute-done.2 = bf16[4,8,32,128]{3,2,1,0:T(8,128)(2,1)S(1)} collective-permute-done((bf16[4,8,32,128]{3,2,1,0:T(8,128)(2,1)S(1)}, bf16[4,8,32,128]{3,2,1,0:T(8,128)(2,1)S(1)}, u32[]{:S(2)}, u32[]{:S(2)}) %collective-permute-start.2) | collective-permute-done | bytes 262176 | tf_op jit(solution)/shard_map/ppermute | solution.py:25
  21.9 0.1 collective-permute-start.3
  22.0 0.5 collective-permute-start.5
  22.5 4.3 %collective-permute-start.4 = (bf16[2,4,8,32,128]{4,3,2,1,0:T(8,128)(2,1)S(1)}, bf16[2,4,8,32,128]{4,3,2,1,0:T(8,128)(2,1)S(1)}, u32[]{:S(2)}, u32[]{:S(2)}) collective-permute-start(bf16[2,4,8,32,128]{4,3,2,1,0:T(8,128)(2,1)S(1)} %pad_maximum_fusion.rest_1_), channel_id=1, source_target_pairs={{8,0},{10,2},{12,4},{14,6},{16,8},{18,10},{20,12},{22,14},{24,16},... | collective-permute-start | bytes 1572872 | tf_op jit(solution)/shard_map/ppermute | solution.py:25
  26.8 15.5 %shard_map.38.rest_3_ = bf16[1,9,1,64,32,400]{5,4,3,2,1,0:T(8,128)(2,1)} custom-call(s32[2048]{0:T(1024)S(1)} %concatenate.3.info, s32[16,128]{1,0:T(8,128)S(1)} %bitcast.28, bf16[2,512,128]{2,1,0:T(8,128)(2,1)S(1)} %fusion.1.cos_tab, bf16[2,512,128]{2,1,0:T(8,128)(2,1)S(1)} %fusion.sin_tab, ...), custom_call_target="tpu_custom_call", output_to_operand_aliasing={{}: (9, {})} | custom-call | flops 6710886400 | bytes 12000000 | tf_op jit(solution)/shard_map/pallas_call | solution.py:193
  42.4 1.9 %collective-permute-done.6.rest_2_ = bf16[2,4,8,32,128]{4,3,2,1,0:T(8,128)(2,1)S(1)} collective-permute-done((bf16[2,4,8,32,128]{4,3,2,1,0:T(8,128)(2,1)S(1)}, bf16[2,4,8,32,128]{4,3,2,1,0:T(8,128)(2,1)S(1)}, u32[]{:S(2)}, u32[]{:S(2)}) %collective-permute-start.6) | collective-permute-done | bytes 524320 | tf_op jit(solution)/shard_map/ppermute | solution.py:229
  44.3 15.5 %shard_map.39 = bf16[1,9,1,64,32,400]{5,4,3,2,1,0:T(8,128)(2,1)} custom-call(s32[2048]{0:T(1024)S(1)} %concatenate.3.info, s32[16,128]{1,0:T(8,128)S(1)} %bitcast.29, bf16[2,512,128]{2,1,0:T(8,128)(2,1)S(1)} %fusion.1.cos_tab, bf16[2,512,128]{2,1,0:T(8,128)(2,1)S(1)} %fusion.sin_tab, ...), custom_call_target="tpu_custom_call", output_to_operand_aliasing={{}: (9, {})} | custom-call | flops 6710886400 | bytes 12000000 | tf_op jit(solution)/shard_map/pallas_call | solution.py:193
  (15 shorter events, 0.2 us)
Async XLA Ops:
  2.7 9.8 %collective-permute-start = (bf16[4,8,32,128]{3,2,1,0:T(8,128)(2,1)S(1)}, bf16[4,8,32,128]{3,2,1,0:T(8,128)(2,1)S(1)}, u32[]{:S(2)}, u32[]{:S(2)}) collective-permute-start(bf16[4,8,32,128]{3,2,1,0:T(8,128)(2,1)S(1)} %bitcast.19), channel_id=1, source_target_pairs={{1,0},{0,1},{3,2},{2,3},{5,4},{4,5},{7,6},{6,7},{9,8},{8,9},{11,10... | collective-permute-start | bytes 786440 | tf_op jit(solution)/shard_map/ppermute | solution.py:25
  6.5 11.5 %collective-permute-start.1 = (bf16[4,8,32,128]{3,2,1,0:T(8,128)(2,1)S(1)}, bf16[4,8,32,128]{3,2,1,0:T(8,128)(2,1)S(1)}, u32[]{:S(2)}, u32[]{:S(2)}) collective-permute-start(bf16[4,8,32,128]{3,2,1,0:T(8,128)(2,1)S(1)} %bitcast.20), channel_id=1, source_target_pairs={{4,0},{6,2},{8,4},{10,6},{12,8},{14,10},{16,12},{18,14},{20,16},{2... | collective-permute-start | bytes 786440 | tf_op jit(solution)/shard_map/ppermute | solution.py:25
  11.0 10.9 %collective-permute-start.2 = (bf16[4,8,32,128]{3,2,1,0:T(8,128)(2,1)S(1)}, bf16[4,8,32,128]{3,2,1,0:T(8,128)(2,1)S(1)}, u32[]{:S(2)}, u32[]{:S(2)}) collective-permute-start(bf16[4,8,32,128]{3,2,1,0:T(8,128)(2,1)S(1)} %bitcast.21), channel_id=1, source_target_pairs={{8,0},{10,2},{12,4},{14,6},{16,8},{18,10},{20,12},{22,14},{24,16},... | collective-permute-start | bytes 786440 | tf_op jit(solution)/shard_map/ppermute | solution.py:25
  21.9 4.9 %collective-permute-start.3 = (bf16[2,4,8,32,128]{4,3,2,1,0:T(8,128)(2,1)S(1)}, bf16[2,4,8,32,128]{4,3,2,1,0:T(8,128)(2,1)S(1)}, u32[]{:S(2)}, u32[]{:S(2)}) collective-permute-start(bf16[2,4,8,32,128]{4,3,2,1,0:T(8,128)(2,1)S(1)} %pad_maximum_fusion.rest_1_), channel_id=1, source_target_pairs={{2,0},{0,2},{6,4},{4,6},{10,8},{8,10},{14,12},{12,14},{18,16},{16,... | collective-permute-start | bytes 1572872 | tf_op jit(solution)/shard_map/ppermute | solution.py:229
  22.0 4.8 %collective-permute-start.5 = (bf16[4,8,32,128]{3,2,1,0:T(8,128)(2,1)S(1)}, bf16[4,8,32,128]{3,2,1,0:T(8,128)(2,1)S(1)}, u32[]{:S(2)}, u32[]{:S(2)}) collective-permute-start(bf16[4,8,32,128]{3,2,1,0:T(8,128)(2,1)S(1)} %bitcast.24), channel_id=1, source_target_pairs={{2,0},{0,2},{6,4},{4,6},{10,8},{8,10},{14,12},{12,14},{18,16},{16,... | collective-permute-start | bytes 786440 | tf_op jit(solution)/shard_map/ppermute | solution.py:229
  22.5 19.8 %collective-permute-start.4 = (bf16[2,4,8,32,128]{4,3,2,1,0:T(8,128)(2,1)S(1)}, bf16[2,4,8,32,128]{4,3,2,1,0:T(8,128)(2,1)S(1)}, u32[]{:S(2)}, u32[]{:S(2)}) collective-permute-start(bf16[2,4,8,32,128]{4,3,2,1,0:T(8,128)(2,1)S(1)} %pad_maximum_fusion.rest_1_), channel_id=1, source_target_pairs={{8,0},{10,2},{12,4},{14,6},{16,8},{18,10},{20,12},{22,14},{24,16},... | collective-permute-start | bytes 1572872 | tf_op jit(solution)/shard_map/ppermute | solution.py:25
  42.3 2.0 %collective-permute-start.6 = (bf16[2,4,8,32,128]{4,3,2,1,0:T(8,128)(2,1)S(1)}, bf16[2,4,8,32,128]{4,3,2,1,0:T(8,128)(2,1)S(1)}, u32[]{:S(2)}, u32[]{:S(2)}) collective-permute-start(bf16[2,4,8,32,128]{4,3,2,1,0:T(8,128)(2,1)S(1)} %collective-permute-done.4.rest_1_), channel_id=1, source_target_pairs={{2,0},{0,2},{6,4},{4,6},{10,8},{8,10},{14,12},{12,14},{18,16},{16,... | collective-permute-start | bytes 1572872 | tf_op jit(solution)/shard_map/ppermute | solution.py:229

commit v5 on v4

--- a/solution.py
+++ b/solution.py
@@ -69,34 +69,37 @@
     return cos_tab.reshape(2, freq_count, LANES), sin_tab.reshape(2, freq_count, LANES)
 
 
-def correlate_kernel(info, ids, cos_tab, sin_tab, own, partner, *rest, first, picks):
+def correlate_kernel(info, ids, cos_tab, sin_tab, *rest, first, picks, side):
+    sources, rest = rest[:2 - (side is not None)], rest[2 - (side is not None):]
     out, rows, turn, cols, sems = rest[-5:]
     count = cols.shape[0]
-    tiles, parts, col_count, _ = own.shape
+    tiles, parts, col_count, _ = sources[0].shape
     seg_count = parts // 2
     row_count = 2 * col_count
     depth = 2 * LANES
     blk, group, blk_count = lax.axis_index("blk"), lax.axis_index("grp"), lax.axis_size("blk")
-    step, half = pl.program_id(0), pl.program_id(1)
+    step = pl.program_id(0)
+    half = pl.program_id(1) if side is None else (group + side) % 2
+    opening = (step == 0) & (pl.program_id(1) == 0)
 
     def fetch(k, parity):
         source, index = picks[k][parity]
         array = rest[source] if index is None else rest[source].at[index]
         return pltpu.make_async_copy(array, cols.at[k], sems.at[k])
 
-    @pl.when((step == 0) & (half == 0))
+    @pl.when(opening)
     def _():
         for parity in range(2):
             @pl.when(blk % 2 == parity)
             def _(parity=parity):
                 for k in range(count):
                     fetch(k, parity).start()
-        for source, place in ((own, group), (partner, 1 - group)):
+        for source, place in zip(sources, (group, 1 - group) if side is None else (half,)):
             for q in range(tiles):
                 rows[place, q] = source[q]
 
     for k in range(count):
-        @pl.when((step == k) & (half == 0))
+        @pl.when((step == k) & (pl.program_id(1) == 0))
         def _(k=k):
             fetch(k, 0).wait()
 
@@ -168,16 +171,17 @@
         *[pltpu.ACC(1)((col_count, depth), jnp.float32)] * col_count,
     )
 
-    if first == 0:
+    if first == 0 and side != 1:
         @pl.when((step == 0) & (half == group))
         def _():
             for j in range(col_count):
                 out[0, 0, 0, j, j:j + 1, :] = jnp.zeros((1, out.shape[-1]), jnp.bfloat16)
 
 
-def correlate(info, plan_start, tables, own, partner, arrays, picks, first, output, step_count):
+def correlate(info, plan_start, tables, sources, arrays, picks, first, output, step_count, side):
     count = len(picks)
-    tiles, parts, col_count, _ = own.shape
+    tiles, parts, col_count, _ = sources[0].shape
+    halves = 2 if side is None else 1
     lag_count = 2 * HALF_LAG
     kept = [] if output is None else [output]
     ids = info.reshape(-1, LANES)
@@ -187,15 +191,15 @@
 
     def slot(d, half, info):
         place = sum(jnp.where(info[plan_start + t] == first + d, t, 0) for t in range(step_count))
-        return (0, place, 0, half, 0, 0)
-
-    pairs = count * 2 * col_count * col_count * tiles * LANES
+        return (0, place, 0, half if side is None else (info[plan_start + step_count] + side) % 2, 0, 0)
+
+    pairs = count * halves * col_count * col_count * tiles * LANES
     return pl.pallas_call(
-        functools.partial(correlate_kernel, first=first, picks=picks),
+        functools.partial(correlate_kernel, first=first, picks=picks, side=side),
         grid_spec=pltpu.PrefetchScalarGridSpec(
             num_scalar_prefetch=1,
-            grid=(count, 2),
-            in_specs=[whole(ids), whole(tables[0]), whole(tables[1]), whole(own), whole(partner)]
+            grid=(count, halves),
+            in_specs=[whole(array) for array in (ids, *tables, *sources)]
             + [pl.BlockSpec(memory_space=pl.ANY)] * (len(arrays) + len(kept)),
             out_specs=pl.BlockSpec((1, 1, 1, col_count, col_count, lag_count), slot),
             scratch_shapes=[
@@ -206,10 +210,10 @@
             ],
         ),
         out_shape=jax.ShapeDtypeStruct((1, step_count, 1, 2 * col_count, col_count, lag_count), jnp.bfloat16),
-        input_output_aliases={6 + len(arrays): 0} if kept else {},
-        cost_estimate=pl.CostEstimate(flops=1600 * pairs, bytes_accessed=count * 3000000, transcendentals=0),
+        input_output_aliases={4 + len(sources) + len(arrays): 0} if kept else {},
+        cost_estimate=pl.CostEstimate(flops=1600 * pairs, bytes_accessed=count * halves * 1500000, transcendentals=0),
         compiler_params=pltpu.CompilerParams(vmem_limit_bytes=40 << 20),
-    )(info, ids, *tables, own, partner, *arrays, *kept)
+    )(info, ids, *tables, *sources, *arrays, *kept)
 
 
 def whiten_tiles(spectra):
@@ -223,7 +227,8 @@
     blk_count = lax.axis_size("blk")
     step_count = blk_count // 2 + 1
     id_count = channel_ids.shape[0]
-    info = jnp.concatenate([channel_ids, plan[0], jnp.zeros((-(id_count + step_count) % (8 * LANES),), jnp.int32)])
+    rest = jnp.zeros((-(id_count + step_count + 1) % (8 * LANES),), jnp.int32)
+    info = jnp.concatenate([channel_ids, plan[0], lax.axis_index("grp")[None], rest])
 
     def other_core(block):
         return lax.ppermute(block, "blk", [(i ^ 1, i) for i in range(blk_count)])
@@ -234,16 +239,19 @@
     near, far = passed_along(sent, "blk", -2), passed_along(sent, "blk", -4)
     tables = half_lag_tables(freq_count, 1.0 / math.sqrt(2.0 * freq_count * seg_count))
 
-    def stage(arrays, picks, first, output):
-        return correlate(info, id_count, tables, own, partner, arrays, picks, first, output, step_count)
-
-    output = stage([own], [((0, None), (0, None))], 0, None)
-    last = own
+    def stage(sources, arrays, picks, first, output, side=None):
+        return correlate(info, id_count, tables, sources, arrays, picks, first, output, step_count, side)
+
+    alone = [((0, None), (0, None))]
+    output = stage([own], [own], alone, 0, None, 0)
+    last, partner, output = lax.optimization_barrier((own, partner, output))
+    swapped = other_core(last)
+    output = stage([partner], [own], alone, 0, output, 1)
     for first in range(1, step_count, 4):
         if first == 1:
-            near, far, last, output = lax.optimization_barrier((near, far, last, output))
+            near, far, swapped, output = lax.optimization_barrier((near, far, swapped, output))
             pair = jnp.stack([near, far])
-            before = (other_core(last), None)
+            before = (swapped, None)
         else:
             pair, output = lax.optimization_barrier((later, output))
             before = (crossed, 1)
@@ -251,7 +259,7 @@
             later = passed_along(pair, "blk", -4)
         crossed = other_core(pair)
         picks = [((0, before[1]), (2, 0)), ((1, 0),) * 2, ((2, 0), (2, 1)), ((1, 1),) * 2]
-        output = stage([before[0], pair, crossed], picks, first, output)
+        output = stage([own, partner], [before[0], pair, crossed], picks, first, output)
     return output
 
 

time: 60 us -> 59.6 us (level)
  waiting for transfers between devices: 5.85 us -> 4.01 us
  Pallas kernels: 36.5 us -> 38.1 us
    ppermute x4, waiting for transfers between devices: 3.95 us -> 2.25 us  [passed_along(): return lax.ppermute(block, axis, route)]
    pallas_call x3 -> x4, Pallas kernels: 36.5 us -> 38.1 us  [correlate(): pl.pallas_call(functools.partial(correlate_kernel, first=first, picks=pic...]
  transfers between devices with their start and end apart: 7 -> 7, of which waited for: 2 -> 2; matrix products, arithmetic and copies ran while one was open for 3% -> 3% of each run, Pallas kernels for 35% -> 38%
where the time goes in v5:
time: 59.6 us; the launch traced here: 59.3 us
  Pallas kernels  38.1 us (64%)
  starting transfers between devices  12.7 us (21%)
  waiting for transfers between devices  4.01 us (7%)
  other arithmetic  3.34 us (6%)
  local copies, waits for them, and re-layouts  1.06 us (2%)
    pallas_call x4, Pallas kernels, correlate(): pl.pallas_call(functools.partial(correlate_kernel, first=first, picks=pic...  38.1 us
    ppermute x4, starting transfers between devices, passed_along(): return lax.ppermute(block, axis, route)  12.3 us
    ppermute x4, waiting for transfers between devices, passed_along(): return lax.ppermute(block, axis, route)  2.25 us
    ppermute x3, waiting for transfers between devices, other_core(): return lax.ppermute(block, 'blk', [(i ^ 1, i) for i in range(blk_count)])  1.75 us
    reduce_sum x1, other arithmetic, whiten(): seg_power = jnp.mean(spectra * spectra, axis=(1, 3))  1.22 us
    convert_element_type x1, other arithmetic, whiten(): whitened = whitened.astype(jnp.bfloat16)  1.2 us
  transfers between devices with their start and end apart: 7, of which 2 were waited for; matrix products, arithmetic and copies ran while one was open for 3% of the time, Pallas kernels for 38%

profile of v5, /device:TPU:0, one launch (start us, length us, event | category | flops | bytes accessed | tf_op | source)
XLA Modules:
  0.0 59.3 jit_solution(6506506024784994280)
XLA Ops:
  0.0 1.2 %multiply_reduce_fusion = f32[32,4]{1,0:T(8,128)S(1)} fusion(f32[32,2,4,512]{3,2,1,0:T(4,128)} %param.3), kind=kLoop, calls=%fused_computation.8 | loop fusion | flops 262016 | bytes 524800 | tf_op jit(solution)/shard_map/reduce_sum | solution.py:29
  1.2 1.2 %multiply_convert_fusion = bf16[32,2,4,512]{3,2,1,0:T(4,128)(2,1)S(1)} fusion(f32[32,2,4,512]{3,2,1,0:T(4,128)} %param.3, f32[32,4]{1,0:T(8,128)S(1)} %add_rsqrt_fusion), kind=kLoop, calls=%fused_computation.7 | loop fusion | flops 262144 | bytes 786944 | tf_op jit(solution)/shard_map/convert_element_type | solution.py:31
  2.4 0.1 reshape.252
  2.5 0.1 copy.20
  2.7 3.0 %collective-permute-start = (bf16[4,8,32,128]{3,2,1,0:T(8,128)(2,1)S(1)}, bf16[4,8,32,128]{3,2,1,0:T(8,128)(2,1)S(1)}, u32[]{:S(2)}, u32[]{:S(2)}) collective-permute-start(bf16[4,8,32,128]{3,2,1,0:T(8,128)(2,1)S(1)} %bitcast.20), channel_id=1, source_target_pairs={{1,0},{0,1},{3,2},{2,3},{5,4},{4,5},{7,6},{6,7},{9,8},{8,9},{11,10... | collective-permute-start | bytes 786440 | tf_op jit(solution)/shard_map/ppermute | solution.py:25
  5.7 0.8 %concatenate.3.info = s32[2048]{0:T(1024)S(1)} concatenate(s32[1024]{0:T(1024)} %param.4, s32[9]{0:T(128)} %bitcast.39, s32[1]{0:T(128)} %bitcast.2, s32[1014]{0:T(1024)S(1)} %broadcast_in_dim.18), dimensions={0} | concatenate | bytes 16384 | tf_op jit(solution)/shard_map/concatenate | solution.py:231
  6.5 4.5 %collective-permute-start.1 = (bf16[4,8,32,128]{3,2,1,0:T(8,128)(2,1)S(1)}, bf16[4,8,32,128]{3,2,1,0:T(8,128)(2,1)S(1)}, u32[]{:S(2)}, u32[]{:S(2)}) collective-permute-start(bf16[4,8,32,128]{3,2,1,0:T(8,128)(2,1)S(1)} %bitcast.21), channel_id=1, source_target_pairs={{4,0},{6,2},{8,4},{10,6},{12,8},{14,10},{16,12},{18,14},{20,16},{2... | collective-permute-start | bytes 786440 | tf_op jit(solution)/shard_map/ppermute | solution.py:25
  11.0 0.4 collective-permute-start.2
  11.5 0.1 select_select_fusion
  11.5 0.1 fusion.13
  11.6 0.2 fusion.6
  11.9 0.1 fusion.16
  11.9 0.1 select_n.104
  12.0 0.1 multiply_add_fusion
  12.1 0.1 fusion.1.cos_tab
  12.3 0.1 fusion.sin_tab
  12.4 3.6 %shard_map.37.rest_2_ = bf16[1,9,1,64,32,400]{5,4,3,2,1,0:T(8,128)(2,1)} custom-call(s32[2048]{0:T(1024)S(1)} %concatenate.3.info, s32[16,128]{1,0:T(8,128)S(1)} %bitcast.29, bf16[2,512,128]{2,1,0:T(8,128)(2,1)S(1)} %fusion.1.cos_tab, bf16[2,512,128]{2,1,0:T(8,128)(2,1)S(1)} %fusion.sin_tab, bf16[4,8,32,128]{3,2,1,0:T(8,128)(2,1)S(1)} %bitcast.23, ...), custom_call_target="tpu_custom_call" | custom-call | flops 838860800 | bytes 1500000 | tf_op jit(solution)/shard_map/pallas_call | solution.py:197
  16.1 3.5 %shard_map.38.rest_5_ = bf16[1,9,1,64,32,400]{5,4,3,2,1,0:T(8,128)(2,1)} custom-call(s32[2048]{0:T(1024)S(1)} %concatenate.3.info, s32[16,128]{1,0:T(8,128)S(1)} %bitcast.30, bf16[2,512,128]{2,1,0:T(8,128)(2,1)S(1)} %fusion.1.cos_tab, bf16[2,512,128]{2,1,0:T(8,128)(2,1)S(1)} %fusion.sin_tab, ...), custom_call_target="tpu_custom_call", output_to_operand_aliasing={{}: (6, {})} | custom-call | flops 838860800 | bytes 1500000 | tf_op jit(solution)/shard_map/pallas_call | solution.py:197
  19.6 2.2 %collective-permute-done.2 = bf16[4,8,32,128]{3,2,1,0:T(8,128)(2,1)S(1)} collective-permute-done((bf16[4,8,32,128]{3,2,1,0:T(8,128)(2,1)S(1)}, bf16[4,8,32,128]{3,2,1,0:T(8,128)(2,1)S(1)}, u32[]{:S(2)}, u32[]{:S(2)}) %collective-permute-start.2) | collective-permute-done | bytes 262176 | tf_op jit(solution)/shard_map/ppermute | solution.py:25
  22.0 4.3 %collective-permute-start.5 = (bf16[2,4,8,32,128]{4,3,2,1,0:T(8,128)(2,1)S(1)}, bf16[2,4,8,32,128]{4,3,2,1,0:T(8,128)(2,1)S(1)}, u32[]{:S(2)}, u32[]{:S(2)}) collective-permute-start(bf16[2,4,8,32,128]{4,3,2,1,0:T(8,128)(2,1)S(1)} %pad_maximum_fusion.rest_3_), channel_id=1, source_target_pairs={{8,0},{10,2},{12,4},{14,6},{16,8},{18,10},{20,12},{22,14},{24,16},... | collective-permute-start | bytes 1572872 | tf_op jit(solution)/shard_map/ppermute | solution.py:25
  26.4 15.5 %shard_map.39.rest_5_ = bf16[1,9,1,64,32,400]{5,4,3,2,1,0:T(8,128)(2,1)} custom-call(s32[2048]{0:T(1024)S(1)} %concatenate.3.info, s32[16,128]{1,0:T(8,128)S(1)} %bitcast.31, bf16[2,512,128]{2,1,0:T(8,128)(2,1)S(1)} %fusion.1.cos_tab, bf16[2,512,128]{2,1,0:T(8,128)(2,1)S(1)} %fusion.sin_tab, ...), custom_call_target="tpu_custom_call", output_to_operand_aliasing={{}: (9, {})} | custom-call | flops 6710886400 | bytes 12000000 | tf_op jit(solution)/shard_map/pallas_call | solution.py:197
  41.9 0.2 collective-permute-start.6
  42.1 1.7 %collective-permute-done.6.rest_4_ = bf16[2,4,8,32,128]{4,3,2,1,0:T(8,128)(2,1)S(1)} collective-permute-done((bf16[2,4,8,32,128]{4,3,2,1,0:T(8,128)(2,1)S(1)}, bf16[2,4,8,32,128]{4,3,2,1,0:T(8,128)(2,1)S(1)}, u32[]{:S(2)}, u32[]{:S(2)}) %collective-permute-start.6) | collective-permute-done | bytes 524320 | tf_op jit(solution)/shard_map/ppermute | solution.py:234
  43.9 15.5 %shard_map.40 = bf16[1,9,1,64,32,400]{5,4,3,2,1,0:T(8,128)(2,1)} custom-call(s32[2048]{0:T(1024)S(1)} %concatenate.3.info, s32[16,128]{1,0:T(8,128)S(1)} %bitcast.32, bf16[2,512,128]{2,1,0:T(8,128)(2,1)S(1)} %fusion.1.cos_tab, bf16[2,512,128]{2,1,0:T(8,128)(2,1)S(1)} %fusion.sin_tab, ...), custom_call_target="tpu_custom_call", output_to_operand_aliasing={{}: (9, {})} | custom-call | flops 6710886400 | bytes 12000000 | tf_op jit(solution)/shard_map/pallas_call | solution.py:197
  (16 shorter events, 0.2 us)
Async XLA Ops:
  2.7 13.3 %collective-permute-start = (bf16[4,8,32,128]{3,2,1,0:T(8,128)(2,1)S(1)}, bf16[4,8,32,128]{3,2,1,0:T(8,128)(2,1)S(1)}, u32[]{:S(2)}, u32[]{:S(2)}) collective-permute-start(bf16[4,8,32,128]{3,2,1,0:T(8,128)(2,1)S(1)} %bitcast.20), channel_id=1, source_target_pairs={{1,0},{0,1},{3,2},{2,3},{5,4},{4,5},{7,6},{6,7},{9,8},{8,9},{11,10... | collective-permute-start | bytes 786440 | tf_op jit(solution)/shard_map/ppermute | solution.py:25
  6.5 13.2 %collective-permute-start.1 = (bf16[4,8,32,128]{3,2,1,0:T(8,128)(2,1)S(1)}, bf16[4,8,32,128]{3,2,1,0:T(8,128)(2,1)S(1)}, u32[]{:S(2)}, u32[]{:S(2)}) collective-permute-start(bf16[4,8,32,128]{3,2,1,0:T(8,128)(2,1)S(1)} %bitcast.21), channel_id=1, source_target_pairs={{4,0},{6,2},{8,4},{10,6},{12,8},{14,10},{16,12},{18,14},{20,16},{2... | collective-permute-start | bytes 786440 | tf_op jit(solution)/shard_map/ppermute | solution.py:25
  11.0 10.9 %collective-permute-start.2 = (bf16[4,8,32,128]{3,2,1,0:T(8,128)(2,1)S(1)}, bf16[4,8,32,128]{3,2,1,0:T(8,128)(2,1)S(1)}, u32[]{:S(2)}, u32[]{:S(2)}) collective-permute-start(bf16[4,8,32,128]{3,2,1,0:T(8,128)(2,1)S(1)} %bitcast.22), channel_id=1, source_target_pairs={{8,0},{10,2},{12,4},{14,6},{16,8},{18,10},{20,12},{22,14},{24,16},... | collective-permute-start | bytes 786440 | tf_op jit(solution)/shard_map/ppermute | solution.py:25
  16.0 5.9 %collective-permute-start.3 = (bf16[4,8,32,128]{3,2,1,0:T(8,128)(2,1)S(1)}, bf16[4,8,32,128]{3,2,1,0:T(8,128)(2,1)S(1)}, u32[]{:S(2)}, u32[]{:S(2)}) collective-permute-start(bf16[4,8,32,128]{3,2,1,0:T(8,128)(2,1)S(1)} %bitcast.25), channel_id=1, source_target_pairs={{2,0},{0,2},{6,4},{4,6},{10,8},{8,10},{14,12},{12,14},{18,16},{16,... | collective-permute-start | bytes 786440 | tf_op jit(solution)/shard_map/ppermute | solution.py:234
  21.9 4.4 %collective-permute-start.4 = (bf16[2,4,8,32,128]{4,3,2,1,0:T(8,128)(2,1)S(1)}, bf16[2,4,8,32,128]{4,3,2,1,0:T(8,128)(2,1)S(1)}, u32[]{:S(2)}, u32[]{:S(2)}) collective-permute-start(bf16[2,4,8,32,128]{4,3,2,1,0:T(8,128)(2,1)S(1)} %pad_maximum_fusion.rest_3_), channel_id=1, source_target_pairs={{2,0},{0,2},{6,4},{4,6},{10,8},{8,10},{14,12},{12,14},{18,16},{16,... | collective-permute-start | bytes 1572872 | tf_op jit(solution)/shard_map/ppermute | solution.py:234
  22.0 19.8 %collective-permute-start.5 = (bf16[2,4,8,32,128]{4,3,2,1,0:T(8,128)(2,1)S(1)}, bf16[2,4,8,32,128]{4,3,2,1,0:T(8,128)(2,1)S(1)}, u32[]{:S(2)}, u32[]{:S(2)}) collective-permute-start(bf16[2,4,8,32,128]{4,3,2,1,0:T(8,128)(2,1)S(1)} %pad_maximum_fusion.rest_3_), channel_id=1, source_target_pairs={{8,0},{10,2},{12,4},{14,6},{16,8},{18,10},{20,12},{22,14},{24,16},... | collective-permute-start | bytes 1572872 | tf_op jit(solution)/shard_map/ppermute | solution.py:25
  41.9 2.0 %collective-permute-start.6 = (bf16[2,4,8,32,128]{4,3,2,1,0:T(8,128)(2,1)S(1)}, bf16[2,4,8,32,128]{4,3,2,1,0:T(8,128)(2,1)S(1)}, u32[]{:S(2)}, u32[]{:S(2)}) collective-permute-start(bf16[2,4,8,32,128]{4,3,2,1,0:T(8,128)(2,1)S(1)} %collective-permute-done.5.rest_3_), channel_id=1, source_target_pairs={{2,0},{0,2},{6,4},{4,6},{10,8},{8,10},{14,12},{12,14},{18,16},{16,... | collective-permute-start | bytes 1572872 | tf_op jit(solution)/shard_map/ppermute | solution.py:234

commit v6 on v5

--- a/solution.py
+++ b/solution.py
@@ -235,8 +235,7 @@
 
     own = whiten_tiles(spectra)
     partner = passed_along(own, "grp", 1)
-    sent, info = lax.optimization_barrier((own, info))
-    near, far = passed_along(sent, "blk", -2), passed_along(sent, "blk", -4)
+    near, far = passed_along(own, "blk", -2), passed_along(own, "blk", -4)
     tables = half_lag_tables(freq_count, 1.0 / math.sqrt(2.0 * freq_count * seg_count))
 
     def stage(sources, arrays, picks, first, output, side=None):
@@ -244,9 +243,9 @@
 
     alone = [((0, None), (0, None))]
     output = stage([own], [own], alone, 0, None, 0)
-    last, partner, output = lax.optimization_barrier((own, partner, output))
+    output = stage([partner], [own], alone, 0, output, 1)
+    last, output = lax.optimization_barrier((own, output))
     swapped = other_core(last)
-    output = stage([partner], [own], alone, 0, output, 1)
     for first in range(1, step_count, 4):
         if first == 1:
             near, far, swapped, output = lax.optimization_barrier((near, far, swapped, output))

time: 59.6 us -> 58.8 us (0.987)
  waiting for transfers between devices: 4.01 us -> 3.27 us
    ppermute x4, waiting for transfers between devices: 2.25 us -> 1.46 us  [passed_along(): return lax.ppermute(block, axis, route)]
  transfers between devices with their start and end apart: 7 -> 7, of which waited for: 2 -> 3; matrix products, arithmetic and copies ran while one was open for 3% -> 3% of each run, Pallas kernels for 38% -> 39%
where the time goes in v6:
time: 58.8 us; the launch traced here: 58.6 us
  Pallas kernels  38.1 us (65%)
  starting transfers between devices  12.7 us (22%)
  other arithmetic  3.34 us (6%)
  waiting for transfers between devices  3.27 us (6%)
  local copies, waits for them, and re-layouts  1.06 us (2%)
    pallas_call x4, Pallas kernels, correlate(): pl.pallas_call(functools.partial(correlate_kernel, first=first, picks=pic...  38.1 us
    ppermute x4, starting transfers between devices, passed_along(): return lax.ppermute(block, axis, route)  12.2 us
    ppermute x3, waiting for transfers between devices, other_core(): return lax.ppermute(block, 'blk', [(i ^ 1, i) for i in range(blk_count)])  1.82 us
    ppermute x4, waiting for transfers between devices, passed_along(): return lax.ppermute(block, axis, route)  1.46 us
    reduce_sum x1, other arithmetic, whiten(): seg_power = jnp.mean(spectra * spectra, axis=(1, 3))  1.22 us
    convert_element_type x1, other arithmetic, whiten(): whitened = whitened.astype(jnp.bfloat16)  1.2 us
  transfers between devices with their start and end apart: 7, of which 3 were waited for; matrix products, arithmetic and copies ran while one was open for 3% of the time, Pallas kernels for 39%

profile of v6, /device:TPU:0, one launch (start us, length us, event | category | flops | bytes accessed | tf_op | source)
XLA Modules:
  0.0 58.6 jit_solution(17020426159087336206)
XLA Ops:
  0.0 1.2 %multiply_reduce_fusion = f32[32,4]{1,0:T(8,128)S(1)} fusion(f32[32,2,4,512]{3,2,1,0:T(4,128)} %param.3), kind=kLoop, calls=%fused_computation.6 | loop fusion | flops 262016 | bytes 524800 | tf_op jit(solution)/shard_map/reduce_sum | solution.py:29
  1.2 1.2 %multiply_convert_fusion = bf16[32,2,4,512]{3,2,1,0:T(4,128)(2,1)S(1)} fusion(f32[32,2,4,512]{3,2,1,0:T(4,128)} %param.3, f32[32,4]{1,0:T(8,128)S(1)} %add_rsqrt_fusion), kind=kLoop, calls=%fused_computation.5 | loop fusion | flops 262144 | bytes 786944 | tf_op jit(solution)/shard_map/convert_element_type | solution.py:31
  2.4 0.1 reshape.252
  2.5 0.1 copy.20
  2.7 3.0 %collective-permute-start = (bf16[4,8,32,128]{3,2,1,0:T(8,128)(2,1)S(1)}, bf16[4,8,32,128]{3,2,1,0:T(8,128)(2,1)S(1)}, u32[]{:S(2)}, u32[]{:S(2)}) collective-permute-start(bf16[4,8,32,128]{3,2,1,0:T(8,128)(2,1)S(1)} %bitcast.20), channel_id=1, source_target_pairs={{1,0},{0,1},{3,2},{2,3},{5,4},{4,5},{7,6},{6,7},{9,8},{8,9},{11,10... | collective-permute-start | bytes 786440 | tf_op jit(solution)/shard_map/ppermute | solution.py:25
  5.7 4.5 %collective-permute-start.1 = (bf16[4,8,32,128]{3,2,1,0:T(8,128)(2,1)S(1)}, bf16[4,8,32,128]{3,2,1,0:T(8,128)(2,1)S(1)}, u32[]{:S(2)}, u32[]{:S(2)}) collective-permute-start(bf16[4,8,32,128]{3,2,1,0:T(8,128)(2,1)S(1)} %bitcast.21), channel_id=1, source_target_pairs={{4,0},{6,2},{8,4},{10,6},{12,8},{14,10},{16,12},{18,14},{20,16},{2... | collective-permute-start | bytes 786440 | tf_op jit(solution)/shard_map/ppermute | solution.py:25
  10.2 0.4 collective-permute-start.2
  10.7 0.1 select_select_fusion
  10.8 0.1 fusion.13
  10.9 0.2 fusion.6
  11.2 0.1 select_n.104
  11.3 0.1 multiply_add_fusion
  11.4 0.1 fusion.1.cos_tab
  11.5 0.8 %concatenate.3.info = s32[2048]{0:T(1024)S(1)} concatenate(s32[1024]{0:T(1024)} %param.4, s32[9]{0:T(128)} %bitcast.39, s32[1]{0:T(128)} %bitcast.1, s32[1014]{0:T(1024)S(1)} %broadcast_in_dim.18), dimensions={0} | concatenate | bytes 16384 | tf_op jit(solution)/shard_map/concatenate | solution.py:231
  12.3 0.1 fusion.sin_tab
  12.4 3.6 %shard_map.37.rest_2_ = bf16[1,9,1,64,32,400]{5,4,3,2,1,0:T(8,128)(2,1)} custom-call(s32[2048]{0:T(1024)S(1)} %concatenate.3.info, s32[16,128]{1,0:T(8,128)S(1)} %bitcast.29, bf16[2,512,128]{2,1,0:T(8,128)(2,1)S(1)} %fusion.1.cos_tab, bf16[2,512,128]{2,1,0:T(8,128)(2,1)S(1)} %fusion.sin_tab, bf16[4,8,32,128]{3,2,1,0:T(8,128)(2,1)S(1)} %bitcast.23, ...), custom_call_target="tpu_custom_call" | custom-call | flops 838860800 | bytes 1500000 | tf_op jit(solution)/shard_map/pallas_call | solution.py:197
  16.0 3.5 %shard_map.38.rest_5_ = bf16[1,9,1,64,32,400]{5,4,3,2,1,0:T(8,128)(2,1)} custom-call(s32[2048]{0:T(1024)S(1)} %concatenate.3.info, s32[16,128]{1,0:T(8,128)S(1)} %bitcast.30, bf16[2,512,128]{2,1,0:T(8,128)(2,1)S(1)} %fusion.1.cos_tab, bf16[2,512,128]{2,1,0:T(8,128)(2,1)S(1)} %fusion.sin_tab, ...), custom_call_target="tpu_custom_call", output_to_operand_aliasing={{}: (6, {})} | custom-call | flops 838860800 | bytes 1500000 | tf_op jit(solution)/shard_map/pallas_call | solution.py:197
  19.7 1.5 %collective-permute-done.2 = bf16[4,8,32,128]{3,2,1,0:T(8,128)(2,1)S(1)} collective-permute-done((bf16[4,8,32,128]{3,2,1,0:T(8,128)(2,1)S(1)}, bf16[4,8,32,128]{3,2,1,0:T(8,128)(2,1)S(1)}, u32[]{:S(2)}, u32[]{:S(2)}) %collective-permute-start.2) | collective-permute-done | bytes 262176 | tf_op jit(solution)/shard_map/ppermute | solution.py:25
  21.2 0.2 collective-permute-start.4
  21.4 4.2 %collective-permute-start.5 = (bf16[2,4,8,32,128]{4,3,2,1,0:T(8,128)(2,1)S(1)}, bf16[2,4,8,32,128]{4,3,2,1,0:T(8,128)(2,1)S(1)}, u32[]{:S(2)}, u32[]{:S(2)}) collective-permute-start(bf16[2,4,8,32,128]{4,3,2,1,0:T(8,128)(2,1)S(1)} %pad_maximum_fusion.rest_3_), channel_id=1, source_target_pairs={{8,0},{10,2},{12,4},{14,6},{16,8},{18,10},{20,12},{22,14},{24,16},... | collective-permute-start | bytes 1572872 | tf_op jit(solution)/shard_map/ppermute | solution.py:25
  25.6 15.5 %shard_map.39.rest_5_ = bf16[1,9,1,64,32,400]{5,4,3,2,1,0:T(8,128)(2,1)} custom-call(s32[2048]{0:T(1024)S(1)} %concatenate.3.info, s32[16,128]{1,0:T(8,128)S(1)} %bitcast.31, bf16[2,512,128]{2,1,0:T(8,128)(2,1)S(1)} %fusion.1.cos_tab, bf16[2,512,128]{2,1,0:T(8,128)(2,1)S(1)} %fusion.sin_tab, ...), custom_call_target="tpu_custom_call", output_to_operand_aliasing={{}: (9, {})} | custom-call | flops 6710886400 | bytes 12000000 | tf_op jit(solution)/shard_map/pallas_call | solution.py:197
  41.1 0.2 collective-permute-start.6
  41.4 1.8 %collective-permute-done.6.rest_4_ = bf16[2,4,8,32,128]{4,3,2,1,0:T(8,128)(2,1)S(1)} collective-permute-done((bf16[2,4,8,32,128]{4,3,2,1,0:T(8,128)(2,1)S(1)}, bf16[2,4,8,32,128]{4,3,2,1,0:T(8,128)(2,1)S(1)}, u32[]{:S(2)}, u32[]{:S(2)}) %collective-permute-start.6) | collective-permute-done | bytes 524320 | tf_op jit(solution)/shard_map/ppermute | solution.py:234
  43.1 15.5 %shard_map.40 = bf16[1,9,1,64,32,400]{5,4,3,2,1,0:T(8,128)(2,1)} custom-call(s32[2048]{0:T(1024)S(1)} %concatenate.3.info, s32[16,128]{1,0:T(8,128)S(1)} %bitcast.32, bf16[2,512,128]{2,1,0:T(8,128)(2,1)S(1)} %fusion.1.cos_tab, bf16[2,512,128]{2,1,0:T(8,128)(2,1)S(1)} %fusion.sin_tab, ...), custom_call_target="tpu_custom_call", output_to_operand_aliasing={{}: (9, {})} | custom-call | flops 6710886400 | bytes 12000000 | tf_op jit(solution)/shard_map/pallas_call | solution.py:197
  (16 shorter events, 0.3 us)
Async XLA Ops:
  2.7 13.4 %collective-permute-start = (bf16[4,8,32,128]{3,2,1,0:T(8,128)(2,1)S(1)}, bf16[4,8,32,128]{3,2,1,0:T(8,128)(2,1)S(1)}, u32[]{:S(2)}, u32[]{:S(2)}) collective-permute-start(bf16[4,8,32,128]{3,2,1,0:T(8,128)(2,1)S(1)} %bitcast.20), channel_id=1, source_target_pairs={{1,0},{0,1},{3,2},{2,3},{5,4},{4,5},{7,6},{6,7},{9,8},{8,9},{11,10... | collective-permute-start | bytes 786440 | tf_op jit(solution)/shard_map/ppermute | solution.py:25
  5.7 14.0 %collective-permute-start.1 = (bf16[4,8,32,128]{3,2,1,0:T(8,128)(2,1)S(1)}, bf16[4,8,32,128]{3,2,1,0:T(8,128)(2,1)S(1)}, u32[]{:S(2)}, u32[]{:S(2)}) collective-permute-start(bf16[4,8,32,128]{3,2,1,0:T(8,128)(2,1)S(1)} %bitcast.21), channel_id=1, source_target_pairs={{4,0},{6,2},{8,4},{10,6},{12,8},{14,10},{16,12},{18,14},{20,16},{2... | collective-permute-start | bytes 786440 | tf_op jit(solution)/shard_map/ppermute | solution.py:25
  10.2 10.9 %collective-permute-start.2 = (bf16[4,8,32,128]{3,2,1,0:T(8,128)(2,1)S(1)}, bf16[4,8,32,128]{3,2,1,0:T(8,128)(2,1)S(1)}, u32[]{:S(2)}, u32[]{:S(2)}) collective-permute-start(bf16[4,8,32,128]{3,2,1,0:T(8,128)(2,1)S(1)} %bitcast.22), channel_id=1, source_target_pairs={{8,0},{10,2},{12,4},{14,6},{16,8},{18,10},{20,12},{22,14},{24,16},... | collective-permute-start | bytes 786440 | tf_op jit(solution)/shard_map/ppermute | solution.py:25
  19.6 1.6 %collective-permute-start.3 = (bf16[4,8,32,128]{3,2,1,0:T(8,128)(2,1)S(1)}, bf16[4,8,32,128]{3,2,1,0:T(8,128)(2,1)S(1)}, u32[]{:S(2)}, u32[]{:S(2)}) collective-permute-start(bf16[4,8,32,128]{3,2,1,0:T(8,128)(2,1)S(1)} %bitcast.26), channel_id=1, source_target_pairs={{2,0},{0,2},{6,4},{4,6},{10,8},{8,10},{14,12},{12,14},{18,16},{16,... | collective-permute-start | bytes 786440 | tf_op jit(solution)/shard_map/ppermute | solution.py:234
  21.2 4.4 %collective-permute-start.4 = (bf16[2,4,8,32,128]{4,3,2,1,0:T(8,128)(2,1)S(1)}, bf16[2,4,8,32,128]{4,3,2,1,0:T(8,128)(2,1)S(1)}, u32[]{:S(2)}, u32[]{:S(2)}) collective-permute-start(bf16[2,4,8,32,128]{4,3,2,1,0:T(8,128)(2,1)S(1)} %pad_maximum_fusion.rest_3_), channel_id=1, source_target_pairs={{2,0},{0,2},{6,4},{4,6},{10,8},{8,10},{14,12},{12,14},{18,16},{16,... | collective-permute-start | bytes 1572872 | tf_op jit(solution)/shard_map/ppermute | solution.py:234
  21.4 19.7 %collective-permute-start.5 = (bf16[2,4,8,32,128]{4,3,2,1,0:T(8,128)(2,1)S(1)}, bf16[2,4,8,32,128]{4,3,2,1,0:T(8,128)(2,1)S(1)}, u32[]{:S(2)}, u32[]{:S(2)}) collective-permute-start(bf16[2,4,8,32,128]{4,3,2,1,0:T(8,128)(2,1)S(1)} %pad_maximum_fusion.rest_3_), channel_id=1, source_target_pairs={{8,0},{10,2},{12,4},{14,6},{16,8},{18,10},{20,12},{22,14},{24,16},... | collective-permute-start | bytes 1572872 | tf_op jit(solution)/shard_map/ppermute | solution.py:25
  41.1 2.0 %collective-permute-start.6 = (bf16[2,4,8,32,128]{4,3,2,1,0:T(8,128)(2,1)S(1)}, bf16[2,4,8,32,128]{4,3,2,1,0:T(8,128)(2,1)S(1)}, u32[]{:S(2)}, u32[]{:S(2)}) collective-permute-start(bf16[2,4,8,32,128]{4,3,2,1,0:T(8,128)(2,1)S(1)} %collective-permute-done.5.rest_3_), channel_id=1, source_target_pairs={{2,0},{0,2},{6,4},{4,6},{10,8},{8,10},{14,12},{12,14},{18,16},{16,... | collective-permute-start | bytes 1572872 | tf_op jit(solution)/shard_map/ppermute | solution.py:234

commit v7 on v6

--- a/solution.py
+++ b/solution.py
@@ -216,10 +216,22 @@
     )(info, ids, *tables, *sources, *arrays, *kept)
 
 
+def whiten_kernel(spectra, out):
+    channels, halves, seg_count, freq_count = spectra.shape
+    for s in range(seg_count):
+        lines = [spectra[:, p, s, :] for p in range(halves)]
+        power = sum(jnp.sum(line * line, axis=1, keepdims=True) for line in lines)
+        level = lax.rsqrt(power / (halves * freq_count) + 1e-06)
+        for p, line in enumerate(lines):
+            for q in range(freq_count // LANES):
+                tile = line[:, q * LANES:(q + 1) * LANES] * level
+                out[q, p * seg_count + s] = tile.astype(jnp.bfloat16)
+
+
 def whiten_tiles(spectra):
-    whitened = whiten(spectra)
-    channels, parts, freq_count = whitened.shape
-    return jnp.transpose(whitened.reshape(channels, parts, freq_count // LANES, LANES), (2, 1, 0, 3))
+    channels, halves, seg_count, freq_count = spectra.shape
+    shape = (freq_count // LANES, halves * seg_count, channels, LANES)
+    return pl.pallas_call(whiten_kernel, out_shape=jax.ShapeDtypeStruct(shape, jnp.bfloat16))(spectra)
 
 
 def on_device_fused(spectra, channel_ids, plan):

time: 58.8 us -> 58.4 us (level)
  other arithmetic: 3.34 us -> 0.91 us
  Pallas kernels: 38.1 us -> 40.2 us
  starting transfers between devices: 12.7 us -> 11.9 us
  local copies, waits for them, and re-layouts: 1.06 us -> 1.8 us
    pallas_call x0 -> x1, Pallas kernels: none -> 2.04 us  [whiten_tiles(): pl.pallas_call(whiten_kernel, out_shape=jax.ShapeDtypeStruct(shape, jnp.b...]
    reduce_sum x1 -> x0, other arithmetic: 1.22 us -> none  [whiten(): seg_power = jnp.mean(spectra * spectra, axis=(1, 3))]
    convert_element_type x1 -> x0, other arithmetic: 1.2 us -> none  [whiten(): whitened = whitened.astype(jnp.bfloat16)]
    unnamed x0 -> x4, local copies, waits for them, and re-layouts: none -> 0.95 us
    ppermute x4, starting transfers between devices: 12.2 us -> 11.3 us  [passed_along(): return lax.ppermute(block, axis, route)]
    ppermute x4, waiting for transfers between devices: 1.46 us -> 0.82 us  [passed_along(): return lax.ppermute(block, axis, route)]
    ppermute x3, waiting for transfers between devices: 1.82 us -> 2.45 us  [other_core(): return lax.ppermute(block, 'blk', [(i ^ 1, i) for i in range(blk_count)])]
where the time goes in v7:
time: 58.4 us; the launch traced here: 58.1 us
  Pallas kernels  40.2 us (69%)
  starting transfers between devices  11.9 us (20%)
  waiting for transfers between devices  3.27 us (6%)
  local copies, waits for them, and re-layouts  1.8 us (3%)
  other arithmetic  0.91 us (2%)
    pallas_call x4, Pallas kernels, correlate(): pl.pallas_call(functools.partial(correlate_kernel, first=first, picks=pic...  38.1 us
    ppermute x4, starting transfers between devices, passed_along(): return lax.ppermute(block, axis, route)  11.3 us
    ppermute x3, waiting for transfers between devices, other_core(): return lax.ppermute(block, 'blk', [(i ^ 1, i) for i in range(blk_count)])  2.45 us
    pallas_call x1, Pallas kernels, whiten_tiles(): pl.pallas_call(whiten_kernel, out_shape=jax.ShapeDtypeStruct(shape, jnp.b...  2.04 us
  transfers between devices with their start and end apart: 7, of which 3 were waited for; matrix products, arithmetic and copies ran while one was open for 3% of the time, Pallas kernels for 39%

profile of v7, /device:TPU:0, one launch (start us, length us, event | category | flops | bytes accessed | tf_op | source)
XLA Modules:
  0.0 58.1 jit_solution(6712673781125013081)
XLA Ops:
  0.0 2.0 %shard_map.37.rest_0_.rest_1_ = bf16[4,8,32,128]{3,2,1,0:T(8,128)(2,1)} custom-call(f32[32,2,4,512]{3,2,1,0:T(4,128)} %spectra.1), custom_call_target="tpu_custom_call" | custom-call | tf_op jit(solution)/shard_map/pallas_call | solution.py:234
  2.0 3.0 %collective-permute-start = (bf16[4,8,32,128]{3,2,1,0:T(8,128)(2,1)}, bf16[4,8,32,128]{3,2,1,0:T(8,128)(2,1)S(1)}, u32[]{:S(2)}, u32[]{:S(2)}) collective-permute-start(bf16[4,8,32,128]{3,2,1,0:T(8,128)(2,1)} %shard_map.37.rest_0_.rest_1_), channel_id=1, source_target_pairs={{1,0},{0,1},{3,2},{2,3},{5,4},{4,5},{7,6},{6,7},{9,8},{8,9},{11,10... | collective-permute-start | bytes 786440 | tf_op jit(solution)/shard_map/ppermute | solution.py:25
  5.0 4.5 %collective-permute-start.1 = (bf16[4,8,32,128]{3,2,1,0:T(8,128)(2,1)}, bf16[4,8,32,128]{3,2,1,0:T(8,128)(2,1)S(1)}, u32[]{:S(2)}, u32[]{:S(2)}) collective-permute-start(bf16[4,8,32,128]{3,2,1,0:T(8,128)(2,1)} %shard_map.37.rest_0_.rest_1_), channel_id=1, source_target_pairs={{4,0},{6,2},{8,4},{10,6},{12,8},{14,10},{16,12},{18,14},{20,16},{2... | collective-permute-start | bytes 786440 | tf_op jit(solution)/shard_map/ppermute | solution.py:25
  9.5 0.4 collective-permute-start.2
  10.0 0.1 select_select_fusion
  10.1 0.1 fusion.13
  10.2 0.2 fusion.6
  10.4 0.1 fusion.16
  10.5 0.1 select_n.104
  10.6 0.1 multiply_add_fusion
  10.7 0.1 fusion.1.cos_tab
  10.9 0.8 %concatenate.3.info = s32[2048]{0:T(1024)S(1)} concatenate(s32[1024]{0:T(1024)} %param.4, s32[9]{0:T(128)} %bitcast.27, s32[1]{0:T(128)} %bitcast.1, s32[1014]{0:T(1024)S(1)} %broadcast_in_dim.17), dimensions={0} | concatenate | bytes 16384 | tf_op jit(solution)/shard_map/concatenate | solution.py:243
  11.6 0.1 fusion.sin_tab
  11.8 0.9 %copy-done = bf16[4,8,32,128]{3,2,1,0:T(8,128)(2,1)S(1)} copy-done((bf16[4,8,32,128]{3,2,1,0:T(8,128)(2,1)S(1)}, bf16[4,8,32,128]{3,2,1,0:T(8,128)(2,1)}, u32[]{:S(2)}) %copy-start) | copy-done | bytes 262168
  12.7 3.6 %shard_map.38.rest_2_ = bf16[1,9,1,64,32,400]{5,4,3,2,1,0:T(8,128)(2,1)} custom-call(s32[2048]{0:T(1024)S(1)} %concatenate.3.info, s32[16,128]{1,0:T(8,128)S(1)} %bitcast.17, bf16[2,512,128]{2,1,0:T(8,128)(2,1)S(1)} %fusion.1.cos_tab, bf16[2,512,128]{2,1,0:T(8,128)(2,1)S(1)} %fusion.sin_tab, bf16[4,8,32,128]{3,2,1,0:T(8,128)(2,1)S(1)} %copy-done, ...), custom_call_target="tpu_custom_call" | custom-call | flops 838860800 | bytes 1500000 | tf_op jit(solution)/shard_map/pallas_call | solution.py:197
  16.3 3.5 %shard_map.39.rest_5_ = bf16[1,9,1,64,32,400]{5,4,3,2,1,0:T(8,128)(2,1)} custom-call(s32[2048]{0:T(1024)S(1)} %concatenate.3.info, s32[16,128]{1,0:T(8,128)S(1)} %bitcast.18, bf16[2,512,128]{2,1,0:T(8,128)(2,1)S(1)} %fusion.1.cos_tab, bf16[2,512,128]{2,1,0:T(8,128)(2,1)S(1)} %fusion.sin_tab, ...), custom_call_target="tpu_custom_call", output_to_operand_aliasing={{}: (6, {})} | custom-call | flops 838860800 | bytes 1500000 | tf_op jit(solution)/shard_map/pallas_call | solution.py:197
  20.0 0.8 %collective-permute-done.2 = bf16[4,8,32,128]{3,2,1,0:T(8,128)(2,1)S(1)} collective-permute-done((bf16[4,8,32,128]{3,2,1,0:T(8,128)(2,1)}, bf16[4,8,32,128]{3,2,1,0:T(8,128)(2,1)S(1)}, u32[]{:S(2)}, u32[]{:S(2)}) %collective-permute-start.2) | collective-permute-done | bytes 262176 | tf_op jit(solution)/shard_map/ppermute | solution.py:25
  20.8 0.7 %collective-permute-done.3.rest_2_ = bf16[4,8,32,128]{3,2,1,0:T(8,128)(2,1)S(1)} collective-permute-done((bf16[4,8,32,128]{3,2,1,0:T(8,128)(2,1)S(1)}, bf16[4,8,32,128]{3,2,1,0:T(8,128)(2,1)S(1)}, u32[]{:S(2)}, u32[]{:S(2)}) %collective-permute-start.3) | collective-permute-done | bytes 262176 | tf_op jit(solution)/shard_map/ppermute | solution.py:246
  21.5 0.2 collective-permute-start.4
  21.7 3.4 %collective-permute-start.5 = (bf16[2,4,8,32,128]{4,3,2,1,0:T(8,128)(2,1)S(1)}, bf16[2,4,8,32,128]{4,3,2,1,0:T(8,128)(2,1)S(1)}, u32[]{:S(2)}, u32[]{:S(2)}) collective-permute-start(bf16[2,4,8,32,128]{4,3,2,1,0:T(8,128)(2,1)S(1)} %pad_maximum_fusion.rest_3_), channel_id=1, source_target_pairs={{8,0},{10,2},{12,4},{14,6},{16,8},{18,10},{20,12},{22,14},{24,16},... | collective-permute-start | bytes 1572872 | tf_op jit(solution)/shard_map/ppermute | solution.py:25
  25.1 15.5 %shard_map.40.rest_5_ = bf16[1,9,1,64,32,400]{5,4,3,2,1,0:T(8,128)(2,1)} custom-call(s32[2048]{0:T(1024)S(1)} %concatenate.3.info, s32[16,128]{1,0:T(8,128)S(1)} %bitcast.19, bf16[2,512,128]{2,1,0:T(8,128)(2,1)S(1)} %fusion.1.cos_tab, bf16[2,512,128]{2,1,0:T(8,128)(2,1)S(1)} %fusion.sin_tab, ...), custom_call_target="tpu_custom_call", output_to_operand_aliasing={{}: (9, {})} | custom-call | flops 6710886400 | bytes 12000000 | tf_op jit(solution)/shard_map/pallas_call | solution.py:197
  40.7 0.2 collective-permute-start.6
  40.9 1.7 %collective-permute-done.6.rest_4_ = bf16[2,4,8,32,128]{4,3,2,1,0:T(8,128)(2,1)S(1)} collective-permute-done((bf16[2,4,8,32,128]{4,3,2,1,0:T(8,128)(2,1)S(1)}, bf16[2,4,8,32,128]{4,3,2,1,0:T(8,128)(2,1)S(1)}, u32[]{:S(2)}, u32[]{:S(2)}) %collective-permute-start.6) | collective-permute-done | bytes 524320 | tf_op jit(solution)/shard_map/ppermute | solution.py:246
  42.6 15.5 %shard_map.41 = bf16[1,9,1,64,32,400]{5,4,3,2,1,0:T(8,128)(2,1)} custom-call(s32[2048]{0:T(1024)S(1)} %concatenate.3.info, s32[16,128]{1,0:T(8,128)S(1)} %bitcast.20, bf16[2,512,128]{2,1,0:T(8,128)(2,1)S(1)} %fusion.1.cos_tab, bf16[2,512,128]{2,1,0:T(8,128)(2,1)S(1)} %fusion.sin_tab, ...), custom_call_target="tpu_custom_call", output_to_operand_aliasing={{}: (9, {})} | custom-call | flops 6710886400 | bytes 12000000 | tf_op jit(solution)/shard_map/pallas_call | solution.py:197
  (16 shorter events, 0.2 us)
Async XLA Ops:
  2.0 14.3 %copy-start.1 = (bf16[4,8,32,128]{3,2,1,0:T(8,128)(2,1)S(1)}, bf16[4,8,32,128]{3,2,1,0:T(8,128)(2,1)}, u32[]{:S(2)}) copy-start(bf16[4,8,32,128]{3,2,1,0:T(8,128)(2,1)} %shard_map.37.rest_0_.rest_1_) | copy-start | bytes 786436
  2.0 14.2 %collective-permute-start = (bf16[4,8,32,128]{3,2,1,0:T(8,128)(2,1)}, bf16[4,8,32,128]{3,2,1,0:T(8,128)(2,1)S(1)}, u32[]{:S(2)}, u32[]{:S(2)}) collective-permute-start(bf16[4,8,32,128]{3,2,1,0:T(8,128)(2,1)} %shard_map.37.rest_0_.rest_1_), channel_id=1, source_target_pairs={{1,0},{0,1},{3,2},{2,3},{5,4},{4,5},{7,6},{6,7},{9,8},{8,9},{11,10... | collective-permute-start | bytes 786440 | tf_op jit(solution)/shard_map/ppermute | solution.py:25
  5.0 14.9 %collective-permute-start.1 = (bf16[4,8,32,128]{3,2,1,0:T(8,128)(2,1)}, bf16[4,8,32,128]{3,2,1,0:T(8,128)(2,1)S(1)}, u32[]{:S(2)}, u32[]{:S(2)}) collective-permute-start(bf16[4,8,32,128]{3,2,1,0:T(8,128)(2,1)} %shard_map.37.rest_0_.rest_1_), channel_id=1, source_target_pairs={{4,0},{6,2},{8,4},{10,6},{12,8},{14,10},{16,12},{18,14},{20,16},{2... | collective-permute-start | bytes 786440 | tf_op jit(solution)/shard_map/ppermute | solution.py:25
  9.5 11.2 %collective-permute-start.2 = (bf16[4,8,32,128]{3,2,1,0:T(8,128)(2,1)}, bf16[4,8,32,128]{3,2,1,0:T(8,128)(2,1)S(1)}, u32[]{:S(2)}, u32[]{:S(2)}) collective-permute-start(bf16[4,8,32,128]{3,2,1,0:T(8,128)(2,1)} %shard_map.37.rest_0_.rest_1_), channel_id=1, source_target_pairs={{8,0},{10,2},{12,4},{14,6},{16,8},{18,10},{20,12},{22,14},{24,16},... | collective-permute-start | bytes 786440 | tf_op jit(solution)/shard_map/ppermute | solution.py:25
  11.8 1.0 %copy-start = (bf16[4,8,32,128]{3,2,1,0:T(8,128)(2,1)S(1)}, bf16[4,8,32,128]{3,2,1,0:T(8,128)(2,1)}, u32[]{:S(2)}) copy-start(bf16[4,8,32,128]{3,2,1,0:T(8,128)(2,1)} %shard_map.37.rest_0_.rest_1_) | copy-start | bytes 786436
  19.9 1.6 %collective-permute-start.3 = (bf16[4,8,32,128]{3,2,1,0:T(8,128)(2,1)S(1)}, bf16[4,8,32,128]{3,2,1,0:T(8,128)(2,1)S(1)}, u32[]{:S(2)}, u32[]{:S(2)}) collective-permute-start(bf16[4,8,32,128]{3,2,1,0:T(8,128)(2,1)S(1)} %copy-done.1), channel_id=1, source_target_pairs={{2,0},{0,2},{6,4},{4,6},{10,8},{8,10},{14,12},{12,14},{18,16},{16,... | collective-permute-start | bytes 786440 | tf_op jit(solution)/shard_map/ppermute | solution.py:246
  21.5 3.6 %collective-permute-start.4 = (bf16[2,4,8,32,128]{4,3,2,1,0:T(8,128)(2,1)S(1)}, bf16[2,4,8,32,128]{4,3,2,1,0:T(8,128)(2,1)S(1)}, u32[]{:S(2)}, u32[]{:S(2)}) collective-permute-start(bf16[2,4,8,32,128]{4,3,2,1,0:T(8,128)(2,1)S(1)} %pad_maximum_fusion.rest_3_), channel_id=1, source_target_pairs={{2,0},{0,2},{6,4},{4,6},{10,8},{8,10},{14,12},{12,14},{18,16},{16,... | collective-permute-start | bytes 1572872 | tf_op jit(solution)/shard_map/ppermute | solution.py:246
  21.7 18.9 %collective-permute-start.5 = (bf16[2,4,8,32,128]{4,3,2,1,0:T(8,128)(2,1)S(1)}, bf16[2,4,8,32,128]{4,3,2,1,0:T(8,128)(2,1)S(1)}, u32[]{:S(2)}, u32[]{:S(2)}) collective-permute-start(bf16[2,4,8,32,128]{4,3,2,1,0:T(8,128)(2,1)S(1)} %pad_maximum_fusion.rest_3_), channel_id=1, source_target_pairs={{8,0},{10,2},{12,4},{14,6},{16,8},{18,10},{20,12},{22,14},{24,16},... | collective-permute-start | bytes 1572872 | tf_op jit(solution)/shard_map/ppermute | solution.py:25
  40.7 2.0 %collective-permute-start.6 = (bf16[2,4,8,32,128]{4,3,2,1,0:T(8,128)(2,1)S(1)}, bf16[2,4,8,32,128]{4,3,2,1,0:T(8,128)(2,1)S(1)}, u32[]{:S(2)}, u32[]{:S(2)}) collective-permute-start(bf16[2,4,8,32,128]{4,3,2,1,0:T(8,128)(2,1)S(1)} %collective-permute-done.5.rest_3_), channel_id=1, source_target_pairs={{2,0},{0,2},{6,4},{4,6},{10,8},{8,10},{14,12},{12,14},{18,16},{16,... | collective-permute-start | bytes 1572872 | tf_op jit(solution)/shard_map/ppermute | solution.py:246

commit v8 on v7

--- a/solution.py
+++ b/solution.py
@@ -231,7 +231,11 @@
 def whiten_tiles(spectra):
     channels, halves, seg_count, freq_count = spectra.shape
     shape = (freq_count // LANES, halves * seg_count, channels, LANES)
-    return pl.pallas_call(whiten_kernel, out_shape=jax.ShapeDtypeStruct(shape, jnp.bfloat16))(spectra)
+    return pl.pallas_call(
+        whiten_kernel,
+        out_specs=pl.BlockSpec(memory_space=pltpu.VMEM),
+        out_shape=pltpu.VMEM(shape, jnp.bfloat16),
+    )(spectra)
 
 
 def on_device_fused(spectra, channel_ids, plan):

time: 58.4 us -> 57.3 us (0.981)
  local copies, waits for them, and re-layouts: 1.8 us -> 0.85 us
  Pallas kernels: 40.2 us -> 39.3 us
  starting transfers between devices: 11.9 us -> 12.7 us
    unnamed x4 -> x0, local copies, waits for them, and re-layouts: 0.95 us -> none
    ppermute x4, starting transfers between devices: 11.3 us -> 12.2 us  [passed_along(): return lax.ppermute(block, axis, route)]
    pallas_call x1, Pallas kernels: 2.04 us -> 1.33 us  [whiten_tiles(): pl.pallas_call(whiten_kernel, out_specs=pl.BlockSpec(memory_space=pltpu.V...]
    ppermute x4, waiting for transfers between devices: 0.82 us -> 1.49 us  [passed_along(): return lax.ppermute(block, axis, route)]
    ppermute x3, waiting for transfers between devices: 2.45 us -> 1.78 us  [other_core(): return lax.ppermute(block, 'blk', [(i ^ 1, i) for i in range(blk_count)])]
  transfers between devices with their start and end apart: 7 -> 7, of which waited for: 3 -> 2; matrix products, arithmetic and copies ran while one was open for 3% -> 3% of each run, Pallas kernels for 39% -> 39%
where the time goes in v8:
time: 57.3 us; the launch traced here: 57.2 us
  Pallas kernels  39.3 us (69%)
  starting transfers between devices  12.7 us (22%)
  waiting for transfers between devices  3.27 us (6%)
  other arithmetic  0.91 us (2%)
  local copies, waits for them, and re-layouts  0.85 us (1%)
    pallas_call x4, Pallas kernels, correlate(): pl.pallas_call(functools.partial(correlate_kernel, first=first, picks=pic...  38 us
    ppermute x4, starting transfers between devices, passed_along(): return lax.ppermute(block, axis, route)  12.2 us
    ppermute x3, waiting for transfers between devices, other_core(): return lax.ppermute(block, 'blk', [(i ^ 1, i) for i in range(blk_count)])  1.78 us
    ppermute x4, waiting for transfers between devices, passed_along(): return lax.ppermute(block, axis, route)  1.49 us
    pallas_call x1, Pallas kernels, whiten_tiles(): pl.pallas_call(whiten_kernel, out_specs=pl.BlockSpec(memory_space=pltpu.V...  1.33 us
  transfers between devices with their start and end apart: 7, of which 2 were waited for; matrix products, arithmetic and copies ran while one was open for 3% of the time, Pallas kernels for 39%

profile of v8, /device:TPU:0, one launch (start us, length us, event | category | flops | bytes accessed | tf_op | source)
XLA Modules:
  0.0 57.2 jit_solution(8275581153813882956)
XLA Ops:
  0.0 1.3 %shard_map.37.rest_0_.rest_1_ = bf16[4,8,32,128]{3,2,1,0:T(8,128)(2,1)S(1)} custom-call(f32[32,2,4,512]{3,2,1,0:T(4,128)} %spectra.1), custom_call_target="tpu_custom_call" | custom-call | tf_op jit(solution)/shard_map/pallas_call | solution.py:234
  1.3 3.0 %collective-permute-start = (bf16[4,8,32,128]{3,2,1,0:T(8,128)(2,1)S(1)}, bf16[4,8,32,128]{3,2,1,0:T(8,128)(2,1)S(1)}, u32[]{:S(2)}, u32[]{:S(2)}) collective-permute-start(bf16[4,8,32,128]{3,2,1,0:T(8,128)(2,1)S(1)} %shard_map.37.rest_0_.rest_1_), channel_id=1, source_target_pairs={{1,0},{0,1},{3,2},{2,3},{5,4},{4,5},{7,6},{6,7},{9,8},{8,9},{11,10... | collective-permute-start | bytes 786440 | tf_op jit(solution)/shard_map/ppermute | solution.py:25
  4.4 4.5 %collective-permute-start.1 = (bf16[4,8,32,128]{3,2,1,0:T(8,128)(2,1)S(1)}, bf16[4,8,32,128]{3,2,1,0:T(8,128)(2,1)S(1)}, u32[]{:S(2)}, u32[]{:S(2)}) collective-permute-start(bf16[4,8,32,128]{3,2,1,0:T(8,128)(2,1)S(1)} %shard_map.37.rest_0_.rest_1_), channel_id=1, source_target_pairs={{4,0},{6,2},{8,4},{10,6},{12,8},{14,10},{16,12},{18,14},{20,16},{2... | collective-permute-start | bytes 786440 | tf_op jit(solution)/shard_map/ppermute | solution.py:25
  8.9 0.4 collective-permute-start.2
  9.4 0.1 select_select_fusion
  9.5 0.1 fusion.13
  9.6 0.2 fusion.6
  9.8 0.1 fusion.16
  9.8 0.1 select_n.104
  9.9 0.1 multiply_add_fusion
  10.1 0.1 fusion.1.cos_tab
  10.2 0.8 %concatenate.3.info = s32[2048]{0:T(1024)S(1)} concatenate(s32[1024]{0:T(1024)} %param.4, s32[9]{0:T(128)} %bitcast.27, s32[1]{0:T(128)} %bitcast.1, s32[1014]{0:T(1024)S(1)} %broadcast_in_dim.17), dimensions={0} | concatenate | bytes 16384 | tf_op jit(solution)/shard_map/concatenate | solution.py:247
  11.0 0.1 fusion.sin_tab
  11.1 3.6 %shard_map.38.rest_2_ = bf16[1,9,1,64,32,400]{5,4,3,2,1,0:T(8,128)(2,1)} custom-call(s32[2048]{0:T(1024)S(1)} %concatenate.3.info, s32[16,128]{1,0:T(8,128)S(1)} %bitcast.17, bf16[2,512,128]{2,1,0:T(8,128)(2,1)S(1)} %fusion.1.cos_tab, bf16[2,512,128]{2,1,0:T(8,128)(2,1)S(1)} %fusion.sin_tab, bf16[4,8,32,128]{3,2,1,0:T(8,128)(2,1)S(1)} %shard_map.37.rest_0_.rest_1_, ...), custom_call_target="tpu_custom_call" | custom-call | flops 838860800 | bytes 1500000 | tf_op jit(solution)/shard_map/pallas_call | solution.py:197
  14.7 3.5 %shard_map.39.rest_5_ = bf16[1,9,1,64,32,400]{5,4,3,2,1,0:T(8,128)(2,1)} custom-call(s32[2048]{0:T(1024)S(1)} %concatenate.3.info, s32[16,128]{1,0:T(8,128)S(1)} %bitcast.18, bf16[2,512,128]{2,1,0:T(8,128)(2,1)S(1)} %fusion.1.cos_tab, bf16[2,512,128]{2,1,0:T(8,128)(2,1)S(1)} %fusion.sin_tab, ...), custom_call_target="tpu_custom_call", output_to_operand_aliasing={{}: (6, {})} | custom-call | flops 838860800 | bytes 1500000 | tf_op jit(solution)/shard_map/pallas_call | solution.py:197
  18.2 0.1 collective-permute-start.3
  18.3 1.5 %collective-permute-done.2 = bf16[4,8,32,128]{3,2,1,0:T(8,128)(2,1)S(1)} collective-permute-done((bf16[4,8,32,128]{3,2,1,0:T(8,128)(2,1)S(1)}, bf16[4,8,32,128]{3,2,1,0:T(8,128)(2,1)S(1)}, u32[]{:S(2)}, u32[]{:S(2)}) %collective-permute-start.2) | collective-permute-done | bytes 262176 | tf_op jit(solution)/shard_map/ppermute | solution.py:25
  19.8 0.1 pad_maximum_fusion.rest_3_
  19.9 0.2 collective-permute-start.4
  20.1 4.2 %collective-permute-start.5 = (bf16[2,4,8,32,128]{4,3,2,1,0:T(8,128)(2,1)S(1)}, bf16[2,4,8,32,128]{4,3,2,1,0:T(8,128)(2,1)S(1)}, u32[]{:S(2)}, u32[]{:S(2)}) collective-permute-start(bf16[2,4,8,32,128]{4,3,2,1,0:T(8,128)(2,1)S(1)} %pad_maximum_fusion.rest_3_), channel_id=1, source_target_pairs={{8,0},{10,2},{12,4},{14,6},{16,8},{18,10},{20,12},{22,14},{24,16},... | collective-permute-start | bytes 1572872 | tf_op jit(solution)/shard_map/ppermute | solution.py:25
  24.3 15.4 %shard_map.40.rest_5_ = bf16[1,9,1,64,32,400]{5,4,3,2,1,0:T(8,128)(2,1)} custom-call(s32[2048]{0:T(1024)S(1)} %concatenate.3.info, s32[16,128]{1,0:T(8,128)S(1)} %bitcast.19, bf16[2,512,128]{2,1,0:T(8,128)(2,1)S(1)} %fusion.1.cos_tab, bf16[2,512,128]{2,1,0:T(8,128)(2,1)S(1)} %fusion.sin_tab, ...), custom_call_target="tpu_custom_call", output_to_operand_aliasing={{}: (9, {})} | custom-call | flops 6710886400 | bytes 12000000 | tf_op jit(solution)/shard_map/pallas_call | solution.py:197
  39.7 0.2 collective-permute-start.6
  40.0 1.7 %collective-permute-done.6.rest_4_ = bf16[2,4,8,32,128]{4,3,2,1,0:T(8,128)(2,1)S(1)} collective-permute-done((bf16[2,4,8,32,128]{4,3,2,1,0:T(8,128)(2,1)S(1)}, bf16[2,4,8,32,128]{4,3,2,1,0:T(8,128)(2,1)S(1)}, u32[]{:S(2)}, u32[]{:S(2)}) %collective-permute-start.6) | collective-permute-done | bytes 524320 | tf_op jit(solution)/shard_map/ppermute | solution.py:250
  41.7 15.4 %shard_map.41 = bf16[1,9,1,64,32,400]{5,4,3,2,1,0:T(8,128)(2,1)} custom-call(s32[2048]{0:T(1024)S(1)} %concatenate.3.info, s32[16,128]{1,0:T(8,128)S(1)} %bitcast.20, bf16[2,512,128]{2,1,0:T(8,128)(2,1)S(1)} %fusion.1.cos_tab, bf16[2,512,128]{2,1,0:T(8,128)(2,1)S(1)} %fusion.sin_tab, ...), custom_call_target="tpu_custom_call", output_to_operand_aliasing={{}: (9, {})} | custom-call | flops 6710886400 | bytes 12000000 | tf_op jit(solution)/shard_map/pallas_call | solution.py:197
  (12 shorter events, 0.1 us)
Async XLA Ops:
  1.3 13.4 %collective-permute-start = (bf16[4,8,32,128]{3,2,1,0:T(8,128)(2,1)S(1)}, bf16[4,8,32,128]{3,2,1,0:T(8,128)(2,1)S(1)}, u32[]{:S(2)}, u32[]{:S(2)}) collective-permute-start(bf16[4,8,32,128]{3,2,1,0:T(8,128)(2,1)S(1)} %shard_map.37.rest_0_.rest_1_), channel_id=1, source_target_pairs={{1,0},{0,1},{3,2},{2,3},{5,4},{4,5},{7,6},{6,7},{9,8},{8,9},{11,10... | collective-permute-start | bytes 786440 | tf_op jit(solution)/shard_map/ppermute | solution.py:25
  4.4 13.9 %collective-permute-start.1 = (bf16[4,8,32,128]{3,2,1,0:T(8,128)(2,1)S(1)}, bf16[4,8,32,128]{3,2,1,0:T(8,128)(2,1)S(1)}, u32[]{:S(2)}, u32[]{:S(2)}) collective-permute-start(bf16[4,8,32,128]{3,2,1,0:T(8,128)(2,1)S(1)} %shard_map.37.rest_0_.rest_1_), channel_id=1, source_target_pairs={{4,0},{6,2},{8,4},{10,6},{12,8},{14,10},{16,12},{18,14},{20,16},{2... | collective-permute-start | bytes 786440 | tf_op jit(solution)/shard_map/ppermute | solution.py:25
  8.9 10.9 %collective-permute-start.2 = (bf16[4,8,32,128]{3,2,1,0:T(8,128)(2,1)S(1)}, bf16[4,8,32,128]{3,2,1,0:T(8,128)(2,1)S(1)}, u32[]{:S(2)}, u32[]{:S(2)}) collective-permute-start(bf16[4,8,32,128]{3,2,1,0:T(8,128)(2,1)S(1)} %shard_map.37.rest_0_.rest_1_), channel_id=1, source_target_pairs={{8,0},{10,2},{12,4},{14,6},{16,8},{18,10},{20,12},{22,14},{24,16},... | collective-permute-start | bytes 786440 | tf_op jit(solution)/shard_map/ppermute | solution.py:25
  18.2 1.6 %collective-permute-start.3 = (bf16[4,8,32,128]{3,2,1,0:T(8,128)(2,1)S(1)}, bf16[4,8,32,128]{3,2,1,0:T(8,128)(2,1)S(1)}, u32[]{:S(2)}, u32[]{:S(2)}) collective-permute-start(bf16[4,8,32,128]{3,2,1,0:T(8,128)(2,1)S(1)} %shard_map.37.rest_0_.rest_1_), channel_id=1, source_target_pairs={{2,0},{0,2},{6,4},{4,6},{10,8},{8,10},{14,12},{12,14},{18,16},{16,... | collective-permute-start | bytes 786440 | tf_op jit(solution)/shard_map/ppermute | solution.py:250
  19.9 4.4 %collective-permute-start.4 = (bf16[2,4,8,32,128]{4,3,2,1,0:T(8,128)(2,1)S(1)}, bf16[2,4,8,32,128]{4,3,2,1,0:T(8,128)(2,1)S(1)}, u32[]{:S(2)}, u32[]{:S(2)}) collective-permute-start(bf16[2,4,8,32,128]{4,3,2,1,0:T(8,128)(2,1)S(1)} %pad_maximum_fusion.rest_3_), channel_id=1, source_target_pairs={{2,0},{0,2},{6,4},{4,6},{10,8},{8,10},{14,12},{12,14},{18,16},{16,... | collective-permute-start | bytes 1572872 | tf_op jit(solution)/shard_map/ppermute | solution.py:250
  20.1 19.6 %collective-permute-start.5 = (bf16[2,4,8,32,128]{4,3,2,1,0:T(8,128)(2,1)S(1)}, bf16[2,4,8,32,128]{4,3,2,1,0:T(8,128)(2,1)S(1)}, u32[]{:S(2)}, u32[]{:S(2)}) collective-permute-start(bf16[2,4,8,32,128]{4,3,2,1,0:T(8,128)(2,1)S(1)} %pad_maximum_fusion.rest_3_), channel_id=1, source_target_pairs={{8,0},{10,2},{12,4},{14,6},{16,8},{18,10},{20,12},{22,14},{24,16},... | collective-permute-start | bytes 1572872 | tf_op jit(solution)/shard_map/ppermute | solution.py:25
  39.7 2.0 %collective-permute-start.6 = (bf16[2,4,8,32,128]{4,3,2,1,0:T(8,128)(2,1)S(1)}, bf16[2,4,8,32,128]{4,3,2,1,0:T(8,128)(2,1)S(1)}, u32[]{:S(2)}, u32[]{:S(2)}) collective-permute-start(bf16[2,4,8,32,128]{4,3,2,1,0:T(8,128)(2,1)S(1)} %collective-permute-done.5.rest_3_), channel_id=1, source_target_pairs={{2,0},{0,2},{6,4},{4,6},{10,8},{8,10},{14,12},{12,14},{18,16},{16,... | collective-permute-start | bytes 1572872 | tf_op jit(solution)/shard_map/ppermute | solution.py:250
